TPU v7x, 256 devices: a whole 4x4x8 slice. The times are simulated.
256 devices in a mesh: fac: 4 (over y_lo, core), col: 64 (over y_hi, x, z).
Axes of the slice: x: 4, y: 4 (y_hi: 2, y_lo: 2; y = y_hi * 2 + y_lo), z: 8, core: 2. Of those that a mesh axis runs over, the one named last changes fastest.
Arguments:
- lower_factor: bfloat16 [1, 4, 4, 256, 256], P(None, 'fac', None, None, 'col'), may hold values from -0.1875 to 0.1875
- panel_inverse: float32 [1, 4, 256, 256], P(None, 'fac', None, 'col'), may hold values from -0.375 to 0.375
- right_side: float32 [1, 4, 256, 8192], P(None, 'fac', None, 'col'), may hold values from -0.1875 to 0.1875
- fill: int32 [4, 4], replicated, may hold values 0 or 1
Outputs:
- schur: float32 [8192, 4, 2048], P('col', 'fac')
All inputs are finite; a program needn't handle non-finite values.
Results may differ from a plain program's by a relative error of at most 0.0034.
Values may be sent and summed in bfloat16 or wider, within the bound.
No kernel may reach another device: no remote copies, remote signals or barrier semaphores. Data moves between devices by JAX's collectives and lax.ppermute only.
A program may use at most 64 MiB of HBM per device.

v0:
```python
import jax
import jax.numpy as jnp
from jax import lax
from jax.sharding import PartitionSpec as P


def broadcast(array, axis, root):
    mine = lax.axis_index(axis) == root
    return lax.psum(jnp.where(mine, array, jnp.zeros_like(array)), axis)


def per_device(lower_factor, panel_inverse, right_side, fill):
    panels = lower_factor.shape[0]
    fac_count = lax.axis_size("fac")
    my_index = lax.axis_index("fac")
    inverses = lax.all_gather(panel_inverse, "col", axis=3, tiled=True)[:, 0]
    pending = right_side[:, 0]
    solved = jnp.zeros(pending.shape, jnp.bfloat16)
    total_panels = panels * fac_count
    selector = (jnp.arange(fac_count) == my_index).astype(jnp.int32)
    for owner in range(fac_count):
        own_solve = jnp.dot(
            inverses[0],
            pending[0],
            precision=lax.Precision.HIGHEST,
            preferred_element_type=jnp.float32,
        ).astype(jnp.bfloat16)
        panel_rows = broadcast(own_solve, "fac", owner)
        solved = solved.at[0].set(jnp.where(my_index == owner, panel_rows, solved[0]))
        if owner + 1 < total_panels:
            later_blocks = lower_factor[0:, 0, owner]
            column_flags = fill[:, owner].reshape(panels, fac_count)
            flags = jnp.sum(column_flags * selector[None, :], axis=1)
            targets = jnp.arange(0, panels) * fac_count + my_index
            keep_mask = ((flags == 1) & (targets > owner)).astype(jnp.float32)
            update = jnp.einsum(
                "nab,bm->nam",
                lax.all_gather(later_blocks, "col", axis=2, tiled=True),
                panel_rows,
                preferred_element_type=jnp.float32,
            )
            pending = pending.at[0:].add(-keep_mask[:, None, None] * update)
    slab_flat = solved.reshape(-1, solved.shape[2])
    columns_dev = slab_flat.shape[1]
    share = columns_dev // fac_count
    all_rows = lax.all_gather(slab_flat, "fac", axis=0, tiled=True)
    my_share = lax.dynamic_slice_in_dim(all_rows, my_index * share, share, 1)
    products = lax.dot_general(
        all_rows,
        lax.all_gather(my_share, "col", axis=1, tiled=True),
        (((0,), (0,)), ((), ())),
        preferred_element_type=jnp.float32,
    )
    result = products[:, None, :]
    return result


def solution(mesh):
    return jax.shard_map(
        per_device,
        mesh=mesh,
        in_specs=(
            P(None, "fac", None, None, "col"),
            P(None, "fac", None, "col"),
            P(None, "fac", None, "col"),
            P(),
        ),
        out_specs=P("col", "fac", None),
        check_vma=False,
    )
```

profile of v0, /device:TPU:8, one launch (start us, length us, event | category | flops | bytes accessed | tf_op | source)
XLA Modules:
  0.0 918.3 jit_solution(4776379949293501510)
XLA Ops:
  6.5 0.0 all-reduce.5.cloned.1.call-start
  6.5 0.7 copy.21
  7.2 185.0 %all_gather.18 = f32[1,1,256,256]{2,1,0,3:T(1,128)S(1)} all-gather(f32[1,1,256,4]{2,1,0,3:T(1,128)S(1)} %copy.21), channel_id=1, replica_groups=mesh['fac'=4,'col'=64] {'col'}, dimensions={3}, use_global_device_ids=true | all-gather | bytes 266240 | tf_op jit(solution)/shard_map/all_gather | solution.py:16
  192.2 2.1 fusion.6
  194.4 0.0 all-reduce.5.cloned.1.call-update
  194.4 0.0 all-reduce.7.cloned.1.call-start
  194.4 1.0 slice_reduce_fusion
  195.5 0.7 fusion.28
  196.2 0.7 fusion.27
  196.8 1.0 copy.20
  198.5 175.3 %all-gather = bf16[1,1,1,256,256]{3,2,1,0,4:T(2,128)(2,1)S(1)} all-gather(bf16[1,1,1,256,4]{3,2,1,0,4:T(2,128)(2,1)S(1)} %copy.37), channel_id=2, replica_groups=mesh['fac'=4,'col'=64] {'col'}, dimensions={4}, use_global_device_ids=true | all-gather | bytes 133120 | tf_op jit(solution)/shard_map/all_gather | solution.py:38
  373.7 0.1 copy.23
  373.9 0.0 all-reduce.5.cloned.1.call-done
  373.9 0.0 copy-start
  373.9 1.1 fusion.3
  375.0 1.2 fusion.8
  376.3 0.0 all-reduce.7.cloned.1.call-update
  376.3 0.0 all-reduce.9.cloned.1.call-start
  376.3 0.6 fusion.26
  377.6 177.3 %all-gather.1 = bf16[1,1,1,256,256]{3,2,1,0,4:T(2,128)(2,1)S(1)} all-gather(bf16[1,1,1,256,4]{3,2,1,0,4:T(2,128)(2,1)S(1)} %copy.38), channel_id=3, replica_groups=mesh['fac'=4,'col'=64] {'col'}, dimensions={4}, use_global_device_ids=true | all-gather | bytes 133120 | tf_op jit(solution)/shard_map/all_gather | solution.py:38
  554.8 0.1 copy.26
  555.0 0.0 all-reduce.7.cloned.1.call-done
  555.0 1.0 fusion.4
  556.0 1.2 fusion.10
  557.3 0.0 all-reduce.9.cloned.1.call-update
  557.3 0.0 all-reduce.11.cloned.1.call-start
  557.3 0.7 fusion.25
  558.7 175.3 %all-gather.2 = bf16[1,1,1,256,256]{3,2,1,0,4:T(2,128)(2,1)S(1)} all-gather(bf16[1,1,1,256,4]{3,2,1,0,4:T(2,128)(2,1)S(1)} %copy.39), channel_id=4, replica_groups=mesh['fac'=4,'col'=64] {'col'}, dimensions={4}, use_global_device_ids=true | all-gather | bytes 133120 | tf_op jit(solution)/shard_map/all_gather | solution.py:38
  733.9 0.1 copy.29
  734.1 0.0 all-reduce.9.cloned.1.call-done
  734.1 1.0 fusion.5
  735.2 1.2 fusion.12
  736.4 0.0 all-reduce.11.cloned.1.call-update
  736.4 0.0 all-gather.5.cloned.1.call-start
  736.5 33.8 %all-reduce.11.cloned.1.call-done = bf16[256,128]{1,0:T(8,128)(2,1)} async-done(((bf16[256,128]{1,0:T(8,128)(2,1)}), bf16[256,128]{1,0:T(8,128)(2,1)}) %all-reduce.11.cloned.1.call-update) | async-done | bytes 65552 | tf_op jit(solution)/shard_map/psum | solution.py:9
  770.2 0.0 copy-done
  770.2 0.9 select_select_fusion
  771.1 6.2 all_gather.22
  777.3 0.1 constant_dynamic-slice_fusion
  777.5 0.8 copy.31
  778.2 0.0 all-gather.5.cloned.1.call-update
  778.2 127.8 %all-gather.5.cloned.1.call-done = bf16[1024,2048]{0,1:T(8,128)(2,1)} async-done(((bf16[1024,32]{0,1:T(8,128)(2,1)}), bf16[1024,2048]{0,1:T(8,128)(2,1)}) %all-gather.5.cloned.1.call-update) | async-done | bytes 4194320 | tf_op jit(solution)/shard_map/all_gather | solution.py:50
  906.0 3.7 convolution_bitcast_fusion
  909.7 2.0 copy.32
  (3 shorter events, 0.0 us)
Async XLA Ops:
  6.5 367.4 %all-reduce.5.cloned.1.call-start = ((), (), s32[]{:S(2)}) async-start(), calls=%async_computation | async-start | bytes 131072 | tf_op jit(solution)/shard_map/psum | solution.py:9
  194.4 360.6 %all-reduce.7.cloned.1.call-start = ((), (), s32[]{:S(2)}) async-start(), calls=%async_computation.1 | async-start | bytes 131072 | tf_op jit(solution)/shard_map/psum | solution.py:9
  373.9 396.3 %copy-start = (bf16[256,128]{1,0:T(8,128)(2,1)S(1)}, bf16[256,128]{1,0:T(8,128)(2,1)}, u32[]{:S(2)}) copy-start(bf16[256,128]{1,0:T(8,128)(2,1)} %all-reduce.5.cloned.1.call-done) | copy-start | bytes 196612
  376.3 357.8 %all-reduce.9.cloned.1.call-start = ((), (), s32[]{:S(2)}) async-start(), calls=%async_computation.2 | async-start | bytes 131072 | tf_op jit(solution)/shard_map/psum | solution.py:9
  557.3 212.9 %all-reduce.11.cloned.1.call-start = ((), (), s32[]{:S(2)}) async-start(), calls=%async_computation.3 | async-start | bytes 131072 | tf_op jit(solution)/shard_map/psum | solution.py:9
  736.4 169.6 %all-gather.5.cloned.1.call-start = ((), (), s32[]{:S(2)}) async-start(), calls=%async_computation.4 | async-start | bytes 4259840 | tf_op jit(solution)/shard_map/all_gather | solution.py:50
Sparse Core Ops, SparseCore 0:
  194.5 32.2 all-reduce.4
  376.4 33.7 all-reduce.6
  557.4 32.2 all-reduce.8
  736.5 33.6 all-reduce.10
  778.4 127.6 all-gather.4
where the time goes:
time: 920 us; the launch traced here: 918 us
  blocking collectives  719 us (78%)
  waiting for transfers between devices  162 us (18%)
  between operations  15.1 us (2%)
  matrix products  12.7 us (1%)
    all_gather x3, blocking collectives, per_device(): lax.all_gather(later_blocks, 'col', axis=2, tiled=True)  528 us
    all_gather x1, blocking collectives, per_device(): inverses = lax.all_gather(panel_inverse, 'col', axis=3, tiled=True)[:, 0]  185 us
    all_gather x1, waiting for transfers between devices, per_device(): lax.all_gather(my_share, 'col', axis=1, tiled=True)  128 us
    psum x4, waiting for transfers between devices, broadcast(): return lax.psum(jnp.where(mine, array, jnp.zeros_like(array)), axis)  33.8 us
  transfers between devices with their start and end apart: 5, of which 2 were waited for; matrix products, arithmetic and copies ran while one was open for 1% of the time, Pallas kernels for 0%

commit v1 on v0

v1 whole, which is shorter than its diff:
```python
import functools

import jax
import jax.numpy as jnp
from jax import lax
from jax.experimental import pallas as pl
from jax.experimental.pallas import tpu as pltpu
from jax.sharding import Mesh, PartitionSpec as P

FAC = ("yl", "core")
COL = ("yh", "x", "z")
NT = (((1,), (1,)), ((), ()))


def shift(a, axis, by):
    n = lax.axis_size(axis)
    return lax.ppermute(a, axis, [(i, (i + by) % n) for i in range(n)])


def spread(piece, axes):
    n = lax.axis_size(axes)
    return lax.all_to_all(
        jnp.broadcast_to(piece[None], (n,) + piece.shape), axes, 0, 0, tiled=True
    )


def ordered(mine, other, index):
    first = index == 0
    return jnp.where(first, mine, other), jnp.where(first, other, mine)


def final_kernel(z_ref, own_ref, *refs):
    blocks, out_ref, stage = refs[:-2], refs[-2], refs[-1]
    nz = len(blocks)
    for k in range(nz):
        stage[lax.rem(z_ref[0] + nz - k, nz)] = blocks[k][...]
    own = own_ref[...]
    groups, wide = stage.shape[1], nz * stage.shape[2]
    for g in range(groups):
        rhs = stage[:, g].reshape(wide, stage.shape[3])
        out_ref[:, g * wide : (g + 1) * wide] = lax.dot_general(
            own, rhs, NT, preferred_element_type=jnp.float32
        )


def per_device(lower_factor, panel_inverse, right_side, fill):
    w = panel_inverse.shape[2]
    fac = lax.axis_index(FAC)
    yl, core, z = (lax.axis_index(a) for a in ("yl", "core", "z"))
    nz = lax.axis_size("z")
    panels = fill.shape[0]

    d = panel_inverse[0, 0].T
    hi = lax.reduce_precision(d, 8, 7)
    lo = d - hi
    keep = lax.dynamic_slice_in_dim(fill, fac, 1, 0)[0, : panels - 1] == 1
    low = lower_factor[0, 0, : panels - 1].transpose(0, 2, 1)
    low = jnp.where(keep[:, None, None], low, jnp.zeros_like(low))
    rows = jnp.concatenate(
        [hi.astype(jnp.bfloat16)[None], lo.astype(jnp.bfloat16)[None], low], axis=0
    )
    kw = rows.shape[1]

    lower, upper = ordered(rows, shift(rows, "yl", 1), yl)
    piece = jnp.concatenate([lower[:3], upper], axis=0)
    got = spread(piece, COL)
    n_col = got.shape[0]
    got = got.transpose(1, 0, 2, 3).reshape(piece.shape[0], n_col * kw, w)
    even, odd = ordered(got, shift(got, "core", 1), core)

    def inverse(t, i):
        return t[i].astype(jnp.float32) + t[i + 1].astype(jnp.float32)

    inv = [inverse(even, 0), inverse(odd, 0), inverse(even, 3), inverse(odd, 3)]
    fact = {
        (1, 0): odd[2],
        (2, 0): even[5],
        (2, 1): even[6],
        (3, 0): odd[5],
        (3, 1): odd[6],
        (3, 2): odd[7],
    }

    b = lax.all_gather(right_side[0, 0].T, FAC, axis=0)
    solved = []
    for p in range(panels):
        r = b[p]
        for q in range(p):
            r = r - jnp.dot(
                solved[q], fact[p, q], preferred_element_type=jnp.float32
            )
        y = jnp.dot(
            r,
            inv[p],
            precision=lax.Precision.HIGHEST,
            preferred_element_type=jnp.float32,
        )
        solved.append(y.astype(jnp.bfloat16))
    own = jnp.concatenate(solved, axis=1)
    cols = own.shape[0]
    share = cols // panels
    mine = lax.dynamic_slice_in_dim(own, fac * share, share, 0)

    block = spread(mine, ("yh", "x"))
    ring = [None] * nz
    ring[0] = up = down = block
    for k in range(1, nz // 2 + 1):
        up = shift(up, "z", 1)
        ring[k] = up
        if k < nz // 2:
            down = shift(down, "z", -1)
            ring[nz - k] = down
    full = pl.pallas_call(
        final_kernel,
        out_shape=jax.ShapeDtypeStruct((cols, n_col * share), jnp.float32),
        in_specs=[pl.BlockSpec(memory_space=pltpu.SMEM)]
        + [pl.BlockSpec(memory_space=pltpu.VMEM)] * (nz + 1),
        out_specs=pl.BlockSpec(memory_space=pltpu.VMEM),
        scratch_shapes=[pltpu.VMEM((nz,) + block.shape, jnp.bfloat16)],
        name="product",
    )(z[None].astype(jnp.int32), own, *ring)
    return full[:, None, :]


def solution(mesh):
    fine = Mesh(mesh.devices.reshape(2, 2, 2, 4, 8), FAC + COL)
    return jax.shard_map(
        per_device,
        mesh=fine,
        in_specs=(
            P(None, FAC, None, None, COL),
            P(None, FAC, None, COL),
            P(None, FAC, None, COL),
            P(),
        ),
        out_specs=P(COL, FAC, None),
        check_vma=False,
    )
```

time: 920 us -> 140 us (0.15)
  blocking collectives: 719 us -> 65.7 us
  waiting for transfers between devices: 162 us -> 45.9 us
  between operations: 15.1 us -> 0.24 us
  starting transfers between devices: 0.17 us -> 12 us
  matrix products: 12.7 us -> 2.16 us
    all_gather x5 -> x1, blocking collectives: 719 us -> 7.03 us  [per_device(): b = lax.all_gather(right_side[0, 0].T, FAC, axis=0)]
    all_gather x1 -> x0, waiting for transfers between devices: 128 us -> none  [per_device(): lax.all_gather(my_share, 'col', axis=1, tiled=True)]
    all_to_all x0 -> x2, blocking collectives: none -> 58.7 us  [spread(): lax.all_to_all(jnp.broadcast_to(piece[None], (n,) + piece.shape), axes, 0...]
    ppermute x0 -> x9, waiting for transfers between devices: none -> 45.9 us  [shift(): return lax.ppermute(a, axis, [(i, (i + by) % n) for i in range(n)])]
    psum x4 -> x0, waiting for transfers between devices: 33.8 us -> none  [broadcast(): return lax.psum(jnp.where(mine, array, jnp.zeros_like(array)), axis)]
    ppermute x0 -> x9, starting transfers between devices: none -> 12 us  [shift(): return lax.ppermute(a, axis, [(i, (i + by) % n) for i in range(n)])]
    dot_general x8 -> x10, matrix products: 12.7 us -> 2.16 us  [the longest x4 1.16 us: per_device(): jnp.dot(r, inv[p], precision=lax.Precision.HIGHEST, preferred_element_typ...]
  transfers between devices with their start and end apart: 5 -> 9, of which waited for: 2 -> 5; matrix products, arithmetic and copies ran while one was open for 1% -> 0% of each run, Pallas kernels for 0% -> 0%
where the time goes in v1:
time: 140 us
  blocking collectives  65.7 us (47%)
  waiting for transfers between devices  45.9 us (33%)
  starting transfers between devices  12 us (9%)
  local copies, waits for them, and re-layouts  7.41 us (5%)
  Pallas kernels  4.99 us (4%)
  matrix products  2.16 us (2%)
  other arithmetic  1.59 us (1%)
    all_to_all x2, blocking collectives, spread(): lax.all_to_all(jnp.broadcast_to(piece[None], (n,) + piece.shape), axes, 0...  58.7 us
    ppermute x9, waiting for transfers between devices, shift(): return lax.ppermute(a, axis, [(i, (i + by) % n) for i in range(n)])  45.9 us
    ppermute x9, starting transfers between devices, shift(): return lax.ppermute(a, axis, [(i, (i + by) % n) for i in range(n)])  12 us
    all_gather x1, blocking collectives, per_device(): b = lax.all_gather(right_side[0, 0].T, FAC, axis=0)  7.03 us
    pallas_call x1, Pallas kernels, per_device(): pl.pallas_call(final_kernel, out_shape=jax.ShapeDtypeStruct((cols, n_col...  4.99 us
    broadcast_in_dim x1, local copies, waits for them, and re-layouts, per_device(): return full[:, None, :]  3.27 us
  transfers between devices with their start and end apart: 9, of which 5 were waited for; matrix products, arithmetic and copies ran while one was open for 0% of the time, Pallas kernels for 0%

profile of v1, /device:TPU:8, one launch (start us, length us, event | category | flops | bytes accessed | tf_op | source)
XLA Modules:
  0.0 140.0 jit_solution(3106679617592557491)
XLA Ops:
  0.0 0.0 copy-start
  0.0 0.0 copy-start.10
  0.0 0.0 copy-start.9
  0.0 0.7 copy-done
  0.7 0.0 copy-done.10
  0.7 0.0 copy-done.9
  0.7 0.1 fusion.25
  0.8 2.2 %collective-permute-start = (bf16[5,4,256]{2,1,0:T(4,128)(2,1)S(1)}, bf16[5,4,256]{2,1,0:T(4,128)(2,1)S(1)}, u32[]{:S(2)}, u32[]{:S(2)}) collective-permute-start(bf16[5,4,256]{2,1,0:T(4,128)(2,1)S(1)} %pad_maximum_fusion.2), channel_id=1, source_target_pairs={{0,128},{128,0},{1,129},{129,1},{2,130},{130,2},{3,131},{131,3},{4... | collective-permute-start | bytes 30728 | tf_op jit(solution)/shard_map/ppermute | solution.py:17
  3.1 1.7 %collective-permute-done = bf16[5,4,256]{2,1,0:T(4,128)(2,1)S(1)} collective-permute-done((bf16[5,4,256]{2,1,0:T(4,128)(2,1)S(1)}, bf16[5,4,256]{2,1,0:T(4,128)(2,1)S(1)}, u32[]{:S(2)}, u32[]{:S(2)}) %collective-permute-start) | collective-permute-done | bytes 10272 | tf_op jit(solution)/shard_map/ppermute | solution.py:17
  4.8 0.5 broadcast_in_dim.41
  5.3 42.2 %all_to_all.10 = bf16[64,8,4,256]{3,2,1,0:T(4,128)(2,1)S(1)} all-to-all(bf16[64,8,4,256]{3,2,1,0:T(4,128)(2,1)S(1)} %broadcast_in_dim.41), channel_id=1, replica_groups=mesh['yl'=2,'core'=2,'yh'=2,'x'=4,'z'=8] {'yh','x','z'}, dimensions={0} | all-to-all | bytes 2097152 | tf_op jit(solution)/shard_map/all_to_all | solution.py:22
  47.5 0.0 copy-start.8
  47.5 0.2 copy.13
  47.8 0.1 collective-permute-start.1
  47.9 0.6 copy-done.8
  48.4 0.1 copy.14
  48.5 7.0 %all-gather = f32[512,256]{1,0:T(8,128)S(1)} all-gather(f32[128,256]{1,0:T(8,128)S(1)} %bitcast.74), channel_id=2, replica_groups=mesh['yl'=2,'core'=2,'yh'=2,'x'=4,'z'=8] {'yl','core'}, dimensions={0}, use_global_device_ids=true | all-gather | bytes 655360 | tf_op jit(solution)/shard_map/all_gather | solution.py:84
  55.6 0.0 collective-permute-done.1
  55.6 0.2 broadcast_select_fusion
  55.8 1.2 fusion
  57.0 1.4 fusion.29
  58.4 0.3 convolution_convert_fusion.3
  58.7 0.2 convolution_subtract_fusion.2
  58.9 0.2 convolution_subtract_fusion.4
  59.0 0.2 convolution_subtract_fusion.5
  59.2 0.3 convolution_convert_fusion.2
  59.5 0.2 convolution_subtract_fusion.1
  59.7 0.2 convolution_subtract_fusion.3
  59.8 0.3 convolution_convert_fusion.1
  60.1 0.2 convolution_subtract_fusion
  60.3 0.3 convolution_convert_fusion
  60.6 0.0 copy-start.2
  60.6 0.1 broadcast_in_dim.42
  60.7 0.6 copy-done.2
  61.3 16.5 %all_to_all.11.refs_0_ = bf16[8,32,1024]{2,1,0:T(8,128)(2,1)S(1)} all-to-all(bf16[8,32,1024]{2,1,0:T(8,128)(2,1)S(1)} %broadcast_in_dim.42), channel_id=1, replica_groups=mesh['yl'=2,'core'=2,'yh'=2,'x'=4,'z'=8] {'yh','x'}, dimensions={0} | all-to-all | bytes 1048576 | tf_op jit(solution)/shard_map/all_to_all | solution.py:22
  77.8 0.0 copy-start.1
  77.8 1.3 collective-permute-start.2
  79.1 2.0 %collective-permute-start.6 = (bf16[8,32,1024]{2,1,0:T(8,128)(2,1)S(1)}, bf16[8,32,1024]{2,1,0:T(8,128)(2,1)S(1)}, u32[]{:S(2)}, u32[]{:S(2)}) collective-permute-start(bf16[8,32,1024]{2,1,0:T(8,128)(2,1)S(1)} %all_to_all.11.refs_0_), channel_id=1, source_target_pairs={{0,7},{1,0},{2,1},{3,2},{4,3},{5,4},{6,5},{7,6},{8,15},{9,8},{10,9... | collective-permute-start | bytes 1572872 | tf_op jit(solution)/shard_map/ppermute | solution.py:17
  81.0 11.5 %collective-permute-done.2.refs_1_ = bf16[8,32,1024]{2,1,0:T(8,128)(2,1)S(1)} collective-permute-done((bf16[8,32,1024]{2,1,0:T(8,128)(2,1)S(1)}, bf16[8,32,1024]{2,1,0:T(8,128)(2,1)S(1)}, u32[]{:S(2)}, u32[]{:S(2)}) %collective-permute-start.2) | collective-permute-done | bytes 524320 | tf_op jit(solution)/shard_map/ppermute | solution.py:17
  92.5 0.0 copy-start.3
  92.5 0.1 collective-permute-start.3
  92.6 0.0 collective-permute-done.6.refs_7_
  92.6 0.0 copy-start.4
  92.6 3.2 %collective-permute-start.7 = (bf16[8,32,1024]{2,1,0:T(8,128)(2,1)S(1)}, bf16[8,32,1024]{2,1,0:T(8,128)(2,1)S(1)}, u32[]{:S(2)}, u32[]{:S(2)}) collective-permute-start(bf16[8,32,1024]{2,1,0:T(8,128)(2,1)S(1)} %collective-permute-done.6.refs_7_), channel_id=1, source_target_pairs={{0,7},{1,0},{2,1},{3,2},{4,3},{5,4},{6,5},{7,6},{8,15},{9,8},{10,9... | collective-permute-start | bytes 1572872 | tf_op jit(solution)/shard_map/ppermute | solution.py:17
  95.8 10.6 %collective-permute-done.3.refs_2_ = bf16[8,32,1024]{2,1,0:T(8,128)(2,1)S(1)} collective-permute-done((bf16[8,32,1024]{2,1,0:T(8,128)(2,1)S(1)}, bf16[8,32,1024]{2,1,0:T(8,128)(2,1)S(1)}, u32[]{:S(2)}, u32[]{:S(2)}) %collective-permute-start.3) | collective-permute-done | bytes 524320 | tf_op jit(solution)/shard_map/ppermute | solution.py:17
  106.4 0.0 copy-start.5
  106.4 0.0 collective-permute-start.4
  106.4 0.0 collective-permute-done.7.refs_6_
  106.4 0.0 copy-start.6
  106.4 3.2 %collective-permute-start.8 = (bf16[8,32,1024]{2,1,0:T(8,128)(2,1)S(1)}, bf16[8,32,1024]{2,1,0:T(8,128)(2,1)}, u32[]{:S(2)}, u32[]{:S(2)}) collective-permute-start(bf16[8,32,1024]{2,1,0:T(8,128)(2,1)S(1)} %collective-permute-done.7.refs_6_), channel_id=1, source_target_pairs={{0,7},{1,0},{2,1},{3,2},{4,3},{5,4},{6,5},{7,6},{8,15},{9,8},{10,9... | collective-permute-start | bytes 1572872 | tf_op jit(solution)/shard_map/ppermute | solution.py:17
  109.7 9.8 %collective-permute-done.4.refs_3_ = bf16[8,32,1024]{2,1,0:T(8,128)(2,1)S(1)} collective-permute-done((bf16[8,32,1024]{2,1,0:T(8,128)(2,1)S(1)}, bf16[8,32,1024]{2,1,0:T(8,128)(2,1)S(1)}, u32[]{:S(2)}, u32[]{:S(2)}) %collective-permute-start.4) | collective-permute-done | bytes 524320 | tf_op jit(solution)/shard_map/ppermute | solution.py:17
  119.5 0.0 copy-start.7
  119.5 0.0 collective-permute-start.5
  119.5 0.0 collective-permute-done.8.refs_5_
  119.5 12.3 %collective-permute-done.5.refs_4_ = bf16[8,32,1024]{2,1,0:T(8,128)(2,1)} collective-permute-done((bf16[8,32,1024]{2,1,0:T(8,128)(2,1)S(1)}, bf16[8,32,1024]{2,1,0:T(8,128)(2,1)}, u32[]{:S(2)}, u32[]{:S(2)}) %collective-permute-start.5) | collective-permute-done | bytes 524320 | tf_op jit(solution)/shard_map/ppermute | solution.py:17
  131.7 0.0 copy-done.1
  131.7 0.0 copy-done.3
  131.7 0.0 copy-done.4
  131.8 0.0 copy-done.5
  131.8 0.0 copy-done.6
  131.8 0.0 copy-done.7
  131.8 5.0 %product.1 = f32[128,2048]{1,0:T(8,128)} custom-call(s32[1]{0:T(128)} %bitcast.z_ref, bf16[128,1024]{1,0:T(8,128)(2,1)} %copy-done.2, bf16[8,32,1024]{2,1,0:T(8,128)(2,1)} %copy-done.1, bf16[8,32,1024]{2,1,0:T(8,128)(2,1)} %copy-done.3, bf16[8,32,1024]{2,1,0:T(8,128)(2,1)} %copy-done.5, bf16[8,32,1024]{2,1,0:T(8,128)(2,1)} %copy-done.7, ...), custom_call_target="tpu_custom_call" | custom-call | tf_op jit(solution)/shard_map/product/pallas_call | solution.py:113
  136.8 3.3 %copy.16 = f32[128,1,2048]{2,1,0:T(1,128)} copy(f32[128,1,2048]{2,0,1:T(8,128)} %bitcast.72) | data formatting | bytes 2097152 | tf_op jit(solution)/shard_map/broadcast_in_dim | solution.py:122
  (9 shorter events, 0.1 us)
Async XLA Ops:
  0.0 0.7 copy-start
  0.0 0.7 copy-start.10
  0.0 0.7 copy-start.9
  0.8 3.9 %collective-permute-start = (bf16[5,4,256]{2,1,0:T(4,128)(2,1)S(1)}, bf16[5,4,256]{2,1,0:T(4,128)(2,1)S(1)}, u32[]{:S(2)}, u32[]{:S(2)}) collective-permute-start(bf16[5,4,256]{2,1,0:T(4,128)(2,1)S(1)} %pad_maximum_fusion.2), channel_id=1, source_target_pairs={{0,128},{128,0},{1,129},{129,1},{2,130},{130,2},{3,131},{131,3},{4... | collective-permute-start | bytes 30728 | tf_op jit(solution)/shard_map/ppermute | solution.py:17
  47.5 0.9 copy-start.8
  47.8 7.8 %collective-permute-start.1 = (bf16[8,256,256]{2,0,1:T(8,128)(2,1)S(1)}, bf16[8,256,256]{2,0,1:T(8,128)(2,1)S(1)}, u32[]{:S(2)}, u32[]{:S(2)}) collective-permute-start(bf16[8,256,256]{2,0,1:T(8,128)(2,1)S(1)} %bitcast.71), channel_id=1, source_target_pairs={{0,64},{64,0},{1,65},{65,1},{2,66},{66,2},{3,67},{67,3},{4,68},{68... | collective-permute-start | bytes 3145736 | tf_op jit(solution)/shard_map/ppermute | solution.py:17
  60.6 0.7 copy-start.2
  77.8 54.0 %copy-start.1 = (bf16[8,32,1024]{2,1,0:T(8,128)(2,1)}, bf16[8,32,1024]{2,1,0:T(8,128)(2,1)S(1)}, u32[]{:S(2)}) copy-start(bf16[8,32,1024]{2,1,0:T(8,128)(2,1)S(1)} %all_to_all.11.refs_0_) | copy-start | bytes 1572868
  77.8 14.7 %collective-permute-start.2 = (bf16[8,32,1024]{2,1,0:T(8,128)(2,1)S(1)}, bf16[8,32,1024]{2,1,0:T(8,128)(2,1)S(1)}, u32[]{:S(2)}, u32[]{:S(2)}) collective-permute-start(bf16[8,32,1024]{2,1,0:T(8,128)(2,1)S(1)} %all_to_all.11.refs_0_), channel_id=1, source_target_pairs={{0,1},{1,2},{2,3},{3,4},{4,5},{5,6},{6,7},{7,0},{8,9},{9,10},{10,1... | collective-permute-start | bytes 1572872 | tf_op jit(solution)/shard_map/ppermute | solution.py:17
  79.1 13.5 %collective-permute-start.6 = (bf16[8,32,1024]{2,1,0:T(8,128)(2,1)S(1)}, bf16[8,32,1024]{2,1,0:T(8,128)(2,1)S(1)}, u32[]{:S(2)}, u32[]{:S(2)}) collective-permute-start(bf16[8,32,1024]{2,1,0:T(8,128)(2,1)S(1)} %all_to_all.11.refs_0_), channel_id=1, source_target_pairs={{0,7},{1,0},{2,1},{3,2},{4,3},{5,4},{6,5},{7,6},{8,15},{9,8},{10,9... | collective-permute-start | bytes 1572872 | tf_op jit(solution)/shard_map/ppermute | solution.py:17
  92.5 39.2 %copy-start.3 = (bf16[8,32,1024]{2,1,0:T(8,128)(2,1)}, bf16[8,32,1024]{2,1,0:T(8,128)(2,1)S(1)}, u32[]{:S(2)}) copy-start(bf16[8,32,1024]{2,1,0:T(8,128)(2,1)S(1)} %collective-permute-done.2.refs_1_) | copy-start | bytes 1572868
  92.5 13.9 %collective-permute-start.3 = (bf16[8,32,1024]{2,1,0:T(8,128)(2,1)S(1)}, bf16[8,32,1024]{2,1,0:T(8,128)(2,1)S(1)}, u32[]{:S(2)}, u32[]{:S(2)}) collective-permute-start(bf16[8,32,1024]{2,1,0:T(8,128)(2,1)S(1)} %collective-permute-done.2.refs_1_), channel_id=1, source_target_pairs={{0,1},{1,2},{2,3},{3,4},{4,5},{5,6},{6,7},{7,0},{8,9},{9,10},{10,1... | collective-permute-start | bytes 1572872 | tf_op jit(solution)/shard_map/ppermute | solution.py:17
  92.6 39.1 %copy-start.4 = (bf16[8,32,1024]{2,1,0:T(8,128)(2,1)}, bf16[8,32,1024]{2,1,0:T(8,128)(2,1)S(1)}, u32[]{:S(2)}) copy-start(bf16[8,32,1024]{2,1,0:T(8,128)(2,1)S(1)} %collective-permute-done.6.refs_7_) | copy-start | bytes 1572868
  92.6 13.8 %collective-permute-start.7 = (bf16[8,32,1024]{2,1,0:T(8,128)(2,1)S(1)}, bf16[8,32,1024]{2,1,0:T(8,128)(2,1)S(1)}, u32[]{:S(2)}, u32[]{:S(2)}) collective-permute-start(bf16[8,32,1024]{2,1,0:T(8,128)(2,1)S(1)} %collective-permute-done.6.refs_7_), channel_id=1, source_target_pairs={{0,7},{1,0},{2,1},{3,2},{4,3},{5,4},{6,5},{7,6},{8,15},{9,8},{10,9... | collective-permute-start | bytes 1572872 | tf_op jit(solution)/shard_map/ppermute | solution.py:17
  106.4 25.3 %copy-start.5 = (bf16[8,32,1024]{2,1,0:T(8,128)(2,1)}, bf16[8,32,1024]{2,1,0:T(8,128)(2,1)S(1)}, u32[]{:S(2)}) copy-start(bf16[8,32,1024]{2,1,0:T(8,128)(2,1)S(1)} %collective-permute-done.3.refs_2_) | copy-start | bytes 1572868
  106.4 13.0 %collective-permute-start.4 = (bf16[8,32,1024]{2,1,0:T(8,128)(2,1)S(1)}, bf16[8,32,1024]{2,1,0:T(8,128)(2,1)S(1)}, u32[]{:S(2)}, u32[]{:S(2)}) collective-permute-start(bf16[8,32,1024]{2,1,0:T(8,128)(2,1)S(1)} %collective-permute-done.3.refs_2_), channel_id=1, source_target_pairs={{0,1},{1,2},{2,3},{3,4},{4,5},{5,6},{6,7},{7,0},{8,9},{9,10},{10,1... | collective-permute-start | bytes 1572872 | tf_op jit(solution)/shard_map/ppermute | solution.py:17
  106.4 25.3 %copy-start.6 = (bf16[8,32,1024]{2,1,0:T(8,128)(2,1)}, bf16[8,32,1024]{2,1,0:T(8,128)(2,1)S(1)}, u32[]{:S(2)}) copy-start(bf16[8,32,1024]{2,1,0:T(8,128)(2,1)S(1)} %collective-permute-done.7.refs_6_) | copy-start | bytes 1572868
  106.4 13.0 %collective-permute-start.8 = (bf16[8,32,1024]{2,1,0:T(8,128)(2,1)S(1)}, bf16[8,32,1024]{2,1,0:T(8,128)(2,1)}, u32[]{:S(2)}, u32[]{:S(2)}) collective-permute-start(bf16[8,32,1024]{2,1,0:T(8,128)(2,1)S(1)} %collective-permute-done.7.refs_6_), channel_id=1, source_target_pairs={{0,7},{1,0},{2,1},{3,2},{4,3},{5,4},{6,5},{7,6},{8,15},{9,8},{10,9... | collective-permute-start | bytes 1572872 | tf_op jit(solution)/shard_map/ppermute | solution.py:17
  119.5 12.3 %copy-start.7 = (bf16[8,32,1024]{2,1,0:T(8,128)(2,1)}, bf16[8,32,1024]{2,1,0:T(8,128)(2,1)S(1)}, u32[]{:S(2)}) copy-start(bf16[8,32,1024]{2,1,0:T(8,128)(2,1)S(1)} %collective-permute-done.4.refs_3_) | copy-start | bytes 1572868
  119.5 12.3 %collective-permute-start.5 = (bf16[8,32,1024]{2,1,0:T(8,128)(2,1)S(1)}, bf16[8,32,1024]{2,1,0:T(8,128)(2,1)}, u32[]{:S(2)}, u32[]{:S(2)}) collective-permute-start(bf16[8,32,1024]{2,1,0:T(8,128)(2,1)S(1)} %collective-permute-done.4.refs_3_), channel_id=1, source_target_pairs={{0,1},{1,2},{2,3},{3,4},{4,5},{5,6},{6,7},{7,0},{8,9},{9,10},{10,1... | collective-permute-start | bytes 1572872 | tf_op jit(solution)/shard_map/ppermute | solution.py:17

commit v2 on v1

v2 whole, which is shorter than its diff:
```python
import jax
import jax.numpy as jnp
from jax import lax
from jax.experimental import pallas as pl
from jax.experimental.pallas import tpu as pltpu
from jax.sharding import Mesh, PartitionSpec as P

FAC = ("yl", "core")
COL = ("yh", "x", "z")
NT = (((1,), (1,)), ((), ()))
BF = jnp.bfloat16
F32 = jnp.float32
LANES = 128


def shift(a, axis, by):
    n = lax.axis_size(axis)
    return lax.ppermute(a, axis, [(i, (i + by) % n) for i in range(n)])


def exchange(a, axes):
    return lax.all_to_all(a, axes, 0, 0, tiled=True)


def split(a):
    hi = lax.reduce_precision(a, 8, 7)
    return hi.astype(BF), (a - hi).astype(BF)


def dot(a, b):
    return jnp.dot(a, b, preferred_element_type=F32)


def solve_kernel(pos_ref, own_ref, other_ref, out_ref, mine_ref):
    peers, _, lanes = own_ref.shape
    half = peers // 2
    share = 32

    def run(pair, sections):
        def square(ref, yl, first):
            parts = [
                ref[yl * half : (yl + 1) * half, r : r + share, :].reshape(
                    half * share, lanes
                )
                for r in (first, first + share)
            ]
            return jnp.concatenate(parts, axis=1)

        solved = []
        for p in range(4):
            yl, core = divmod(p, 2)
            ref, section = pair[core], sections[core]
            base = 320 + section * 128
            r = square(ref, yl, base).astype(F32) + square(
                ref, yl, base + 64
            ).astype(F32)
            for q in range(p):
                r = r - dot(solved[q], square(ref, yl, 128 + 64 * q))
            rhi = r.astype(BF)
            rlo = (r - rhi.astype(F32)).astype(BF)
            dhi = square(ref, yl, 0)
            y = (dot(rlo, dhi) + dot(rhi, square(ref, yl, 64))) + dot(rhi, dhi)
            y = y.astype(BF)
            solved.append(y)
            out_ref[:, :, p * 256 : (p + 1) * 256] = y.reshape(half, share, 256)

    @pl.when(pos_ref[0] == 0)
    def _():
        run((own_ref, other_ref), (0, 1))

    @pl.when(pos_ref[0] == 1)
    def _():
        run((other_ref, own_ref), (1, 0))

    mine_ref[...] = out_ref[pos_ref[1]]


def final_kernel(pos_ref, m0, m1, m2, *refs):
    blocks, out_ref, own, stage = refs[:-3], refs[-3], refs[-2], refs[-1]
    nz = len(blocks)
    z, yl, core = pos_ref[0], pos_ref[1], pos_ref[2]
    share = m0.shape[0]
    own[2 * yl + core] = m0[...]
    own[2 * (1 - yl) + core] = m1[...]
    own[2 * yl + (1 - core)] = m2[0]
    own[2 * (1 - yl) + (1 - core)] = m2[1]
    for k in range(nz):
        stage[lax.rem(z + nz - k, nz)] = blocks[k][...]
    lhs = own[...].reshape(4 * share, own.shape[2])
    groups, wide = stage.shape[1], nz * share
    for g in range(groups):
        rhs = stage[:, g].reshape(wide, stage.shape[3])
        out_ref[:, 0, g * wide : (g + 1) * wide] = lax.dot_general(
            lhs, rhs, NT, preferred_element_type=F32
        )


def per_device(lower_factor, panel_inverse, right_side, fill):
    w, kw = panel_inverse.shape[2:]
    fac = lax.axis_index(FAC)
    yl, core, yh, x, z = (lax.axis_index(a) for a in FAC + COL)
    nz, nx = lax.axis_size("z"), lax.axis_size("x")
    panels = fill.shape[0]

    hi, lo = split(panel_inverse[0, 0].T)
    keep = lax.dynamic_slice_in_dim(fill, fac, 1, 0)[0, : panels - 1] == 1
    low = lower_factor[0, 0, : panels - 1].transpose(0, 2, 1)
    low = jnp.where(keep[:, None, None], low, jnp.zeros_like(low))
    rows = jnp.concatenate([hi[None], lo[None], low], axis=0)
    nt = rows.shape[0]
    rows = rows.reshape(nt, kw, w // LANES, LANES).transpose(0, 2, 1, 3)
    rows = rows.reshape(nt * w // LANES * kw, LANES)
    got = exchange(jnp.broadcast_to(rows[None], (nz,) + rows.shape), "z")
    got = got.reshape(nz, nt * w // LANES, kw, LANES).transpose(1, 0, 2, 3)
    got = got.reshape(-1, LANES)

    share = right_side.shape[3] // panels
    bt = jnp.stack(split(right_side[0, 0].T))
    bt = bt.reshape(2, 2, 2, share, w // LANES, LANES).transpose(1, 2, 0, 4, 3, 5)
    bt = jnp.where(core == 0, bt, bt[:, ::-1]).reshape(2, -1, LANES)

    npeer = 2 * 2 * nx
    send = jnp.concatenate(
        [
            jnp.broadcast_to(got[None, None], (2, npeer // 2) + got.shape),
            jnp.broadcast_to(bt[:, None], (2, npeer // 2) + bt.shape[1:]),
        ],
        axis=2,
    ).reshape(npeer, -1, LANES)
    held = exchange(send, ("yl", "yh", "x"))
    other = shift(held, "core", 1)

    vm = pl.BlockSpec(memory_space=pltpu.VMEM)
    sm = pl.BlockSpec(memory_space=pltpu.SMEM)
    block, mine = pl.pallas_call(
        solve_kernel,
        out_shape=(
            jax.ShapeDtypeStruct((npeer // 2, share, panels * w), BF),
            jax.ShapeDtypeStruct((share, panels * w), BF),
        ),
        in_specs=[sm, vm, vm],
        out_specs=(vm, vm),
        name="solve",
    )(jnp.stack([core, yh * nx + x]).astype(jnp.int32), held, other)

    m1 = shift(mine, "yl", 1)
    m2 = shift(jnp.stack([mine, m1]), "core", 1)

    ring = [None] * nz
    ring[0] = up = down = block
    for k in range(1, nz // 2 + 1):
        up = shift(up, "z", 1)
        ring[k] = up
        if k < nz // 2:
            down = shift(down, "z", -1)
            ring[nz - k] = down
    return pl.pallas_call(
        final_kernel,
        out_shape=jax.ShapeDtypeStruct(
            (panels * share, 1, npeer // 2 * nz * share), F32
        ),
        in_specs=[sm] + [vm] * (nz + 3),
        out_specs=vm,
        scratch_shapes=[
            pltpu.VMEM((panels,) + mine.shape, BF),
            pltpu.VMEM((nz,) + block.shape, BF),
        ],
        name="product",
    )(jnp.stack([z, yl, core]).astype(jnp.int32), mine, m1, m2, *ring)


def solution(mesh):
    fine = Mesh(mesh.devices.reshape(2, 2, 2, 4, 8), FAC + COL)
    return jax.shard_map(
        per_device,
        mesh=fine,
        in_specs=(
            P(None, FAC, None, None, COL),
            P(None, FAC, None, COL),
            P(None, FAC, None, COL),
            P(),
        ),
        out_specs=P(COL, FAC, None),
        check_vma=False,
    )
```

time: 140 us -> 128 us (0.914)
  blocking collectives: 65.7 us -> 36.3 us
  starting transfers between devices: 12 us -> 20 us
  waiting for transfers between devices: 45.9 us -> 53.7 us
  local copies, waits for them, and re-layouts: 7.41 us -> 2.13 us
  Pallas kernels: 4.99 us -> 9.79 us
  other arithmetic: 1.59 us -> 5.08 us
  matrix products: 2.16 us -> 0 us
    all_to_all x2 -> x1, blocking collectives: 58.7 us -> 36.3 us  [exchange(): return lax.all_to_all(a, axes, 0, 0, tiled=True)]
    all_to_all x0 -> x1, starting transfers between devices: none -> 8.47 us  [exchange(): return lax.all_to_all(a, axes, 0, 0, tiled=True)]
    all_gather x1 -> x0, blocking collectives: 7.03 us -> none  [per_device(): b = lax.all_gather(right_side[0, 0].T, FAC, axis=0)]
    all_to_all x0 -> x1, waiting for transfers between devices: none -> 7 us  [exchange(): return lax.all_to_all(a, axes, 0, 0, tiled=True)]
    pallas_call x1 -> x2, Pallas kernels: 4.99 us -> 9.79 us  [the longest x1 5.09 us: per_device(): pl.pallas_call(final_kernel, out_shape=jax.ShapeDtypeStruct((panels * sha...]
    broadcast_in_dim x3, local copies, waits for them, and re-layouts: 3.82 us -> 1.09 us  [the longest x1 0.65 us: per_device(): got = exchange(jnp.broadcast_to(rows[None], (nz,) + rows.shape), 'z')]
    another operation x0 -> x3, other arithmetic: none -> 2.21 us  [the longest x1 0.88 us: per_device(): m2 = shift(jnp.stack([mine, m1]), 'core', 1)]
    dot_general x10 -> x0, matrix products: 2.16 us -> none  [the longest x4 1.16 us: per_device(): jnp.dot(r, inv[p], precision=lax.Precision.HIGHEST, preferred_element_typ...]
  transfers between devices with their start and end apart: 9 -> 11, of which waited for: 5 -> 8; matrix products, arithmetic and copies ran while one was open for 0% -> 3% of each run, Pallas kernels for 0% -> 0%
where the time goes in v2:
time: 128 us; the launch traced here: 127 us
  waiting for transfers between devices  53.7 us (42%)
  blocking collectives  36.3 us (28%)
  starting transfers between devices  20 us (16%)
  Pallas kernels  9.79 us (8%)
  other arithmetic  5.08 us (4%)
  local copies, waits for them, and re-layouts  2.13 us (2%)
    ppermute x10, waiting for transfers between devices, shift(): return lax.ppermute(a, axis, [(i, (i + by) % n) for i in range(n)])  46.7 us
    all_to_all x1, blocking collectives, exchange(): return lax.all_to_all(a, axes, 0, 0, tiled=True)  36.3 us
    ppermute x10, starting transfers between devices, shift(): return lax.ppermute(a, axis, [(i, (i + by) % n) for i in range(n)])  11.6 us
    all_to_all x1, starting transfers between devices, exchange(): return lax.all_to_all(a, axes, 0, 0, tiled=True)  8.47 us
    all_to_all x1, waiting for transfers between devices, exchange(): return lax.all_to_all(a, axes, 0, 0, tiled=True)  7 us
    pallas_call x1, Pallas kernels, per_device(): pl.pallas_call(final_kernel, out_shape=jax.ShapeDtypeStruct((panels * sha...  5.09 us
    pallas_call x1, Pallas kernels, per_device(): pl.pallas_call(solve_kernel, out_shape=(jax.ShapeDtypeStruct((npeer // 2,...  4.69 us
  transfers between devices with their start and end apart: 11, of which 8 were waited for; matrix products, arithmetic and copies ran while one was open for 3% of the time, Pallas kernels for 0%

profile of v2, /device:TPU:8, one launch (start us, length us, event | category | flops | bytes accessed | tf_op | source)
XLA Modules:
  0.0 127.3 jit_solution(16714106898499282462)
XLA Ops:
  0.0 0.0 copy-start
  0.0 0.7 copy-done
  0.7 0.7 fusion.4
  1.4 0.8 fusion.1
  2.2 0.6 broadcast_in_dim.38
  2.8 8.5 %all-to-all-start = ((bf16[8,40,128]{2,1,0:T(8,128)(2,1)}), bf16[8,40,128]{2,1,0:T(8,128)(2,1)S(1)}, u32[]{:S(2)}, u32[]{:S(2)}) async-start(bf16[8,40,128]{2,1,0:T(8,128)(2,1)} %broadcast_in_dim.38), calls=%async_computation | async-start | bytes 163840 | tf_op jit(solution)/shard_map/all_to_all | solution.py:22
  11.3 0.9 reduce-precision_convert_fusion
  12.2 0.1 copy.23
  12.4 0.1 copy.24
  12.5 0.2 maximum_bitcast_fusion
  12.7 0.1 broadcast_select_fusion
  12.8 7.0 %all-to-all-done = bf16[8,40,128]{2,1,0:T(8,128)(2,1)S(1)} async-done(((bf16[8,40,128]{2,1,0:T(8,128)(2,1)}), bf16[8,40,128]{2,1,0:T(8,128)(2,1)S(1)}, u32[]{:S(2)}, u32[]{:S(2)}) %all-to-all-start) | async-done | bytes 81952 | tf_op jit(solution)/shard_map/all_to_all | solution.py:22
  19.9 0.2 broadcast_in_dim.42
  20.1 0.2 broadcast_in_dim.40
  20.4 0.2 pad_maximum_fusion
  20.5 36.3 %all_to_all.10.own_ref = bf16[16,576,128]{2,1,0:T(8,128)(2,1)S(1)} all-to-all(bf16[16,576,128]{2,1,0:T(8,128)(2,1)S(1)} %bitcast.45), channel_id=1, replica_groups=mesh['yl'=2,'core'=2,'yh'=2,'x'=4,'z'=8] {'yl','yh','x'}, dimensions={0} | all-to-all | bytes 4718592 | tf_op jit(solution)/shard_map/all_to_all | solution.py:22
  56.9 0.0 copy-start.1
  56.9 0.0 collective-permute-start
  56.9 0.7 pad_add_fusion.1.pos_ref
  57.6 4.0 %collective-permute-done.other_ref = bf16[16,576,128]{2,1,0:T(8,128)(2,1)} collective-permute-done((bf16[16,576,128]{2,1,0:T(8,128)(2,1)S(1)}, bf16[16,576,128]{2,1,0:T(8,128)(2,1)}, u32[]{:S(2)}, u32[]{:S(2)}) %collective-permute-start) | collective-permute-done | bytes 2359328 | tf_op jit(solution)/shard_map/ppermute | solution.py:18
  61.5 0.0 copy-done.1
  61.5 4.7 %solve.1 = (bf16[8,32,1024]{2,1,0:T(8,128)(2,1)}, bf16[32,1024]{1,0:T(8,128)(2,1)}) custom-call(s32[2]{0:T(128)} %pad_add_fusion.1.pos_ref, bf16[16,576,128]{2,1,0:T(8,128)(2,1)} %copy-done.1, bf16[16,576,128]{2,1,0:T(8,128)(2,1)} %collective-permute-done.other_ref), custom_call_target="tpu_custom_call" | custom-call | tf_op jit(solution)/shard_map/solve/pallas_call | solution.py:135
  66.2 0.6 collective-permute-start.3
  66.8 2.7 %collective-permute-start.7 = (bf16[8,32,1024]{2,1,0:T(8,128)(2,1)}, bf16[8,32,1024]{2,1,0:T(8,128)(2,1)S(1)}, u32[]{:S(2)}, u32[]{:S(2)}) collective-permute-start(bf16[8,32,1024]{2,1,0:T(8,128)(2,1)} %get-tuple-element.8.refs_0_), channel_id=1, source_target_pairs={{0,7},{1,0},{2,1},{3,2},{4,3},{5,4},{6,5},{7,6},{8,15},{9,8},{10,9... | collective-permute-start | bytes 1572872 | tf_op jit(solution)/shard_map/ppermute | solution.py:18
  69.5 12.2 %collective-permute-done.3.refs_1_ = bf16[8,32,1024]{2,1,0:T(8,128)(2,1)S(1)} collective-permute-done((bf16[8,32,1024]{2,1,0:T(8,128)(2,1)}, bf16[8,32,1024]{2,1,0:T(8,128)(2,1)S(1)}, u32[]{:S(2)}, u32[]{:S(2)}) %collective-permute-start.3) | collective-permute-done | bytes 524320 | tf_op jit(solution)/shard_map/ppermute | solution.py:18
  81.6 0.0 copy-start.2
  81.6 0.0 collective-permute-start.4
  81.6 0.0 collective-permute-done.7.refs_7_
  81.6 0.0 copy-start.3
  81.6 3.2 %collective-permute-start.8 = (bf16[8,32,1024]{2,1,0:T(8,128)(2,1)S(1)}, bf16[8,32,1024]{2,1,0:T(8,128)(2,1)S(1)}, u32[]{:S(2)}, u32[]{:S(2)}) collective-permute-start(bf16[8,32,1024]{2,1,0:T(8,128)(2,1)S(1)} %collective-permute-done.7.refs_7_), channel_id=1, source_target_pairs={{0,7},{1,0},{2,1},{3,2},{4,3},{5,4},{6,5},{7,6},{8,15},{9,8},{10,9... | collective-permute-start | bytes 1572872 | tf_op jit(solution)/shard_map/ppermute | solution.py:18
  84.9 11.1 %collective-permute-done.4.refs_2_ = bf16[8,32,1024]{2,1,0:T(8,128)(2,1)S(1)} collective-permute-done((bf16[8,32,1024]{2,1,0:T(8,128)(2,1)S(1)}, bf16[8,32,1024]{2,1,0:T(8,128)(2,1)S(1)}, u32[]{:S(2)}, u32[]{:S(2)}) %collective-permute-start.4) | collective-permute-done | bytes 524320 | tf_op jit(solution)/shard_map/ppermute | solution.py:18
  96.0 0.0 copy-start.4
  96.0 0.0 collective-permute-start.5
  96.0 0.0 collective-permute-done.8.refs_6_
  96.0 0.0 copy-start.5
  96.0 3.2 %collective-permute-start.9 = (bf16[8,32,1024]{2,1,0:T(8,128)(2,1)S(1)}, bf16[8,32,1024]{2,1,0:T(8,128)(2,1)S(1)}, u32[]{:S(2)}, u32[]{:S(2)}) collective-permute-start(bf16[8,32,1024]{2,1,0:T(8,128)(2,1)S(1)} %collective-permute-done.8.refs_6_), channel_id=1, source_target_pairs={{0,7},{1,0},{2,1},{3,2},{4,3},{5,4},{6,5},{7,6},{8,15},{9,8},{10,9... | collective-permute-start | bytes 1572872 | tf_op jit(solution)/shard_map/ppermute | solution.py:18
  99.2 10.2 %collective-permute-done.5.refs_3_ = bf16[8,32,1024]{2,1,0:T(8,128)(2,1)S(1)} collective-permute-done((bf16[8,32,1024]{2,1,0:T(8,128)(2,1)S(1)}, bf16[8,32,1024]{2,1,0:T(8,128)(2,1)S(1)}, u32[]{:S(2)}, u32[]{:S(2)}) %collective-permute-start.5) | collective-permute-done | bytes 524320 | tf_op jit(solution)/shard_map/ppermute | solution.py:18
  109.4 0.0 copy-start.6
  109.4 0.0 collective-permute-start.6
  109.4 1.8 %collective-permute-start.1 = (bf16[32,1024]{1,0:T(8,128)(2,1)}, bf16[32,1024]{1,0:T(8,128)(2,1)S(1)}, u32[]{:S(2)}, u32[]{:S(2)}) collective-permute-start(bf16[32,1024]{1,0:T(8,128)(2,1)} %get-tuple-element.7.m0), channel_id=1, source_target_pairs={{0,128},{128,0},{1,129},{129,1},{2,130},{130,2},{3,131},{131,3},{4... | collective-permute-start | bytes 196616 | tf_op jit(solution)/shard_map/ppermute | solution.py:18
  111.2 2.7 %collective-permute-done.1.m1 = bf16[32,1024]{1,0:T(8,128)(2,1)S(1)} collective-permute-done((bf16[32,1024]{1,0:T(8,128)(2,1)}, bf16[32,1024]{1,0:T(8,128)(2,1)S(1)}, u32[]{:S(2)}, u32[]{:S(2)}) %collective-permute-start.1) | collective-permute-done | bytes 65568 | tf_op jit(solution)/shard_map/ppermute | solution.py:18
  113.9 0.0 copy-start.8
  113.9 0.9 pad_maximum_fusion.1
  114.8 0.1 collective-permute-start.2
  114.9 0.7 pad_add_fusion.pos_ref
  115.5 0.7 collective-permute-done.2.m2
  116.2 0.0 copy-start.9
  116.2 0.0 collective-permute-done.9.refs_5_
  116.2 0.0 copy-start.7
  116.2 5.9 %collective-permute-done.6.refs_4_ = bf16[8,32,1024]{2,1,0:T(8,128)(2,1)} collective-permute-done((bf16[8,32,1024]{2,1,0:T(8,128)(2,1)S(1)}, bf16[8,32,1024]{2,1,0:T(8,128)(2,1)}, u32[]{:S(2)}, u32[]{:S(2)}) %collective-permute-start.6) | collective-permute-done | bytes 524320 | tf_op jit(solution)/shard_map/ppermute | solution.py:18
  122.1 0.0 copy-done.2
  122.2 0.0 copy-done.3
  122.2 0.0 copy-done.4
  122.2 0.0 copy-done.5
  122.2 0.0 copy-done.6
  122.2 0.0 copy-done.8
  122.2 0.0 copy-done.9
  122.2 0.0 copy-done.7
  122.2 5.1 %product.1 = f32[128,1,2048]{2,1,0:T(1,128)} custom-call(s32[3]{0:T(128)} %pad_add_fusion.pos_ref, bf16[32,1024]{1,0:T(8,128)(2,1)} %get-tuple-element.7.m0, bf16[32,1024]{1,0:T(8,128)(2,1)} %copy-done.8, bf16[2,32,1024]{2,1,0:T(8,128)(2,1)} %copy-done.9, bf16[8,32,1024]{2,1,0:T(8,128)(2,1)} %get-tuple-element.8.refs_0_, bf16[8,32,1024]{2,1,0:T(8,128)(2,1)} %copy-done.2, ...), custom_call_target="tpu_custom_call" | custom-call | tf_op jit(solution)/shard_map/product/pallas_call | solution.py:157
  (8 shorter events, 0.1 us)
Async XLA Ops:
  0.0 0.7 copy-start
  2.8 17.0 %all-to-all-start = ((bf16[8,40,128]{2,1,0:T(8,128)(2,1)}), bf16[8,40,128]{2,1,0:T(8,128)(2,1)S(1)}, u32[]{:S(2)}, u32[]{:S(2)}) async-start(bf16[8,40,128]{2,1,0:T(8,128)(2,1)} %broadcast_in_dim.38), calls=%async_computation | async-start | bytes 163840 | tf_op jit(solution)/shard_map/all_to_all | solution.py:22
  56.9 4.7 %copy-start.1 = (bf16[16,576,128]{2,1,0:T(8,128)(2,1)}, bf16[16,576,128]{2,1,0:T(8,128)(2,1)S(1)}, u32[]{:S(2)}) copy-start(bf16[16,576,128]{2,1,0:T(8,128)(2,1)S(1)} %all_to_all.10.own_ref) | copy-start | bytes 7077892
  56.9 4.7 %collective-permute-start = (bf16[16,576,128]{2,1,0:T(8,128)(2,1)S(1)}, bf16[16,576,128]{2,1,0:T(8,128)(2,1)}, u32[]{:S(2)}, u32[]{:S(2)}) collective-permute-start(bf16[16,576,128]{2,1,0:T(8,128)(2,1)S(1)} %all_to_all.10.own_ref), channel_id=1, source_target_pairs={{0,64},{64,0},{1,65},{65,1},{2,66},{66,2},{3,67},{67,3},{4,68},{68... | collective-permute-start | bytes 7077896 | tf_op jit(solution)/shard_map/ppermute | solution.py:18
  66.2 15.4 %collective-permute-start.3 = (bf16[8,32,1024]{2,1,0:T(8,128)(2,1)}, bf16[8,32,1024]{2,1,0:T(8,128)(2,1)S(1)}, u32[]{:S(2)}, u32[]{:S(2)}) collective-permute-start(bf16[8,32,1024]{2,1,0:T(8,128)(2,1)} %get-tuple-element.8.refs_0_), channel_id=1, source_target_pairs={{0,1},{1,2},{2,3},{3,4},{4,5},{5,6},{6,7},{7,0},{8,9},{9,10},{10,1... | collective-permute-start | bytes 1572872 | tf_op jit(solution)/shard_map/ppermute | solution.py:18
  66.8 14.8 %collective-permute-start.7 = (bf16[8,32,1024]{2,1,0:T(8,128)(2,1)}, bf16[8,32,1024]{2,1,0:T(8,128)(2,1)S(1)}, u32[]{:S(2)}, u32[]{:S(2)}) collective-permute-start(bf16[8,32,1024]{2,1,0:T(8,128)(2,1)} %get-tuple-element.8.refs_0_), channel_id=1, source_target_pairs={{0,7},{1,0},{2,1},{3,2},{4,3},{5,4},{6,5},{7,6},{8,15},{9,8},{10,9... | collective-permute-start | bytes 1572872 | tf_op jit(solution)/shard_map/ppermute | solution.py:18
  81.6 40.5 %copy-start.2 = (bf16[8,32,1024]{2,1,0:T(8,128)(2,1)}, bf16[8,32,1024]{2,1,0:T(8,128)(2,1)S(1)}, u32[]{:S(2)}) copy-start(bf16[8,32,1024]{2,1,0:T(8,128)(2,1)S(1)} %collective-permute-done.3.refs_1_) | copy-start | bytes 1572868
  81.6 14.3 %collective-permute-start.4 = (bf16[8,32,1024]{2,1,0:T(8,128)(2,1)S(1)}, bf16[8,32,1024]{2,1,0:T(8,128)(2,1)S(1)}, u32[]{:S(2)}, u32[]{:S(2)}) collective-permute-start(bf16[8,32,1024]{2,1,0:T(8,128)(2,1)S(1)} %collective-permute-done.3.refs_1_), channel_id=1, source_target_pairs={{0,1},{1,2},{2,3},{3,4},{4,5},{5,6},{6,7},{7,0},{8,9},{9,10},{10,1... | collective-permute-start | bytes 1572872 | tf_op jit(solution)/shard_map/ppermute | solution.py:18
  81.6 40.5 %copy-start.3 = (bf16[8,32,1024]{2,1,0:T(8,128)(2,1)}, bf16[8,32,1024]{2,1,0:T(8,128)(2,1)S(1)}, u32[]{:S(2)}) copy-start(bf16[8,32,1024]{2,1,0:T(8,128)(2,1)S(1)} %collective-permute-done.7.refs_7_) | copy-start | bytes 1572868
  81.6 14.3 %collective-permute-start.8 = (bf16[8,32,1024]{2,1,0:T(8,128)(2,1)S(1)}, bf16[8,32,1024]{2,1,0:T(8,128)(2,1)S(1)}, u32[]{:S(2)}, u32[]{:S(2)}) collective-permute-start(bf16[8,32,1024]{2,1,0:T(8,128)(2,1)S(1)} %collective-permute-done.7.refs_7_), channel_id=1, source_target_pairs={{0,7},{1,0},{2,1},{3,2},{4,3},{5,4},{6,5},{7,6},{8,15},{9,8},{10,9... | collective-permute-start | bytes 1572872 | tf_op jit(solution)/shard_map/ppermute | solution.py:18
  96.0 26.2 %copy-start.4 = (bf16[8,32,1024]{2,1,0:T(8,128)(2,1)}, bf16[8,32,1024]{2,1,0:T(8,128)(2,1)S(1)}, u32[]{:S(2)}) copy-start(bf16[8,32,1024]{2,1,0:T(8,128)(2,1)S(1)} %collective-permute-done.4.refs_2_) | copy-start | bytes 1572868
  96.0 13.5 %collective-permute-start.5 = (bf16[8,32,1024]{2,1,0:T(8,128)(2,1)S(1)}, bf16[8,32,1024]{2,1,0:T(8,128)(2,1)S(1)}, u32[]{:S(2)}, u32[]{:S(2)}) collective-permute-start(bf16[8,32,1024]{2,1,0:T(8,128)(2,1)S(1)} %collective-permute-done.4.refs_2_), channel_id=1, source_target_pairs={{0,1},{1,2},{2,3},{3,4},{4,5},{5,6},{6,7},{7,0},{8,9},{9,10},{10,1... | collective-permute-start | bytes 1572872 | tf_op jit(solution)/shard_map/ppermute | solution.py:18
  96.0 26.2 %copy-start.5 = (bf16[8,32,1024]{2,1,0:T(8,128)(2,1)}, bf16[8,32,1024]{2,1,0:T(8,128)(2,1)S(1)}, u32[]{:S(2)}) copy-start(bf16[8,32,1024]{2,1,0:T(8,128)(2,1)S(1)} %collective-permute-done.8.refs_6_) | copy-start | bytes 1572868
  96.0 20.3 %collective-permute-start.9 = (bf16[8,32,1024]{2,1,0:T(8,128)(2,1)S(1)}, bf16[8,32,1024]{2,1,0:T(8,128)(2,1)S(1)}, u32[]{:S(2)}, u32[]{:S(2)}) collective-permute-start(bf16[8,32,1024]{2,1,0:T(8,128)(2,1)S(1)} %collective-permute-done.8.refs_6_), channel_id=1, source_target_pairs={{0,7},{1,0},{2,1},{3,2},{4,3},{5,4},{6,5},{7,6},{8,15},{9,8},{10,9... | collective-permute-start | bytes 1572872 | tf_op jit(solution)/shard_map/ppermute | solution.py:18
  109.4 12.7 %copy-start.6 = (bf16[8,32,1024]{2,1,0:T(8,128)(2,1)}, bf16[8,32,1024]{2,1,0:T(8,128)(2,1)S(1)}, u32[]{:S(2)}) copy-start(bf16[8,32,1024]{2,1,0:T(8,128)(2,1)S(1)} %collective-permute-done.5.refs_3_) | copy-start | bytes 1572868
  109.4 12.7 %collective-permute-start.6 = (bf16[8,32,1024]{2,1,0:T(8,128)(2,1)S(1)}, bf16[8,32,1024]{2,1,0:T(8,128)(2,1)}, u32[]{:S(2)}, u32[]{:S(2)}) collective-permute-start(bf16[8,32,1024]{2,1,0:T(8,128)(2,1)S(1)} %collective-permute-done.5.refs_3_), channel_id=1, source_target_pairs={{0,1},{1,2},{2,3},{3,4},{4,5},{5,6},{6,7},{7,0},{8,9},{9,10},{10,1... | collective-permute-start | bytes 1572872 | tf_op jit(solution)/shard_map/ppermute | solution.py:18
  109.4 4.5 %collective-permute-start.1 = (bf16[32,1024]{1,0:T(8,128)(2,1)}, bf16[32,1024]{1,0:T(8,128)(2,1)S(1)}, u32[]{:S(2)}, u32[]{:S(2)}) collective-permute-start(bf16[32,1024]{1,0:T(8,128)(2,1)} %get-tuple-element.7.m0), channel_id=1, source_target_pairs={{0,128},{128,0},{1,129},{129,1},{2,130},{130,2},{3,131},{131,3},{4... | collective-permute-start | bytes 196616 | tf_op jit(solution)/shard_map/ppermute | solution.py:18
  113.9 8.3 %copy-start.8 = (bf16[32,1024]{1,0:T(8,128)(2,1)}, bf16[32,1024]{1,0:T(8,128)(2,1)S(1)}, u32[]{:S(2)}) copy-start(bf16[32,1024]{1,0:T(8,128)(2,1)S(1)} %collective-permute-done.1.m1) | copy-start | bytes 196612
  114.8 1.4 %collective-permute-start.2 = (bf16[2,32,1024]{2,1,0:T(8,128)(2,1)S(1)}, bf16[2,32,1024]{2,1,0:T(8,128)(2,1)S(1)}, u32[]{:S(2)}, u32[]{:S(2)}) collective-permute-start(bf16[2,32,1024]{2,1,0:T(8,128)(2,1)S(1)} %pad_maximum_fusion.1), channel_id=1, source_target_pairs={{0,64},{64,0},{1,65},{65,1},{2,66},{66,2},{3,67},{67,3},{4,68},{68... | collective-permute-start | bytes 393224 | tf_op jit(solution)/shard_map/ppermute | solution.py:18
  116.2 6.0 %copy-start.9 = (bf16[2,32,1024]{2,1,0:T(8,128)(2,1)}, bf16[2,32,1024]{2,1,0:T(8,128)(2,1)S(1)}, u32[]{:S(2)}) copy-start(bf16[2,32,1024]{2,1,0:T(8,128)(2,1)S(1)} %collective-permute-done.2.m2) | copy-start | bytes 393220
  116.2 6.0 %copy-start.7 = (bf16[8,32,1024]{2,1,0:T(8,128)(2,1)}, bf16[8,32,1024]{2,1,0:T(8,128)(2,1)S(1)}, u32[]{:S(2)}) copy-start(bf16[8,32,1024]{2,1,0:T(8,128)(2,1)S(1)} %collective-permute-done.9.refs_5_) | copy-start | bytes 1572868

commit v3 on v2

v3 whole, which is shorter than its diff:
```python
import jax
import jax.numpy as jnp
from jax import lax
from jax.experimental import pallas as pl
from jax.experimental.pallas import tpu as pltpu
from jax.sharding import Mesh, PartitionSpec as P


FAC = ("yl", "core")
COL = ("yh", "x", "z")
NT = (((1,), (1,)), ((), ()))
BF = jnp.bfloat16
F32 = jnp.float32
LANES = 128


def shift(a, axis, by=1):
    n = lax.axis_size(axis)
    return lax.ppermute(a, axis, [(i, (i + by) % n) for i in range(n)])


def opposite(a, axes):
    n = lax.axis_size(axes)
    return lax.ppermute(a, axes, [(i, n - 1 - i) for i in range(n)])


def exchange(a, axes):
    return lax.all_to_all(a, axes, 0, 0, tiled=True)


def by_index(mine, other, index):
    first = index == 0
    return jnp.stack([jnp.where(first, mine, other), jnp.where(first, other, mine)])


def split(a):
    hi = lax.reduce_precision(a, 8, 7)
    return hi.astype(BF), (a - hi).astype(BF)


def dot(a, b):
    return jnp.dot(a, b, preferred_element_type=F32)


def solve_panels(panels, pos_ref, own_ref, other_ref, rights, before, out_ref):
    peers, _, lanes = own_ref.shape
    half = peers // 2
    share, w = 32, rights.shape[3]

    def run(pair):
        def square(ref, yl, first):
            parts = [
                ref[yl * half : (yl + 1) * half, r : r + 32, :].reshape(
                    half * 32, lanes
                )
                for r in (first, first + 32)
            ]
            return jnp.concatenate(parts, axis=1)

        solved = [
            ref[:, :, i * w : (i + 1) * w].reshape(half * share, w)
            for ref in before
            for i in range(2)
        ]
        for n, p in enumerate(panels):
            yl, core = divmod(p, 2)
            ref = pair[core]
            r = rights[yl, core]
            for q in range(p):
                r = r - dot(solved[q], square(ref, yl, 128 + 64 * q))
            rhi = r.astype(BF)
            rlo = (r - rhi.astype(F32)).astype(BF)
            dhi = square(ref, yl, 0)
            y = (dot(rlo, dhi) + dot(rhi, square(ref, yl, 64))) + dot(rhi, dhi)
            y = y.astype(BF)
            solved.append(y)
            out_ref[:, :, n * w : (n + 1) * w] = y.reshape(half, share, w)

    @pl.when(pos_ref[0] == 0)
    def _():
        run((own_ref, other_ref))

    @pl.when(pos_ref[0] == 1)
    def _():
        run((other_ref, own_ref))


def first_kernel(pos_ref, own, other, rights, out_ref):
    solve_panels((0, 1), pos_ref, own, other, rights, (), out_ref)


def second_kernel(pos_ref, own, other, rights, a_ref, out_ref, mine_ref):
    solve_panels((2, 3), pos_ref, own, other, rights, (a_ref,), out_ref)
    wide = a_ref.shape[2]
    mine_ref[:, :wide] = a_ref[0]
    mine_ref[:, wide:] = out_ref[0]


def product_kernel(pos_ref, m0, m1, m2, *refs):
    blocks, out_ref, own, stage = refs[:-3], refs[-3], refs[-2], refs[-1]
    nz = stage.shape[0]
    z, yl, core, yh, x = (pos_ref[i] for i in range(5))
    share = m0.shape[0]
    own[2 * yl + core] = m0[...]
    own[2 * (1 - yl) + core] = m1[...]
    own[2 * yl + (1 - core)] = m2[0]
    own[2 * (1 - yl) + (1 - core)] = m2[1]
    groups = stage.shape[1]
    wide = stage.shape[3] // 2
    per = nz + 1
    for c in range(2):
        for k in range(per):
            src = blocks[c * per + k]
            if k < nz - 1:
                off = k if k < nz // 2 else nz // 2 - 1 - k
                part = slice(0, groups)
            else:
                off = nz // 2
                part = slice(0, groups // 2) if k == nz - 1 else slice(groups // 2, groups)
            stage[
                lax.rem(z + nz - off, nz), part, :, c * wide : (c + 1) * wide
            ] = src[...]
    lhs = own[...].reshape(4 * share, own.shape[2])
    cols = nz * share
    for g in range(groups):
        dyh, dx = divmod(g, 4)
        rhs = stage[:, g].reshape(cols, stage.shape[3])
        at = lax.rem(yh + dyh, 2) * 4 + lax.rem(x + dx, 4)
        out_ref[:, 0, pl.ds(pl.multiple_of(at * cols, cols), cols)] = lax.dot_general(
            lhs, rhs, NT, preferred_element_type=F32
        )


def z_ring(chunks):
    half = lax.axis_size("z") // 2
    ups = [[c] for c in chunks]
    downs = [[c] for c in chunks]
    for _ in range(1, half):
        for u, d in zip(ups, downs):
            u.append(shift(u[-1], "z", 1))
            d.append(shift(d[-1], "z", -1))
    out = []
    for u, d in zip(ups, downs):
        h = u[-1].shape[0] // 2
        last = [shift(u[-1][:h], "z", 1), shift(d[-1][h:], "z", -1)]
        out.extend(u + d[1:] + last)
    return out


def compute(lower_factor, panel_inverse, right_side, fill):
    w, kw = panel_inverse.shape[2:]
    fac = lax.axis_index(FAC)
    yl, core, yh, x, z = (lax.axis_index(a) for a in FAC + COL)
    nz, nx = lax.axis_size("z"), lax.axis_size("x")
    panels = fill.shape[0]

    hi, lo = split(panel_inverse[0, 0].T)
    keep = lax.dynamic_slice_in_dim(fill, fac, 1, 0)[0, : panels - 1] == 1
    low = lower_factor[0, 0, : panels - 1].transpose(0, 2, 1)
    low = jnp.where(keep[:, None, None], low, jnp.zeros_like(low))
    rows = jnp.concatenate([hi[None], lo[None], low], axis=0)
    nt = rows.shape[0]
    rows = rows.reshape(nt, kw, w // LANES, LANES).transpose(0, 2, 1, 3)
    rows = rows.reshape(nt * w // LANES * kw, LANES)
    rows = jnp.broadcast_to(rows[None], (nz,) + rows.shape)
    got = exchange(rows, "z")
    got = got.reshape(nz, nt * w // LANES, kw, LANES).transpose(1, 0, 2, 3)
    got = got.reshape(-1, LANES)
    npeer = 2 * 2 * nx
    got = jnp.broadcast_to(got[None], (npeer,) + got.shape)
    held = exchange(got, ("yl", "yh", "x"))
    other = shift(held, "core")

    share = right_side.shape[3] // panels
    bt = right_side[0, 0].T
    bo = shift(bt, "core")
    bt = by_index(bt, bo, core)
    bt = bt.reshape(2, 2, 2, share, w)
    bt = lax.dynamic_index_in_dim(bt, core, 2, keepdims=False)
    same = lax.dynamic_index_in_dim(bt, yl, 1, keepdims=False)
    cross = lax.dynamic_index_in_dim(bt, 1 - yl, 1, keepdims=False)
    near = jnp.stack([same, shift(same, "yh")])
    far = jnp.stack([shift(cross, "yl"), opposite(cross, ("yl", "yh"))])
    bt = by_index(near, far, yl)
    parts = [bt] + [shift(bt, "x", nx - k) for k in range(1, nx)]
    rights = jnp.stack(parts, axis=2).transpose(0, 3, 1, 2, 4, 5)
    rights = rights.reshape(2, 2, 2 * nx * share, w)

    vm = pl.BlockSpec(memory_space=pltpu.VMEM)
    sm = pl.BlockSpec(memory_space=pltpu.SMEM)
    pos = jnp.stack([core]).astype(jnp.int32)
    half = jax.ShapeDtypeStruct((npeer // 2, share, panels * w // 2), BF)
    params = pltpu.CompilerParams(vmem_limit_bytes=16 * 1024 * 1024)
    first = pl.pallas_call(
        first_kernel,
        out_shape=half,
        in_specs=[sm] + [vm] * 3,
        out_specs=vm,
        compiler_params=params,
        name="solve_a",
    )(pos, held, other, rights)
    second, mine = pl.pallas_call(
        second_kernel,
        out_shape=(half, jax.ShapeDtypeStruct((share, panels * w), BF)),
        in_specs=[sm] + [vm] * 4,
        out_specs=(vm, vm),
        compiler_params=params,
        name="solve_b",
    )(pos, held, other, rights, first)

    m1 = shift(mine, "yl")
    m2 = shift(jnp.stack([mine, m1]), "core")
    ring = z_ring([first, second])
    return pl.pallas_call(
        product_kernel,
        out_shape=jax.ShapeDtypeStruct(
            (panels * share, 1, npeer // 2 * nz * share), F32
        ),
        in_specs=[sm] + [vm] * (3 + len(ring)),
        out_specs=vm,
        scratch_shapes=[
            pltpu.VMEM((panels,) + mine.shape, BF),
            pltpu.VMEM((nz, npeer // 2, share, panels * w), BF),
        ],
        compiler_params=pltpu.CompilerParams(vmem_limit_bytes=20 * 1024 * 1024),
        name="product",
    )(jnp.stack([z, yl, core, yh, x]).astype(jnp.int32), mine, m1, m2, *ring)


def solution(mesh):
    fine = Mesh(mesh.devices.reshape(2, 2, 2, 4, 8), FAC + COL)
    return jax.shard_map(
        compute,
        mesh=fine,
        in_specs=(
            P(None, FAC, None, None, COL),
            P(None, FAC, None, COL),
            P(None, FAC, None, COL),
            P(),
        ),
        out_specs=P(COL, FAC, None),
        check_vma=False,
    )
```

time: 128 us -> 127 us (level)
  waiting for transfers between devices: 53.7 us -> 41.8 us
  starting transfers between devices: 20 us -> 28.5 us
  blocking collectives: 36.3 us -> 41.5 us
  Pallas kernels: 9.79 us -> 5.71 us
  local copies, waits for them, and re-layouts: 2.13 us -> 5.71 us
  other arithmetic: 5.08 us -> 2.32 us
    ppermute x10 -> x25, starting transfers between devices: 11.6 us -> 27.4 us  [shift(): return lax.ppermute(a, axis, [(i, (i + by) % n) for i in range(n)])]
    all_to_all x1 -> x0, starting transfers between devices: 8.47 us -> none  [exchange(): return lax.all_to_all(a, axes, 0, 0, tiled=True)]
    all_to_all x1 -> x0, waiting for transfers between devices: 7 us -> none  [exchange(): return lax.all_to_all(a, axes, 0, 0, tiled=True)]
    ppermute x10 -> x25, waiting for transfers between devices: 46.7 us -> 40.6 us  [shift(): return lax.ppermute(a, axis, [(i, (i + by) % n) for i in range(n)])]
    all_to_all x1 -> x2, blocking collectives: 36.3 us -> 41.5 us  [exchange(): return lax.all_to_all(a, axes, 0, 0, tiled=True)]
    pallas_call x2 -> x3, Pallas kernels: 9.79 us -> 5.71 us  [the longest x1 4.06 us: compute(): pl.pallas_call(product_kernel, out_shape=jax.ShapeDtypeStruct((panels * s...]
    slice x0 -> x4, local copies, waits for them, and re-layouts: none -> 2.62 us  [z_ring(): last = [shift(u[-1][:h], 'z', 1), shift(d[-1][h:], 'z', -1)]]
    unnamed x20 -> x13, local copies, waits for them, and re-layouts: 0.72 us -> 2.69 us
  transfers between devices with their start and end apart: 11 -> 26, of which waited for: 8 -> 14; matrix products, arithmetic and copies ran while one was open for 3% -> 3% of each run, Pallas kernels for 0% -> 0%
where the time goes in v3:
time: 127 us; the launch traced here: 126 us
  waiting for transfers between devices  41.8 us (33%)
  blocking collectives  41.5 us (33%)
  starting transfers between devices  28.5 us (22%)
  local copies, waits for them, and re-layouts  5.71 us (4%)
  Pallas kernels  5.71 us (4%)
  other arithmetic  2.32 us (2%)
    all_to_all x2, blocking collectives, exchange(): return lax.all_to_all(a, axes, 0, 0, tiled=True)  41.5 us
    ppermute x25, waiting for transfers between devices, shift(): return lax.ppermute(a, axis, [(i, (i + by) % n) for i in range(n)])  40.6 us
    ppermute x25, starting transfers between devices, shift(): return lax.ppermute(a, axis, [(i, (i + by) % n) for i in range(n)])  27.4 us
    pallas_call x1, Pallas kernels, compute(): pl.pallas_call(product_kernel, out_shape=jax.ShapeDtypeStruct((panels * s...  4.06 us
    unnamed x13, local copies, waits for them, and re-layouts  2.69 us
    slice x4, local copies, waits for them, and re-layouts, z_ring(): last = [shift(u[-1][:h], 'z', 1), shift(d[-1][h:], 'z', -1)]  2.62 us
  transfers between devices with their start and end apart: 26, of which 14 were waited for; matrix products, arithmetic and copies ran while one was open for 3% of the time, Pallas kernels for 0%

profile of v3, /device:TPU:8, one launch (start us, length us, event | category | flops | bytes accessed | tf_op | source)
XLA Modules:
  0.0 125.7 jit_solution(10420169260770803660)
XLA Ops:
  0.0 0.7 copy-done
  0.7 0.7 fusion.8
  1.4 0.8 fusion.5
  2.2 16.8 %all_to_all.10 = bf16[8,40,128]{2,1,0:T(8,128)(2,1)S(1)} all-to-all(bf16[8,40,128]{2,1,0:T(8,128)(2,1)S(1)} %broadcast_in_dim.31), channel_id=1, replica_groups=mesh['yl'=2,'core'=2,'yh'=2,'x'=4,'z'=8] {'z'}, dimensions={0} | all-to-all | bytes 163840 | tf_op jit(solution)/shard_map/all_to_all | solution.py:28
  19.1 0.2 broadcast_in_dim.33
  19.3 0.0 copy-start.5
  19.3 24.6 %all_to_all.11.own = bf16[16,320,128]{2,1,0:T(8,128)(2,1)S(1)} all-to-all(bf16[16,320,128]{2,1,0:T(8,128)(2,1)S(1)} %broadcast_in_dim.33), channel_id=1, replica_groups=mesh['yl'=2,'core'=2,'yh'=2,'x'=4,'z'=8] {'yl','yh','x'}, dimensions={0} | all-to-all | bytes 2621440 | tf_op jit(solution)/shard_map/all_to_all | solution.py:28
  44.0 0.0 collective-permute-start
  44.0 0.1 copy.34
  44.1 0.6 collective-permute-start.1
  44.7 2.5 %collective-permute-done.1 = f32[128,256]{1,0:T(8,128)S(1)} collective-permute-done((f32[128,256]{1,0:T(8,128)S(1)}, f32[128,256]{1,0:T(8,128)S(1)}, u32[]{:S(2)}, u32[]{:S(2)}) %collective-permute-start.1) | collective-permute-done | bytes 131104 | tf_op jit(solution)/shard_map/ppermute | solution.py:19
  47.3 2.2 %collective-permute-start.2 = (f32[2,32,256]{2,1,0:T(8,128)S(1)}, f32[2,32,256]{2,1,0:T(8,128)S(1)}, u32[]{:S(2)}, u32[]{:S(2)}) collective-permute-start(f32[2,32,256]{2,1,0:T(8,128)S(1)} %get-tuple-element.15), channel_id=1, source_target_pairs={{0,32},{32,0},{1,33},{33,1},{2,34},{34,2},{3,35},{35,3},{4,36},{36... | collective-permute-start | bytes 196616 | tf_op jit(solution)/shard_map/ppermute | solution.py:19
  49.5 1.1 collective-permute-start.4
  50.6 1.5 %collective-permute-start.3 = (f32[2,32,256]{2,1,0:T(8,128)S(1)}, f32[2,32,256]{2,1,0:T(8,128)S(1)}, u32[]{:S(2)}, u32[]{:S(2)}) collective-permute-start(f32[2,32,256]{2,1,0:T(8,128)S(1)} %get-tuple-element.14), channel_id=1, source_target_pairs={{0,128},{128,0},{1,129},{129,1},{2,130},{130,2},{3,131},{131,3},{4... | collective-permute-start | bytes 196616 | tf_op jit(solution)/shard_map/ppermute | solution.py:19
  52.1 1.1 collective-permute-done.2
  53.1 1.2 collective-permute-done.4
  54.4 0.5 collective-permute-done.3
  54.9 1.2 collective-permute-start.6
  56.1 2.1 %collective-permute-start.5 = (f32[2,2,2,32,256]{4,3,1,2,0:T(8,128)S(1)}, f32[2,2,2,32,256]{4,3,1,2,0:T(8,128)S(1)}, u32[]{:S(2)}, u32[]{:S(2)}) collective-permute-start(f32[2,2,2,32,256]{4,3,1,2,0:T(8,128)S(1)} %get-tuple-element.10), channel_id=1, source_target_pairs={{0,24},{8,0},{16,8},{24,16},{1,25},{9,1},{17,9},{25,17},{2,26},{10... | collective-permute-start | bytes 786440 | tf_op jit(solution)/shard_map/ppermute | solution.py:19
  58.3 7.5 %collective-permute-done.6 = f32[2,2,2,32,256]{4,3,1,2,0:T(8,128)S(1)} collective-permute-done((f32[2,2,2,32,256]{4,3,1,2,0:T(8,128)S(1)}, f32[2,2,2,32,256]{4,3,1,2,0:T(8,128)S(1)}, u32[]{:S(2)}, u32[]{:S(2)}) %collective-permute-start.6) | collective-permute-done | bytes 262176 | tf_op jit(solution)/shard_map/ppermute | solution.py:19
  65.7 1.5 %collective-permute-done.5 = f32[2,2,2,32,256]{4,3,1,2,0:T(8,128)S(1)} collective-permute-done((f32[2,2,2,32,256]{4,3,1,2,0:T(8,128)S(1)}, f32[2,2,2,32,256]{4,3,1,2,0:T(8,128)S(1)}, u32[]{:S(2)}, u32[]{:S(2)}) %collective-permute-start.5) | collective-permute-done | bytes 262176 | tf_op jit(solution)/shard_map/ppermute | solution.py:19
  67.2 2.7 %collective-permute-done.7 = f32[2,2,2,32,256]{4,3,1,2,0:T(8,128)S(1)} collective-permute-done((f32[2,2,2,32,256]{4,3,1,2,0:T(8,128)S(1)}, f32[2,2,2,32,256]{4,3,1,2,0:T(8,128)S(1)}, u32[]{:S(2)}, u32[]{:S(2)}) %collective-permute-start.7) | collective-permute-done | bytes 262176 | tf_op jit(solution)/shard_map/ppermute | solution.py:19
  69.9 0.1 pad_maximum_fusion
  69.9 0.0 collective-permute-done.other
  70.0 0.7 solve_a.1.a_ref.refs_0_
  70.7 0.9 solve_b.1
  71.6 0.2 collective-permute-start.21
  71.8 1.9 %collective-permute-start.18 = (bf16[8,32,512]{2,1,0:T(8,128)(2,1)S(1)}, bf16[8,32,512]{2,1,0:T(8,128)(2,1)S(1)}, u32[]{:S(2)}, u32[]{:S(2)}) collective-permute-start(bf16[8,32,512]{2,1,0:T(8,128)(2,1)S(1)} %get-tuple-element.8.refs_9_), channel_id=1, source_target_pairs={{0,1},{1,2},{2,3},{3,4},{4,5},{5,6},{6,7},{7,0},{8,9},{9,10},{10,1... | collective-permute-start | bytes 786440 | tf_op jit(solution)/shard_map/ppermute | solution.py:19
  73.7 1.3 %collective-permute-start.13 = (bf16[8,32,512]{2,1,0:T(8,128)(2,1)S(1)}, bf16[8,32,512]{2,1,0:T(8,128)(2,1)S(1)}, u32[]{:S(2)}, u32[]{:S(2)}) collective-permute-start(bf16[8,32,512]{2,1,0:T(8,128)(2,1)S(1)} %solve_a.1.a_ref.refs_0_), channel_id=1, source_target_pairs={{0,7},{1,0},{2,1},{3,2},{4,3},{5,4},{6,5},{7,6},{8,15},{9,8},{10,9... | collective-permute-start | bytes 786440 | tf_op jit(solution)/shard_map/ppermute | solution.py:19
  75.1 0.7 collective-permute-start.10
  75.8 5.1 %collective-permute-done.21.refs_13_ = bf16[8,32,512]{2,1,0:T(8,128)(2,1)S(1)} collective-permute-done((bf16[8,32,512]{2,1,0:T(8,128)(2,1)S(1)}, bf16[8,32,512]{2,1,0:T(8,128)(2,1)S(1)}, u32[]{:S(2)}, u32[]{:S(2)}) %collective-permute-start.21) | collective-permute-done | bytes 262176 | tf_op jit(solution)/shard_map/ppermute | solution.py:19
  80.9 1.3 %collective-permute-start.22 = (bf16[8,32,512]{2,1,0:T(8,128)(2,1)S(1)}, bf16[8,32,512]{2,1,0:T(8,128)(2,1)S(1)}, u32[]{:S(2)}, u32[]{:S(2)}) collective-permute-start(bf16[8,32,512]{2,1,0:T(8,128)(2,1)S(1)} %collective-permute-done.21.refs_13_), channel_id=1, source_target_pairs={{0,7},{1,0},{2,1},{3,2},{4,3},{5,4},{6,5},{7,6},{8,15},{9,8},{10,9... | collective-permute-start | bytes 786440 | tf_op jit(solution)/shard_map/ppermute | solution.py:19
  82.2 0.0 collective-permute-done.18.refs_10_
  82.2 0.7 collective-permute-start.19
  82.9 3.6 %collective-permute-done.13.refs_4_ = bf16[8,32,512]{2,1,0:T(8,128)(2,1)S(1)} collective-permute-done((bf16[8,32,512]{2,1,0:T(8,128)(2,1)S(1)}, bf16[8,32,512]{2,1,0:T(8,128)(2,1)S(1)}, u32[]{:S(2)}, u32[]{:S(2)}) %collective-permute-start.13) | collective-permute-done | bytes 262176 | tf_op jit(solution)/shard_map/ppermute | solution.py:19
  86.5 1.3 %collective-permute-start.14 = (bf16[8,32,512]{2,1,0:T(8,128)(2,1)S(1)}, bf16[8,32,512]{2,1,0:T(8,128)(2,1)S(1)}, u32[]{:S(2)}, u32[]{:S(2)}) collective-permute-start(bf16[8,32,512]{2,1,0:T(8,128)(2,1)S(1)} %collective-permute-done.13.refs_4_), channel_id=1, source_target_pairs={{0,7},{1,0},{2,1},{3,2},{4,3},{5,4},{6,5},{7,6},{8,15},{9,8},{10,9... | collective-permute-start | bytes 786440 | tf_op jit(solution)/shard_map/ppermute | solution.py:19
  87.8 0.7 collective-permute-start.11
  88.5 3.6 %collective-permute-done.22.refs_14_ = bf16[8,32,512]{2,1,0:T(8,128)(2,1)S(1)} collective-permute-done((bf16[8,32,512]{2,1,0:T(8,128)(2,1)S(1)}, bf16[8,32,512]{2,1,0:T(8,128)(2,1)S(1)}, u32[]{:S(2)}, u32[]{:S(2)}) %collective-permute-start.22) | collective-permute-done | bytes 262176 | tf_op jit(solution)/shard_map/ppermute | solution.py:19
  92.1 1.3 %collective-permute-start.23 = (bf16[8,32,512]{2,1,0:T(8,128)(2,1)S(1)}, bf16[8,32,512]{2,1,0:T(8,128)(2,1)S(1)}, u32[]{:S(2)}, u32[]{:S(2)}) collective-permute-start(bf16[8,32,512]{2,1,0:T(8,128)(2,1)S(1)} %collective-permute-done.22.refs_14_), channel_id=1, source_target_pairs={{0,7},{1,0},{2,1},{3,2},{4,3},{5,4},{6,5},{7,6},{8,15},{9,8},{10,9... | collective-permute-start | bytes 786440 | tf_op jit(solution)/shard_map/ppermute | solution.py:19
  93.4 0.0 collective-permute-done.19.refs_11_
  93.4 0.7 collective-permute-start.20
  94.1 3.6 %collective-permute-done.14.refs_5_ = bf16[8,32,512]{2,1,0:T(8,128)(2,1)S(1)} collective-permute-done((bf16[8,32,512]{2,1,0:T(8,128)(2,1)S(1)}, bf16[8,32,512]{2,1,0:T(8,128)(2,1)S(1)}, u32[]{:S(2)}, u32[]{:S(2)}) %collective-permute-start.14) | collective-permute-done | bytes 262176 | tf_op jit(solution)/shard_map/ppermute | solution.py:19
  97.7 1.3 %collective-permute-start.15 = (bf16[8,32,512]{2,1,0:T(8,128)(2,1)S(1)}, bf16[8,32,512]{2,1,0:T(8,128)(2,1)S(1)}, u32[]{:S(2)}, u32[]{:S(2)}) collective-permute-start(bf16[8,32,512]{2,1,0:T(8,128)(2,1)S(1)} %collective-permute-done.14.refs_5_), channel_id=1, source_target_pairs={{0,7},{1,0},{2,1},{3,2},{4,3},{5,4},{6,5},{7,6},{8,15},{9,8},{10,9... | collective-permute-start | bytes 786440 | tf_op jit(solution)/shard_map/ppermute | solution.py:19
  99.1 0.0 collective-permute-done.11.refs_2_
  99.1 0.7 collective-permute-start.12
  99.8 1.8 %collective-permute-start.8 = (bf16[32,1024]{1,0:T(8,128)(2,1)S(1)}, bf16[32,1024]{1,0:T(8,128)(2,1)S(1)}, u32[]{:S(2)}, u32[]{:S(2)}) collective-permute-start(bf16[32,1024]{1,0:T(8,128)(2,1)S(1)} %get-tuple-element.7.m0), channel_id=1, source_target_pairs={{0,128},{128,0},{1,129},{129,1},{2,130},{130,2},{3,131},{131,3},{4... | collective-permute-start | bytes 196616 | tf_op jit(solution)/shard_map/ppermute | solution.py:19
  101.5 2.5 %collective-permute-done.8.m1 = bf16[32,1024]{1,0:T(8,128)(2,1)S(1)} collective-permute-done((bf16[32,1024]{1,0:T(8,128)(2,1)S(1)}, bf16[32,1024]{1,0:T(8,128)(2,1)S(1)}, u32[]{:S(2)}, u32[]{:S(2)}) %collective-permute-start.8) | collective-permute-done | bytes 65568 | tf_op jit(solution)/shard_map/ppermute | solution.py:19
  104.0 0.7 pad_maximum_fusion.4
  104.7 0.0 collective-permute-start.9
  104.7 0.0 collective-permute-done.23.refs_15_
  104.7 0.6 slice.27
  105.4 2.5 %collective-permute-start.25 = (bf16[4,32,512]{2,1,0:T(8,128)(2,1)}, bf16[4,32,512]{2,1,0:T(8,128)(2,1)}, u32[]{:S(2)}, u32[]{:S(2)}) collective-permute-start(bf16[4,32,512]{2,1,0:T(8,128)(2,1)} %slice.27), channel_id=1, source_target_pairs={{0,7},{1,0},{2,1},{3,2},{4,3},{5,4},{6,5},{7,6},{8,15},{9,8},{10,9... | collective-permute-start | bytes 393224 | tf_op jit(solution)/shard_map/ppermute | solution.py:19
  107.9 0.0 collective-permute-done.20.refs_12_
  107.9 0.7 slice.26
  108.6 0.7 slice.25
  109.2 3.2 %collective-permute-start.17 = (bf16[4,32,512]{2,1,0:T(8,128)(2,1)}, bf16[4,32,512]{2,1,0:T(8,128)(2,1)}, u32[]{:S(2)}, u32[]{:S(2)}) collective-permute-start(bf16[4,32,512]{2,1,0:T(8,128)(2,1)} %slice.25), channel_id=1, source_target_pairs={{0,7},{1,0},{2,1},{3,2},{4,3},{5,4},{6,5},{7,6},{8,15},{9,8},{10,9... | collective-permute-start | bytes 393224 | tf_op jit(solution)/shard_map/ppermute | solution.py:19
  112.5 0.7 slice.24
  113.1 0.1 stack.80.pos_ref
  113.2 0.0 collective-permute-done.9.m2
  113.2 2.5 %collective-permute-done.24.refs_16_ = bf16[4,32,512]{2,1,0:T(8,128)(2,1)} collective-permute-done((bf16[4,32,512]{2,1,0:T(8,128)(2,1)}, bf16[4,32,512]{2,1,0:T(8,128)(2,1)}, u32[]{:S(2)}, u32[]{:S(2)}) %collective-permute-start.24) | collective-permute-done | bytes 131104 | tf_op jit(solution)/shard_map/ppermute | solution.py:19
  115.7 4.0 %collective-permute-done.16.refs_7_ = bf16[4,32,512]{2,1,0:T(8,128)(2,1)} collective-permute-done((bf16[4,32,512]{2,1,0:T(8,128)(2,1)}, bf16[4,32,512]{2,1,0:T(8,128)(2,1)}, u32[]{:S(2)}, u32[]{:S(2)}) %collective-permute-start.16) | collective-permute-done | bytes 131104 | tf_op jit(solution)/shard_map/ppermute | solution.py:19
  119.7 0.9 copy-done.2
  120.7 0.9 copy-done.4
  121.6 4.1 %product.1 = f32[128,1,2048]{2,1,0:T(1,128)} custom-call(s32[5]{0:T(128)S(1)} %stack.80.pos_ref, bf16[32,1024]{1,0:T(8,128)(2,1)S(1)} %get-tuple-element.7.m0, bf16[32,1024]{1,0:T(8,128)(2,1)S(1)} %collective-permute-done.8.m1, bf16[2,32,1024]{2,1,0:T(8,128)(2,1)S(1)} %collective-permute-done.9.m2, bf16[8,32,512]{2,1,0:T(8,128)(2,1)S(1)} %solve_a.1.a_ref.refs_0_, ...), custom_call_target="tpu_custom_call" | custom-call | tf_op jit(solution)/shard_map/product/pallas_call | solution.py:214
  (26 shorter events, 0.2 us)
Async XLA Ops:
  0.0 0.7 copy-start
  19.3 24.7 %copy-start.5 = (f32[1,1,256,128]{3,2,1,0:T(8,128)S(1)}, f32[1,1,256,128]{3,2,1,0:T(8,128)}, u32[]{:S(2)}) copy-start(f32[1,1,256,128]{3,2,1,0:T(8,128)} %param.6) | copy-start | bytes 393220
  44.0 26.0 %collective-permute-start = (bf16[16,320,128]{2,1,0:T(8,128)(2,1)S(1)}, bf16[16,320,128]{2,1,0:T(8,128)(2,1)S(1)}, u32[]{:S(2)}, u32[]{:S(2)}) collective-permute-start(bf16[16,320,128]{2,1,0:T(8,128)(2,1)S(1)} %all_to_all.11.own), channel_id=1, source_target_pairs={{0,64},{64,0},{1,65},{65,1},{2,66},{66,2},{3,67},{67,3},{4,68},{68... | collective-permute-start | bytes 3932168 | tf_op jit(solution)/shard_map/ppermute | solution.py:19
  44.1 3.1 %collective-permute-start.1 = (f32[128,256]{1,0:T(8,128)S(1)}, f32[128,256]{1,0:T(8,128)S(1)}, u32[]{:S(2)}, u32[]{:S(2)}) collective-permute-start(f32[128,256]{1,0:T(8,128)S(1)} %bitcast.73), channel_id=1, source_target_pairs={{0,64},{64,0},{1,65},{65,1},{2,66},{66,2},{3,67},{67,3},{4,68},{68... | collective-permute-start | bytes 393224 | tf_op jit(solution)/shard_map/ppermute | solution.py:19
  47.3 5.9 %collective-permute-start.2 = (f32[2,32,256]{2,1,0:T(8,128)S(1)}, f32[2,32,256]{2,1,0:T(8,128)S(1)}, u32[]{:S(2)}, u32[]{:S(2)}) collective-permute-start(f32[2,32,256]{2,1,0:T(8,128)S(1)} %get-tuple-element.15), channel_id=1, source_target_pairs={{0,32},{32,0},{1,33},{33,1},{2,34},{34,2},{3,35},{35,3},{4,36},{36... | collective-permute-start | bytes 196616 | tf_op jit(solution)/shard_map/ppermute | solution.py:19
  49.5 4.9 %collective-permute-start.4 = (f32[2,32,256]{2,1,0:T(8,128)S(1)}, f32[2,32,256]{2,1,0:T(8,128)S(1)}, u32[]{:S(2)}, u32[]{:S(2)}) collective-permute-start(f32[2,32,256]{2,1,0:T(8,128)S(1)} %get-tuple-element.14), channel_id=1, source_target_pairs={{0,160},{32,128},{128,32},{160,0},{1,161},{33,129},{129,33},{161,1... | collective-permute-start | bytes 196616 | tf_op jit(solution)/shard_map/ppermute | solution.py:24
  50.6 4.3 %collective-permute-start.3 = (f32[2,32,256]{2,1,0:T(8,128)S(1)}, f32[2,32,256]{2,1,0:T(8,128)S(1)}, u32[]{:S(2)}, u32[]{:S(2)}) collective-permute-start(f32[2,32,256]{2,1,0:T(8,128)S(1)} %get-tuple-element.14), channel_id=1, source_target_pairs={{0,128},{128,0},{1,129},{129,1},{2,130},{130,2},{3,131},{131,3},{4... | collective-permute-start | bytes 196616 | tf_op jit(solution)/shard_map/ppermute | solution.py:19
  54.9 10.8 %collective-permute-start.6 = (f32[2,2,2,32,256]{4,3,1,2,0:T(8,128)S(1)}, f32[2,2,2,32,256]{4,3,1,2,0:T(8,128)S(1)}, u32[]{:S(2)}, u32[]{:S(2)}) collective-permute-start(f32[2,2,2,32,256]{4,3,1,2,0:T(8,128)S(1)} %get-tuple-element.10), channel_id=1, source_target_pairs={{0,16},{8,24},{16,0},{24,8},{1,17},{9,25},{17,1},{25,9},{2,18},{10... | collective-permute-start | bytes 786440 | tf_op jit(solution)/shard_map/ppermute | solution.py:19
  56.1 11.1 %collective-permute-start.5 = (f32[2,2,2,32,256]{4,3,1,2,0:T(8,128)S(1)}, f32[2,2,2,32,256]{4,3,1,2,0:T(8,128)S(1)}, u32[]{:S(2)}, u32[]{:S(2)}) collective-permute-start(f32[2,2,2,32,256]{4,3,1,2,0:T(8,128)S(1)} %get-tuple-element.10), channel_id=1, source_target_pairs={{0,24},{8,0},{16,8},{24,16},{1,25},{9,1},{17,9},{25,17},{2,26},{10... | collective-permute-start | bytes 786440 | tf_op jit(solution)/shard_map/ppermute | solution.py:19
  58.3 11.6 %collective-permute-start.7 = (f32[2,2,2,32,256]{4,3,1,2,0:T(8,128)S(1)}, f32[2,2,2,32,256]{4,3,1,2,0:T(8,128)S(1)}, u32[]{:S(2)}, u32[]{:S(2)}) collective-permute-start(f32[2,2,2,32,256]{4,3,1,2,0:T(8,128)S(1)} %get-tuple-element.10), channel_id=1, source_target_pairs={{0,8},{8,16},{16,24},{24,0},{1,9},{9,17},{17,25},{25,1},{2,10},{10... | collective-permute-start | bytes 786440 | tf_op jit(solution)/shard_map/ppermute | solution.py:19
  71.6 9.3 %collective-permute-start.21 = (bf16[8,32,512]{2,1,0:T(8,128)(2,1)S(1)}, bf16[8,32,512]{2,1,0:T(8,128)(2,1)S(1)}, u32[]{:S(2)}, u32[]{:S(2)}) collective-permute-start(bf16[8,32,512]{2,1,0:T(8,128)(2,1)S(1)} %get-tuple-element.8.refs_9_), channel_id=1, source_target_pairs={{0,7},{1,0},{2,1},{3,2},{4,3},{5,4},{6,5},{7,6},{8,15},{9,8},{10,9... | collective-permute-start | bytes 786440 | tf_op jit(solution)/shard_map/ppermute | solution.py:19
  71.8 10.4 %collective-permute-start.18 = (bf16[8,32,512]{2,1,0:T(8,128)(2,1)S(1)}, bf16[8,32,512]{2,1,0:T(8,128)(2,1)S(1)}, u32[]{:S(2)}, u32[]{:S(2)}) collective-permute-start(bf16[8,32,512]{2,1,0:T(8,128)(2,1)S(1)} %get-tuple-element.8.refs_9_), channel_id=1, source_target_pairs={{0,1},{1,2},{2,3},{3,4},{4,5},{5,6},{6,7},{7,0},{8,9},{9,10},{10,1... | collective-permute-start | bytes 786440 | tf_op jit(solution)/shard_map/ppermute | solution.py:19
  73.7 12.8 %collective-permute-start.13 = (bf16[8,32,512]{2,1,0:T(8,128)(2,1)S(1)}, bf16[8,32,512]{2,1,0:T(8,128)(2,1)S(1)}, u32[]{:S(2)}, u32[]{:S(2)}) collective-permute-start(bf16[8,32,512]{2,1,0:T(8,128)(2,1)S(1)} %solve_a.1.a_ref.refs_0_), channel_id=1, source_target_pairs={{0,7},{1,0},{2,1},{3,2},{4,3},{5,4},{6,5},{7,6},{8,15},{9,8},{10,9... | collective-permute-start | bytes 786440 | tf_op jit(solution)/shard_map/ppermute | solution.py:19
  75.1 12.8 %collective-permute-start.10 = (bf16[8,32,512]{2,1,0:T(8,128)(2,1)S(1)}, bf16[8,32,512]{2,1,0:T(8,128)(2,1)S(1)}, u32[]{:S(2)}, u32[]{:S(2)}) collective-permute-start(bf16[8,32,512]{2,1,0:T(8,128)(2,1)S(1)} %solve_a.1.a_ref.refs_0_), channel_id=1, source_target_pairs={{0,1},{1,2},{2,3},{3,4},{4,5},{5,6},{6,7},{7,0},{8,9},{9,10},{10,1... | collective-permute-start | bytes 786440 | tf_op jit(solution)/shard_map/ppermute | solution.py:19
  80.9 11.2 %collective-permute-start.22 = (bf16[8,32,512]{2,1,0:T(8,128)(2,1)S(1)}, bf16[8,32,512]{2,1,0:T(8,128)(2,1)S(1)}, u32[]{:S(2)}, u32[]{:S(2)}) collective-permute-start(bf16[8,32,512]{2,1,0:T(8,128)(2,1)S(1)} %collective-permute-done.21.refs_13_), channel_id=1, source_target_pairs={{0,7},{1,0},{2,1},{3,2},{4,3},{5,4},{6,5},{7,6},{8,15},{9,8},{10,9... | collective-permute-start | bytes 786440 | tf_op jit(solution)/shard_map/ppermute | solution.py:19
  82.2 11.2 %collective-permute-start.19 = (bf16[8,32,512]{2,1,0:T(8,128)(2,1)S(1)}, bf16[8,32,512]{2,1,0:T(8,128)(2,1)S(1)}, u32[]{:S(2)}, u32[]{:S(2)}) collective-permute-start(bf16[8,32,512]{2,1,0:T(8,128)(2,1)S(1)} %collective-permute-done.18.refs_10_), channel_id=1, source_target_pairs={{0,1},{1,2},{2,3},{3,4},{4,5},{5,6},{6,7},{7,0},{8,9},{9,10},{10,1... | collective-permute-start | bytes 786440 | tf_op jit(solution)/shard_map/ppermute | solution.py:19
  86.5 11.2 %collective-permute-start.14 = (bf16[8,32,512]{2,1,0:T(8,128)(2,1)S(1)}, bf16[8,32,512]{2,1,0:T(8,128)(2,1)S(1)}, u32[]{:S(2)}, u32[]{:S(2)}) collective-permute-start(bf16[8,32,512]{2,1,0:T(8,128)(2,1)S(1)} %collective-permute-done.13.refs_4_), channel_id=1, source_target_pairs={{0,7},{1,0},{2,1},{3,2},{4,3},{5,4},{6,5},{7,6},{8,15},{9,8},{10,9... | collective-permute-start | bytes 786440 | tf_op jit(solution)/shard_map/ppermute | solution.py:19
  87.8 11.2 %collective-permute-start.11 = (bf16[8,32,512]{2,1,0:T(8,128)(2,1)S(1)}, bf16[8,32,512]{2,1,0:T(8,128)(2,1)S(1)}, u32[]{:S(2)}, u32[]{:S(2)}) collective-permute-start(bf16[8,32,512]{2,1,0:T(8,128)(2,1)S(1)} %collective-permute-done.10.refs_1_), channel_id=1, source_target_pairs={{0,1},{1,2},{2,3},{3,4},{4,5},{5,6},{6,7},{7,0},{8,9},{9,10},{10,1... | collective-permute-start | bytes 786440 | tf_op jit(solution)/shard_map/ppermute | solution.py:19
  92.1 12.6 %collective-permute-start.23 = (bf16[8,32,512]{2,1,0:T(8,128)(2,1)S(1)}, bf16[8,32,512]{2,1,0:T(8,128)(2,1)S(1)}, u32[]{:S(2)}, u32[]{:S(2)}) collective-permute-start(bf16[8,32,512]{2,1,0:T(8,128)(2,1)S(1)} %collective-permute-done.22.refs_14_), channel_id=1, source_target_pairs={{0,7},{1,0},{2,1},{3,2},{4,3},{5,4},{6,5},{7,6},{8,15},{9,8},{10,9... | collective-permute-start | bytes 786440 | tf_op jit(solution)/shard_map/ppermute | solution.py:19
  93.4 14.4 %collective-permute-start.20 = (bf16[8,32,512]{2,1,0:T(8,128)(2,1)S(1)}, bf16[8,32,512]{2,1,0:T(8,128)(2,1)S(1)}, u32[]{:S(2)}, u32[]{:S(2)}) collective-permute-start(bf16[8,32,512]{2,1,0:T(8,128)(2,1)S(1)} %collective-permute-done.19.refs_11_), channel_id=1, source_target_pairs={{0,1},{1,2},{2,3},{3,4},{4,5},{5,6},{6,7},{7,0},{8,9},{9,10},{10,1... | collective-permute-start | bytes 786440 | tf_op jit(solution)/shard_map/ppermute | solution.py:19
  97.7 14.7 %copy-start.1 = (bf16[8,32,512]{2,1,0:T(8,128)(2,1)}, bf16[8,32,512]{2,1,0:T(8,128)(2,1)S(1)}, u32[]{:S(2)}) copy-start(bf16[8,32,512]{2,1,0:T(8,128)(2,1)S(1)} %collective-permute-done.14.refs_5_) | copy-start | bytes 786436
  97.7 10.8 %collective-permute-start.15 = (bf16[8,32,512]{2,1,0:T(8,128)(2,1)S(1)}, bf16[8,32,512]{2,1,0:T(8,128)(2,1)S(1)}, u32[]{:S(2)}, u32[]{:S(2)}) collective-permute-start(bf16[8,32,512]{2,1,0:T(8,128)(2,1)S(1)} %collective-permute-done.14.refs_5_), channel_id=1, source_target_pairs={{0,7},{1,0},{2,1},{3,2},{4,3},{5,4},{6,5},{7,6},{8,15},{9,8},{10,9... | collective-permute-start | bytes 786440 | tf_op jit(solution)/shard_map/ppermute | solution.py:19
  99.1 14.1 %copy-start.3 = (bf16[8,32,512]{2,1,0:T(8,128)(2,1)}, bf16[8,32,512]{2,1,0:T(8,128)(2,1)S(1)}, u32[]{:S(2)}) copy-start(bf16[8,32,512]{2,1,0:T(8,128)(2,1)S(1)} %collective-permute-done.11.refs_2_) | copy-start | bytes 786436
  99.1 13.4 %collective-permute-start.12 = (bf16[8,32,512]{2,1,0:T(8,128)(2,1)S(1)}, bf16[8,32,512]{2,1,0:T(8,128)(2,1)S(1)}, u32[]{:S(2)}, u32[]{:S(2)}) collective-permute-start(bf16[8,32,512]{2,1,0:T(8,128)(2,1)S(1)} %collective-permute-done.11.refs_2_), channel_id=1, source_target_pairs={{0,1},{1,2},{2,3},{3,4},{4,5},{5,6},{6,7},{7,0},{8,9},{9,10},{10,1... | collective-permute-start | bytes 786440 | tf_op jit(solution)/shard_map/ppermute | solution.py:19
  99.8 4.3 %collective-permute-start.8 = (bf16[32,1024]{1,0:T(8,128)(2,1)S(1)}, bf16[32,1024]{1,0:T(8,128)(2,1)S(1)}, u32[]{:S(2)}, u32[]{:S(2)}) collective-permute-start(bf16[32,1024]{1,0:T(8,128)(2,1)S(1)} %get-tuple-element.7.m0), channel_id=1, source_target_pairs={{0,128},{128,0},{1,129},{129,1},{2,130},{130,2},{3,131},{131,3},{4... | collective-permute-start | bytes 196616 | tf_op jit(solution)/shard_map/ppermute | solution.py:19
  104.7 8.5 %collective-permute-start.9 = (bf16[2,32,1024]{2,1,0:T(8,128)(2,1)}, bf16[2,32,1024]{2,1,0:T(8,128)(2,1)S(1)}, u32[]{:S(2)}, u32[]{:S(2)}) collective-permute-start(bf16[2,32,1024]{2,1,0:T(8,128)(2,1)} %pad_maximum_fusion.4), channel_id=1, source_target_pairs={{0,64},{64,0},{1,65},{65,1},{2,66},{66,2},{3,67},{67,3},{4,68},{68... | collective-permute-start | bytes 393224 | tf_op jit(solution)/shard_map/ppermute | solution.py:19
  105.4 7.9 %collective-permute-start.25 = (bf16[4,32,512]{2,1,0:T(8,128)(2,1)}, bf16[4,32,512]{2,1,0:T(8,128)(2,1)}, u32[]{:S(2)}, u32[]{:S(2)}) collective-permute-start(bf16[4,32,512]{2,1,0:T(8,128)(2,1)} %slice.27), channel_id=1, source_target_pairs={{0,7},{1,0},{2,1},{3,2},{4,3},{5,4},{6,5},{7,6},{8,15},{9,8},{10,9... | collective-permute-start | bytes 393224 | tf_op jit(solution)/shard_map/ppermute | solution.py:19
  108.6 7.2 %collective-permute-start.24 = (bf16[4,32,512]{2,1,0:T(8,128)(2,1)}, bf16[4,32,512]{2,1,0:T(8,128)(2,1)}, u32[]{:S(2)}, u32[]{:S(2)}) collective-permute-start(bf16[4,32,512]{2,1,0:T(8,128)(2,1)} %slice.26), channel_id=1, source_target_pairs={{0,1},{1,2},{2,3},{3,4},{4,5},{5,6},{6,7},{7,0},{8,9},{9,10},{10,1... | collective-permute-start | bytes 393224 | tf_op jit(solution)/shard_map/ppermute | solution.py:19
  109.2 6.5 %collective-permute-start.17 = (bf16[4,32,512]{2,1,0:T(8,128)(2,1)}, bf16[4,32,512]{2,1,0:T(8,128)(2,1)}, u32[]{:S(2)}, u32[]{:S(2)}) collective-permute-start(bf16[4,32,512]{2,1,0:T(8,128)(2,1)} %slice.25), channel_id=1, source_target_pairs={{0,7},{1,0},{2,1},{3,2},{4,3},{5,4},{6,5},{7,6},{8,15},{9,8},{10,9... | collective-permute-start | bytes 393224 | tf_op jit(solution)/shard_map/ppermute | solution.py:19
  113.1 6.6 %collective-permute-start.16 = (bf16[4,32,512]{2,1,0:T(8,128)(2,1)}, bf16[4,32,512]{2,1,0:T(8,128)(2,1)}, u32[]{:S(2)}, u32[]{:S(2)}) collective-permute-start(bf16[4,32,512]{2,1,0:T(8,128)(2,1)} %slice.24), channel_id=1, source_target_pairs={{0,1},{1,2},{2,3},{3,4},{4,5},{5,6},{6,7},{7,0},{8,9},{9,10},{10,1... | collective-permute-start | bytes 393224 | tf_op jit(solution)/shard_map/ppermute | solution.py:19
  119.7 1.0 copy-start.2
  120.7 0.9 copy-start.4

commit v4 on v3

v4 whole, which is shorter than its diff:
```python
import jax
import jax.numpy as jnp
from jax import lax
from jax.experimental import pallas as pl
from jax.experimental.pallas import tpu as pltpu
from jax.sharding import Mesh, PartitionSpec as P


FAC = ("yl", "core")
COL = ("yh", "x", "z")
NT = (((1,), (1,)), ((), ()))
BF = jnp.bfloat16
F32 = jnp.float32
LANES = 128
MIB = 1024 * 1024


def shift(a, axis, by=1):
    n = lax.axis_size(axis)
    return lax.ppermute(a, axis, [(i, (i + by) % n) for i in range(n)])


def opposite(a, axes):
    n = lax.axis_size(axes)
    return lax.ppermute(a, axes, [(i, n - 1 - i) for i in range(n)])


def by_index(mine, other, index):
    first = index == 0
    return jnp.stack([jnp.where(first, mine, other), jnp.where(first, other, mine)])


def split(a):
    hi = lax.reduce_precision(a, 8, 7)
    return hi.astype(BF), (a - hi).astype(BF)


def dot(a, b):
    return jnp.dot(a, b, preferred_element_type=F32)


def solve_kernel(pos_ref, own_ref, twin_ref, rights, a_ref, b_ref, mine_ref):
    w = rights.shape[3]
    groups, share = a_ref.shape[:2]
    cut = groups * share

    def run(pair):
        solved = []
        for p in range(4):
            yl, core = divmod(p, 2)
            ref, base = pair[core], 3 * yl
            r = rights[yl, core]
            for q in range(p):
                r = r - dot(solved[q], ref[base + 2 + q])
            rhi = r.astype(BF)
            rlo = (r - rhi.astype(F32)).astype(BF)
            dhi = ref[base]
            y = (dot(rlo, dhi) + dot(rhi, ref[base + 1])) + dot(rhi, dhi)
            y = y.astype(BF)
            solved.append(y)
            at = slice(p * w, (p + 1) * w)
            a_ref[:, :, at] = y[:cut].reshape(groups, share, w)
            b_ref[:, :, at] = y[cut:].reshape(groups, share, w)
            mine_ref[:, at] = y[:share]

    @pl.when(pos_ref[0] == 0)
    def _():
        run((own_ref, twin_ref))

    @pl.when(pos_ref[0] == 1)
    def _():
        run((twin_ref, own_ref))


def product(lhs, chunks, place):
    n = 0
    for blocks in chunks:
        for g in range(blocks[0].shape[0]):
            rhs = jnp.concatenate([b[g] for b in blocks], axis=0)
            place(n, lax.dot_general(lhs, rhs, NT, preferred_element_type=F32))
            n += 1


def near_kernel(pos_ref, m0, m1, m2, *refs):
    blocks, out_ref, own = refs[:-2], refs[-2], refs[-1]
    yl, core = pos_ref[1], pos_ref[2]
    own[2 * yl + core] = m0[...]
    own[2 * (1 - yl) + core] = m1[...]
    own[2 * yl + (1 - core)] = m2[0]
    own[2 * (1 - yl) + (1 - core)] = m2[1]
    lhs = own[...].reshape(-1, own.shape[2])

    def place(g, value):
        out_ref[g] = value

    product(lhs, (blocks[:4], blocks[4:]), place)


def far_kernel(pos_ref, near, own, *refs):
    blocks, out_ref = refs[:-1], refs[-1]
    z, yh, x = pos_ref[0], pos_ref[3], pos_ref[4]
    lhs = own[...].reshape(-1, own.shape[2])
    cols = 2 * near.shape[2]
    turn = lax.rem(z + 6, 8) * (cols // 8)

    def place(g, value):
        full = jnp.concatenate([near[g], value], axis=1)
        full = pltpu.roll(full, turn, 1)
        dyh, dx = divmod(g, 4)
        at = lax.rem(yh + dyh, 2) * 4 + lax.rem(x + dx, 4)
        out_ref[:, 0, pl.ds(pl.multiple_of(at * cols, cols), cols)] = full

    product(lhs, (blocks[:4], blocks[4:]), place)


def z_ring(chunks):
    ups = [[c] for c in chunks]
    downs = [[c] for c in chunks]
    for _ in range(1, 4):
        for u, d in zip(ups, downs):
            u.append(shift(u[-1], "z", 1))
            d.append(shift(d[-1], "z", -1))
    last = [shift(ups[0][-1], "z", 1)]
    last.append(shift(downs[1][-1], "z", -1))
    return [
        {0: u[0], -1: u[1], -2: u[2], -3: u[3], 1: d[1], 2: d[2], 3: d[3], 4: end}
        for u, d, end in zip(ups, downs, last)
    ]


def compute(lower_factor, panel_inverse, right_side, fill):
    w, kw = panel_inverse.shape[2:]
    fac = lax.axis_index(FAC)
    yl, core, yh, x, z = (lax.axis_index(a) for a in FAC + COL)
    nx = lax.axis_size("x")
    panels = fill.shape[0]
    halves = w // LANES

    hi, lo = split(panel_inverse[0, 0].T)
    keep = lax.dynamic_slice_in_dim(fill, fac, 1, 0)[0, : panels - 1] == 1
    low = lower_factor[0, 0, : panels - 1].transpose(0, 2, 1)
    low = jnp.where(keep[:, None, None], low, jnp.zeros_like(low))
    rows = jnp.concatenate([hi[None], lo[None], low], axis=0)
    nt = rows.shape[0]
    rows = rows.reshape(nt, kw, halves, LANES).transpose(0, 2, 1, 3)
    rows = rows.reshape(-1, LANES)
    wide = ("yl",) + COL
    peers = lax.axis_size(wide)
    rows = jnp.broadcast_to(rows[None], (peers,) + rows.shape)
    got = lax.all_to_all(rows, wide, 0, 0, tiled=True)
    got = got.reshape(2, peers // 2, nt, halves, kw, LANES)
    got = got.transpose(0, 2, 1, 4, 3, 5).reshape(2, nt, w, w)
    held = jnp.concatenate([got[0, :3], got[1]], axis=0)
    twin = shift(held, "core")

    share = right_side.shape[3] // panels
    bt = right_side[0, 0].T
    bo = shift(bt, "core")
    bt = by_index(bt, bo, core)
    bt = bt.reshape(2, 2, 2, share, w)
    bt = lax.dynamic_index_in_dim(bt, core, 2, keepdims=False)
    same = lax.dynamic_index_in_dim(bt, yl, 1, keepdims=False)
    cross = lax.dynamic_index_in_dim(bt, 1 - yl, 1, keepdims=False)
    near = jnp.stack([same, shift(same, "yh")])
    far = jnp.stack([shift(cross, "yl"), opposite(cross, ("yl", "yh"))])
    bt = by_index(near, far, yl)
    after = shift(bt, "x", -1)
    before = shift(bt, "x", 1)
    second = shift(after, "x", -1)
    rights = jnp.stack([bt, after, second, before], axis=2)
    rights = rights.transpose(0, 3, 1, 2, 4, 5)
    rights = rights.reshape(2, 2, 2 * nx * share, w)

    vm = pl.BlockSpec(memory_space=pltpu.VMEM)
    sm = pl.BlockSpec(memory_space=pltpu.SMEM)
    params = pltpu.CompilerParams(vmem_limit_bytes=16 * MIB)
    pos = jnp.stack([core]).astype(jnp.int32)
    half = jax.ShapeDtypeStruct((nx, share, panels * w), BF)
    one, two, mine = pl.pallas_call(
        solve_kernel,
        out_shape=(half, half, jax.ShapeDtypeStruct((share, panels * w), BF)),
        in_specs=[sm] + [vm] * 3,
        out_specs=(vm, vm, vm),
        compiler_params=params,
        name="solve",
    )(pos, held, twin, rights)

    m1 = shift(mine, "yl")
    m2 = shift(jnp.stack([mine, m1]), "core")
    ring = z_ring([one, two])

    pos = jnp.stack([z, yl, core, yh, x]).astype(jnp.int32)
    groups = 2 * nx
    cols = panels * share
    part, own = pl.pallas_call(
        near_kernel,
        out_shape=(
            jax.ShapeDtypeStruct((groups, cols, 4 * share), F32),
            jax.ShapeDtypeStruct((panels, share, panels * w), BF),
        ),
        in_specs=[sm] + [vm] * 11,
        out_specs=(vm, vm),
        compiler_params=params,
        name="near",
    )(pos, mine, m1, m2, *(c[k] for c in ring for k in (-2, -1, 0, 1)))
    return pl.pallas_call(
        far_kernel,
        out_shape=jax.ShapeDtypeStruct((cols, 1, groups * 8 * share), F32),
        in_specs=[sm] + [vm] * 10,
        out_specs=vm,
        compiler_params=params,
        name="far",
    )(pos, part, own, *(c[k] for c in ring for k in (2, 3, 4, -3)))


def solution(mesh):
    fine = Mesh(mesh.devices.reshape(2, 2, 2, 4, 8), FAC + COL)
    return jax.shard_map(
        compute,
        mesh=fine,
        in_specs=(
            P(None, FAC, None, None, COL),
            P(None, FAC, None, COL),
            P(None, FAC, None, COL),
            P(),
        ),
        out_specs=P(COL, FAC, None),
        check_vma=False,
    )
```

time: 127 us -> 130 us (1.024)
  blocking collectives: 41.5 us -> 0 us
  waiting for transfers between devices: 41.8 us -> 65.4 us
  starting transfers between devices: 28.5 us -> 48.5 us
    all_to_all x2 -> x0, blocking collectives: 41.5 us -> none  [exchange(): return lax.all_to_all(a, axes, 0, 0, tiled=True)]
    all_to_all x0 -> x1, waiting for transfers between devices: none -> 34.3 us  [compute(): got = lax.all_to_all(rows, wide, 0, 0, tiled=True)]
    all_to_all x0 -> x1, starting transfers between devices: none -> 15.8 us  [compute(): got = lax.all_to_all(rows, wide, 0, 0, tiled=True)]
    ppermute x25 -> x23, waiting for transfers between devices: 40.6 us -> 30.9 us  [shift(): return lax.ppermute(a, axis, [(i, (i + by) % n) for i in range(n)])]
    ppermute x25 -> x23, starting transfers between devices: 27.4 us -> 32.2 us  [shift(): return lax.ppermute(a, axis, [(i, (i + by) % n) for i in range(n)])]
    unnamed x13 -> x5, local copies, waits for them, and re-layouts: 2.69 us -> 0.78 us
    slice x4 -> x2, local copies, waits for them, and re-layouts: 2.62 us -> 0.73 us  [compute(): held = jnp.concatenate([got[0, :3], got[1]], axis=0)]
    transpose x1, local copies, waits for them, and re-layouts: 0.03 us -> 1.35 us  [compute(): got = got.transpose(0, 2, 1, 4, 3, 5).reshape(2, nt, w, w)]
  transfers between devices with their start and end apart: 26 -> 25, of which waited for: 14 -> 15; matrix products, arithmetic and copies ran while one was open for 3% -> 1% of each run, Pallas kernels for 0% -> 1%
where the time goes in v4:
time: 130 us; the launch traced here: 129 us
  waiting for transfers between devices  65.4 us (50%)
  starting transfers between devices  48.5 us (37%)
  Pallas kernels  6.41 us (5%)
  local copies, waits for them, and re-layouts  5.82 us (4%)
  other arithmetic  2.42 us (2%)
    all_to_all x1, waiting for transfers between devices, compute(): got = lax.all_to_all(rows, wide, 0, 0, tiled=True)  34.3 us
    ppermute x23, starting transfers between devices, shift(): return lax.ppermute(a, axis, [(i, (i + by) % n) for i in range(n)])  32.2 us
    ppermute x23, waiting for transfers between devices, shift(): return lax.ppermute(a, axis, [(i, (i + by) % n) for i in range(n)])  30.9 us
    all_to_all x1, starting transfers between devices, compute(): got = lax.all_to_all(rows, wide, 0, 0, tiled=True)  15.8 us
    pallas_call x1, Pallas kernels, compute(): pl.pallas_call(far_kernel, out_shape=jax.ShapeDtypeStruct((cols, 1, group...  3.12 us
  transfers between devices with their start and end apart: 25, of which 15 were waited for; matrix products, arithmetic and copies ran while one was open for 1% of the time, Pallas kernels for 1%

profile of v4, /device:TPU:8, one launch (start us, length us, event | category | flops | bytes accessed | tf_op | source)
XLA Modules:
  0.0 128.7 jit_solution(13558589653444148233)
XLA Ops:
  0.0 0.7 copy-done
  0.7 0.7 fusion.8
  1.4 0.8 fusion.5
  2.2 1.2 broadcast_in_dim.24
  3.4 15.8 %all-to-all-start = ((bf16[128,40,128]{2,1,0:T(8,128)(2,1)}), bf16[128,40,128]{2,1,0:T(8,128)(2,1)S(1)}, u32[]{:S(2)}, u32[]{:S(2)}) async-start(bf16[128,40,128]{2,1,0:T(8,128)(2,1)} %broadcast_in_dim.24), calls=%async_computation | async-start | bytes 2621440 | tf_op jit(solution)/shard_map/all_to_all | solution.py:150
  19.2 0.1 copy.28
  19.3 0.1 collective-permute-start.1
  19.5 1.3 %collective-permute-done.1 = f32[128,256]{1,0:T(8,128)S(1)} collective-permute-done((f32[128,256]{1,0:T(8,128)S(1)}, f32[128,256]{1,0:T(8,128)S(1)}, u32[]{:S(2)}, u32[]{:S(2)}) %collective-permute-start.1) | collective-permute-done | bytes 131104 | tf_op jit(solution)/shard_map/ppermute | solution.py:20
  20.8 34.3 %all-to-all-done = bf16[128,40,128]{2,1,0:T(8,128)(2,1)S(1)} async-done(((bf16[128,40,128]{2,1,0:T(8,128)(2,1)}), bf16[128,40,128]{2,1,0:T(8,128)(2,1)S(1)}, u32[]{:S(2)}, u32[]{:S(2)}) %all-to-all-start) | async-done | bytes 1310752 | tf_op jit(solution)/shard_map/all_to_all | solution.py:150
  55.1 0.3 copy.25
  55.4 0.1 slice.18
  55.5 1.4 %copy.26 = bf16[2,5,64,4,2,128]{5,4,3,2,1,0:T(2,128)(2,1)S(1)} copy(bf16[2,5,64,4,2,128]{5,2,0,3,4,1:T(8,128)(2,1)S(1)} %bitcast.74) | data formatting | bytes 2621440 | tf_op jit(solution)/shard_map/transpose | solution.py:152
  56.9 0.7 copy.27
  57.5 0.4 squeeze.28
  58.0 0.9 reshape.154
  58.9 0.1 pad_maximum_fusion.own_ref
  59.0 0.1 collective-permute-start
  59.1 0.4 collective-permute-start.4
  59.6 3.1 %collective-permute-start.3 = (f32[2,32,256]{2,1,0:T(8,128)S(1)}, f32[2,32,256]{2,1,0:T(8,128)S(1)}, u32[]{:S(2)}, u32[]{:S(2)}) collective-permute-start(f32[2,32,256]{2,1,0:T(8,128)S(1)} %get-tuple-element.20), channel_id=1, source_target_pairs={{0,128},{128,0},{1,129},{129,1},{2,130},{130,2},{3,131},{131,3},{4... | collective-permute-start | bytes 196616 | tf_op jit(solution)/shard_map/ppermute | solution.py:20
  62.7 0.8 collective-permute-start.2
  63.5 0.2 collective-permute-done.4
  63.7 1.4 %collective-permute-done.3 = f32[2,32,256]{2,1,0:T(8,128)S(1)} collective-permute-done((f32[2,32,256]{2,1,0:T(8,128)S(1)}, f32[2,32,256]{2,1,0:T(8,128)S(1)}, u32[]{:S(2)}, u32[]{:S(2)}) %collective-permute-start.3) | collective-permute-done | bytes 65568 | tf_op jit(solution)/shard_map/ppermute | solution.py:20
  65.1 3.3 %collective-permute-done.2 = f32[2,32,256]{2,1,0:T(8,128)S(1)} collective-permute-done((f32[2,32,256]{2,1,0:T(8,128)S(1)}, f32[2,32,256]{2,1,0:T(8,128)S(1)}, u32[]{:S(2)}, u32[]{:S(2)}) %collective-permute-start.2) | collective-permute-done | bytes 65568 | tf_op jit(solution)/shard_map/ppermute | solution.py:20
  68.5 0.2 collective-permute-start.5
  68.7 1.9 %collective-permute-start.7 = (f32[2,2,2,32,256]{4,3,1,2,0:T(8,128)S(1)}, f32[2,2,2,32,256]{4,3,1,2,0:T(8,128)S(1)}, u32[]{:S(2)}, u32[]{:S(2)}) collective-permute-start(f32[2,2,2,32,256]{4,3,1,2,0:T(8,128)S(1)} %get-tuple-element.16), channel_id=1, source_target_pairs={{0,8},{8,16},{16,24},{24,0},{1,9},{9,17},{17,25},{25,1},{2,10},{10... | collective-permute-start | bytes 786440 | tf_op jit(solution)/shard_map/ppermute | solution.py:20
  70.6 5.0 %collective-permute-done.5 = f32[2,2,2,32,256]{4,3,1,2,0:T(8,128)S(1)} collective-permute-done((f32[2,2,2,32,256]{4,3,1,2,0:T(8,128)S(1)}, f32[2,2,2,32,256]{4,3,1,2,0:T(8,128)S(1)}, u32[]{:S(2)}, u32[]{:S(2)}) %collective-permute-start.5) | collective-permute-done | bytes 262176 | tf_op jit(solution)/shard_map/ppermute | solution.py:20
  75.6 1.5 %collective-permute-start.6 = (f32[2,2,2,32,256]{4,3,1,2,0:T(8,128)S(1)}, f32[2,2,2,32,256]{4,3,1,2,0:T(8,128)S(1)}, u32[]{:S(2)}, u32[]{:S(2)}) collective-permute-start(f32[2,2,2,32,256]{4,3,1,2,0:T(8,128)S(1)} %collective-permute-done.5), channel_id=1, source_target_pairs={{0,24},{8,0},{16,8},{24,16},{1,25},{9,1},{17,9},{25,17},{2,26},{10... | collective-permute-start | bytes 786440 | tf_op jit(solution)/shard_map/ppermute | solution.py:20
  77.1 0.0 collective-permute-done.7
  77.1 4.9 %collective-permute-done.6 = f32[2,2,2,32,256]{4,3,1,2,0:T(8,128)S(1)} collective-permute-done((f32[2,2,2,32,256]{4,3,1,2,0:T(8,128)S(1)}, f32[2,2,2,32,256]{4,3,1,2,0:T(8,128)S(1)}, u32[]{:S(2)}, u32[]{:S(2)}) %collective-permute-start.6) | collective-permute-done | bytes 262176 | tf_op jit(solution)/shard_map/ppermute | solution.py:20
  81.9 0.1 pad_maximum_fusion.1
  82.0 0.0 collective-permute-done.twin_ref
  82.0 1.7 %solve.1 = (bf16[4,32,1024]{2,1,0:T(8,128)(2,1)S(1)}, bf16[4,32,1024]{2,1,0:T(8,128)(2,1)S(1)}, bf16[32,1024]{1,0:T(8,128)(2,1)S(1)}) custom-call(s32[1]{0:T(128)} %bitcast.2.pos_ref, bf16[8,256,256]{2,1,0:T(8,128)(2,1)S(1)} %pad_maximum_fusion.own_ref, bf16[8,256,256]{2,1,0:T(8,128)(2,1)S(1)} %collective-permute-done.twin_ref, f32[2,2,256,256]{3,2,1,0:T(8,128)S(1)} %bitcast.70), custom_call_target="tpu_custom_call" | custom-call | tf_op jit(solution)/shard_map/solve/pallas_call | solution.py:179
  83.7 0.6 collective-permute-start.10
  84.3 2.7 %collective-permute-start.15 = (bf16[4,32,1024]{2,1,0:T(8,128)(2,1)S(1)}, bf16[4,32,1024]{2,1,0:T(8,128)(2,1)S(1)}, u32[]{:S(2)}, u32[]{:S(2)}) collective-permute-start(bf16[4,32,1024]{2,1,0:T(8,128)(2,1)S(1)} %get-tuple-element.12.refs_6_), channel_id=1, source_target_pairs={{0,7},{1,0},{2,1},{3,2},{4,3},{5,4},{6,5},{7,6},{8,15},{9,8},{10,9... | collective-permute-start | bytes 786440 | tf_op jit(solution)/shard_map/ppermute | solution.py:20
  87.0 0.0 collective-permute-start.12
  87.0 2.0 %collective-permute-start.13 = (bf16[4,32,1024]{2,1,0:T(8,128)(2,1)S(1)}, bf16[4,32,1024]{2,1,0:T(8,128)(2,1)S(1)}, u32[]{:S(2)}, u32[]{:S(2)}) collective-permute-start(bf16[4,32,1024]{2,1,0:T(8,128)(2,1)S(1)} %get-tuple-element.12.refs_6_), channel_id=1, source_target_pairs={{0,1},{1,2},{2,3},{3,4},{4,5},{5,6},{6,7},{7,0},{8,9},{9,10},{10,1... | collective-permute-start | bytes 786440 | tf_op jit(solution)/shard_map/ppermute | solution.py:20
  89.0 5.1 %collective-permute-done.10.refs_1_ = bf16[4,32,1024]{2,1,0:T(8,128)(2,1)S(1)} collective-permute-done((bf16[4,32,1024]{2,1,0:T(8,128)(2,1)S(1)}, bf16[4,32,1024]{2,1,0:T(8,128)(2,1)S(1)}, u32[]{:S(2)}, u32[]{:S(2)}) %collective-permute-start.10) | collective-permute-done | bytes 262176 | tf_op jit(solution)/shard_map/ppermute | solution.py:20
  94.2 0.0 collective-permute-start.11
  94.2 0.0 collective-permute-done.15.refs_7_
  94.2 3.2 %collective-permute-start.20 = (bf16[4,32,1024]{2,1,0:T(8,128)(2,1)S(1)}, bf16[4,32,1024]{2,1,0:T(8,128)(2,1)S(1)}, u32[]{:S(2)}, u32[]{:S(2)}) collective-permute-start(bf16[4,32,1024]{2,1,0:T(8,128)(2,1)S(1)} %collective-permute-done.15.refs_7_), channel_id=1, source_target_pairs={{0,7},{1,0},{2,1},{3,2},{4,3},{5,4},{6,5},{7,6},{8,15},{9,8},{10,9... | collective-permute-start | bytes 786440 | tf_op jit(solution)/shard_map/ppermute | solution.py:20
  97.4 1.9 %collective-permute-done.12.refs_3_ = bf16[4,32,1024]{2,1,0:T(8,128)(2,1)S(1)} collective-permute-done((bf16[4,32,1024]{2,1,0:T(8,128)(2,1)S(1)}, bf16[4,32,1024]{2,1,0:T(8,128)(2,1)S(1)}, u32[]{:S(2)}, u32[]{:S(2)}) %collective-permute-start.12) | collective-permute-done | bytes 262176 | tf_op jit(solution)/shard_map/ppermute | solution.py:20
  99.3 3.7 %collective-permute-start.16 = (bf16[4,32,1024]{2,1,0:T(8,128)(2,1)S(1)}, bf16[4,32,1024]{2,1,0:T(8,128)(2,1)S(1)}, u32[]{:S(2)}, u32[]{:S(2)}) collective-permute-start(bf16[4,32,1024]{2,1,0:T(8,128)(2,1)S(1)} %collective-permute-done.12.refs_3_), channel_id=1, source_target_pairs={{0,7},{1,0},{2,1},{3,2},{4,3},{5,4},{6,5},{7,6},{8,15},{9,8},{10,9... | collective-permute-start | bytes 786440 | tf_op jit(solution)/shard_map/ppermute | solution.py:20
  103.0 0.0 collective-permute-done.13.refs_5_
  103.0 0.0 collective-permute-start.14
  103.0 1.7 %collective-permute-done.11.refs_0_ = bf16[4,32,1024]{2,1,0:T(8,128)(2,1)S(1)} collective-permute-done((bf16[4,32,1024]{2,1,0:T(8,128)(2,1)S(1)}, bf16[4,32,1024]{2,1,0:T(8,128)(2,1)S(1)}, u32[]{:S(2)}, u32[]{:S(2)}) %collective-permute-start.11) | collective-permute-done | bytes 262176 | tf_op jit(solution)/shard_map/ppermute | solution.py:20
  104.7 0.1 collective-permute-start.18
  104.8 0.2 collective-permute-done.20.refs_4_
  105.0 3.7 %collective-permute-start.21 = (bf16[4,32,1024]{2,1,0:T(8,128)(2,1)S(1)}, bf16[4,32,1024]{2,1,0:T(8,128)(2,1)S(1)}, u32[]{:S(2)}, u32[]{:S(2)}) collective-permute-start(bf16[4,32,1024]{2,1,0:T(8,128)(2,1)S(1)} %collective-permute-done.20.refs_4_), channel_id=1, source_target_pairs={{0,7},{1,0},{2,1},{3,2},{4,3},{5,4},{6,5},{7,6},{8,15},{9,8},{10,9... | collective-permute-start | bytes 786440 | tf_op jit(solution)/shard_map/ppermute | solution.py:20
  108.6 1.6 %collective-permute-start.8 = (bf16[32,1024]{1,0:T(8,128)(2,1)S(1)}, bf16[32,1024]{1,0:T(8,128)(2,1)S(1)}, u32[]{:S(2)}, u32[]{:S(2)}) collective-permute-start(bf16[32,1024]{1,0:T(8,128)(2,1)S(1)} %get-tuple-element.10.m0), channel_id=1, source_target_pairs={{0,128},{128,0},{1,129},{129,1},{2,130},{130,2},{3,131},{131,3},{4... | collective-permute-start | bytes 196616 | tf_op jit(solution)/shard_map/ppermute | solution.py:20
  110.2 0.4 collective-permute-done.16.refs_0_
  110.6 3.7 %collective-permute-start.17 = (bf16[4,32,1024]{2,1,0:T(8,128)(2,1)S(1)}, bf16[4,32,1024]{2,1,0:T(8,128)(2,1)S(1)}, u32[]{:S(2)}, u32[]{:S(2)}) collective-permute-start(bf16[4,32,1024]{2,1,0:T(8,128)(2,1)S(1)} %collective-permute-done.16.refs_0_), channel_id=1, source_target_pairs={{0,7},{1,0},{2,1},{3,2},{4,3},{5,4},{6,5},{7,6},{8,15},{9,8},{10,9... | collective-permute-start | bytes 786440 | tf_op jit(solution)/shard_map/ppermute | solution.py:20
  114.3 0.0 collective-permute-done.14.refs_4_
  114.3 3.6 %collective-permute-done.18.refs_3_ = bf16[4,32,1024]{2,1,0:T(8,128)(2,1)S(1)} collective-permute-done((bf16[4,32,1024]{2,1,0:T(8,128)(2,1)S(1)}, bf16[4,32,1024]{2,1,0:T(8,128)(2,1)S(1)}, u32[]{:S(2)}, u32[]{:S(2)}) %collective-permute-start.18) | collective-permute-done | bytes 262176 | tf_op jit(solution)/shard_map/ppermute | solution.py:20
  117.9 0.0 collective-permute-start.19
  117.9 0.0 collective-permute-done.21.refs_5_
  117.9 3.2 %collective-permute-start.22 = (bf16[4,32,1024]{2,1,0:T(8,128)(2,1)S(1)}, bf16[4,32,1024]{2,1,0:T(8,128)(2,1)}, u32[]{:S(2)}, u32[]{:S(2)}) collective-permute-start(bf16[4,32,1024]{2,1,0:T(8,128)(2,1)S(1)} %collective-permute-done.21.refs_5_), channel_id=1, source_target_pairs={{0,7},{1,0},{2,1},{3,2},{4,3},{5,4},{6,5},{7,6},{8,15},{9,8},{10,9... | collective-permute-start | bytes 786440 | tf_op jit(solution)/shard_map/ppermute | solution.py:20
  121.1 0.0 collective-permute-done.8.m1
  121.1 0.7 pad_maximum_fusion.5
  121.8 0.1 stack.80.pos_ref
  121.9 1.6 %collective-permute-done.9.m2 = bf16[2,32,1024]{2,1,0:T(8,128)(2,1)} collective-permute-done((bf16[2,32,1024]{2,1,0:T(8,128)(2,1)}, bf16[2,32,1024]{2,1,0:T(8,128)(2,1)}, u32[]{:S(2)}, u32[]{:S(2)}) %collective-permute-start.9) | collective-permute-done | bytes 131104 | tf_op jit(solution)/shard_map/ppermute | solution.py:20
  123.5 1.6 %near.1 = (f32[8,128,128]{2,1,0:T(8,128)S(1)}, bf16[4,32,1024]{2,1,0:T(8,128)(2,1)S(1)}) custom-call(s32[5]{0:T(128)S(1)} %stack.80.pos_ref, bf16[32,1024]{1,0:T(8,128)(2,1)S(1)} %get-tuple-element.10.m0, bf16[32,1024]{1,0:T(8,128)(2,1)S(1)} %collective-permute-done.8.m1, bf16[2,32,1024]{2,1,0:T(8,128)(2,1)} %collective-permute-done.9.m2, ...), custom_call_target="tpu_custom_call" | custom-call | tf_op jit(solution)/shard_map/near/pallas_call | solution.py:195
  125.1 0.0 collective-permute-done.17.refs_1_
  125.2 0.4 collective-permute-done.19.refs_2_
  125.6 3.1 %far.1 = f32[128,1,2048]{2,1,0:T(1,128)} custom-call(s32[5]{0:T(128)S(1)} %stack.80.pos_ref, f32[8,128,128]{2,1,0:T(8,128)S(1)} %get-tuple-element.13.near, bf16[4,32,1024]{2,1,0:T(8,128)(2,1)S(1)} %get-tuple-element.14.own, bf16[4,32,1024]{2,1,0:T(8,128)(2,1)S(1)} %collective-permute-done.16.refs_0_, ...), custom_call_target="tpu_custom_call" | custom-call | tf_op jit(solution)/shard_map/far/pallas_call | solution.py:206
  (15 shorter events, 0.2 us)
Async XLA Ops:
  0.0 0.7 copy-start
  3.4 15.8 %copy-start.1 = (f32[1,1,256,128]{3,2,1,0:T(8,128)S(1)}, f32[1,1,256,128]{3,2,1,0:T(8,128)}, u32[]{:S(2)}) copy-start(f32[1,1,256,128]{3,2,1,0:T(8,128)} %param.6) | copy-start | bytes 393220
  3.4 51.7 %all-to-all-start = ((bf16[128,40,128]{2,1,0:T(8,128)(2,1)}), bf16[128,40,128]{2,1,0:T(8,128)(2,1)S(1)}, u32[]{:S(2)}, u32[]{:S(2)}) async-start(bf16[128,40,128]{2,1,0:T(8,128)(2,1)} %broadcast_in_dim.24), calls=%async_computation | async-start | bytes 2621440 | tf_op jit(solution)/shard_map/all_to_all | solution.py:150
  19.3 1.4 %collective-permute-start.1 = (f32[128,256]{1,0:T(8,128)S(1)}, f32[128,256]{1,0:T(8,128)S(1)}, u32[]{:S(2)}, u32[]{:S(2)}) collective-permute-start(f32[128,256]{1,0:T(8,128)S(1)} %bitcast.75), channel_id=1, source_target_pairs={{0,64},{64,0},{1,65},{65,1},{2,66},{66,2},{3,67},{67,3},{4,68},{68... | collective-permute-start | bytes 393224 | tf_op jit(solution)/shard_map/ppermute | solution.py:20
  59.0 23.0 %collective-permute-start = (bf16[8,256,256]{2,1,0:T(8,128)(2,1)S(1)}, bf16[8,256,256]{2,1,0:T(8,128)(2,1)S(1)}, u32[]{:S(2)}, u32[]{:S(2)}) collective-permute-start(bf16[8,256,256]{2,1,0:T(8,128)(2,1)S(1)} %pad_maximum_fusion.own_ref), channel_id=1, source_target_pairs={{0,64},{64,0},{1,65},{65,1},{2,66},{66,2},{3,67},{67,3},{4,68},{68... | collective-permute-start | bytes 3145736 | tf_op jit(solution)/shard_map/ppermute | solution.py:20
  59.1 4.6 %collective-permute-start.4 = (f32[2,32,256]{2,1,0:T(8,128)S(1)}, f32[2,32,256]{2,1,0:T(8,128)S(1)}, u32[]{:S(2)}, u32[]{:S(2)}) collective-permute-start(f32[2,32,256]{2,1,0:T(8,128)S(1)} %get-tuple-element.20), channel_id=1, source_target_pairs={{0,160},{32,128},{128,32},{160,0},{1,161},{33,129},{129,33},{161,1... | collective-permute-start | bytes 196616 | tf_op jit(solution)/shard_map/ppermute | solution.py:25
  59.6 5.6 %collective-permute-start.3 = (f32[2,32,256]{2,1,0:T(8,128)S(1)}, f32[2,32,256]{2,1,0:T(8,128)S(1)}, u32[]{:S(2)}, u32[]{:S(2)}) collective-permute-start(f32[2,32,256]{2,1,0:T(8,128)S(1)} %get-tuple-element.20), channel_id=1, source_target_pairs={{0,128},{128,0},{1,129},{129,1},{2,130},{130,2},{3,131},{131,3},{4... | collective-permute-start | bytes 196616 | tf_op jit(solution)/shard_map/ppermute | solution.py:20
  62.7 5.8 %collective-permute-start.2 = (f32[2,32,256]{2,1,0:T(8,128)S(1)}, f32[2,32,256]{2,1,0:T(8,128)S(1)}, u32[]{:S(2)}, u32[]{:S(2)}) collective-permute-start(f32[2,32,256]{2,1,0:T(8,128)S(1)} %get-tuple-element.21), channel_id=1, source_target_pairs={{0,32},{32,0},{1,33},{33,1},{2,34},{34,2},{3,35},{35,3},{4,36},{36... | collective-permute-start | bytes 196616 | tf_op jit(solution)/shard_map/ppermute | solution.py:20
  68.5 7.1 %collective-permute-start.5 = (f32[2,2,2,32,256]{4,3,1,2,0:T(8,128)S(1)}, f32[2,2,2,32,256]{4,3,1,2,0:T(8,128)S(1)}, u32[]{:S(2)}, u32[]{:S(2)}) collective-permute-start(f32[2,2,2,32,256]{4,3,1,2,0:T(8,128)S(1)} %get-tuple-element.16), channel_id=1, source_target_pairs={{0,24},{8,0},{16,8},{24,16},{1,25},{9,1},{17,9},{25,17},{2,26},{10... | collective-permute-start | bytes 786440 | tf_op jit(solution)/shard_map/ppermute | solution.py:20
  68.7 8.4 %collective-permute-start.7 = (f32[2,2,2,32,256]{4,3,1,2,0:T(8,128)S(1)}, f32[2,2,2,32,256]{4,3,1,2,0:T(8,128)S(1)}, u32[]{:S(2)}, u32[]{:S(2)}) collective-permute-start(f32[2,2,2,32,256]{4,3,1,2,0:T(8,128)S(1)} %get-tuple-element.16), channel_id=1, source_target_pairs={{0,8},{8,16},{16,24},{24,0},{1,9},{9,17},{17,25},{25,1},{2,10},{10... | collective-permute-start | bytes 786440 | tf_op jit(solution)/shard_map/ppermute | solution.py:20
  75.6 6.4 %collective-permute-start.6 = (f32[2,2,2,32,256]{4,3,1,2,0:T(8,128)S(1)}, f32[2,2,2,32,256]{4,3,1,2,0:T(8,128)S(1)}, u32[]{:S(2)}, u32[]{:S(2)}) collective-permute-start(f32[2,2,2,32,256]{4,3,1,2,0:T(8,128)S(1)} %collective-permute-done.5), channel_id=1, source_target_pairs={{0,24},{8,0},{16,8},{24,16},{1,25},{9,1},{17,9},{25,17},{2,26},{10... | collective-permute-start | bytes 786440 | tf_op jit(solution)/shard_map/ppermute | solution.py:20
  83.7 10.5 %collective-permute-start.10 = (bf16[4,32,1024]{2,1,0:T(8,128)(2,1)S(1)}, bf16[4,32,1024]{2,1,0:T(8,128)(2,1)S(1)}, u32[]{:S(2)}, u32[]{:S(2)}) collective-permute-start(bf16[4,32,1024]{2,1,0:T(8,128)(2,1)S(1)} %get-tuple-element.11.refs_2_), channel_id=1, source_target_pairs={{0,1},{1,2},{2,3},{3,4},{4,5},{5,6},{6,7},{7,0},{8,9},{9,10},{10,1... | collective-permute-start | bytes 786440 | tf_op jit(solution)/shard_map/ppermute | solution.py:20
  84.3 9.8 %collective-permute-start.15 = (bf16[4,32,1024]{2,1,0:T(8,128)(2,1)S(1)}, bf16[4,32,1024]{2,1,0:T(8,128)(2,1)S(1)}, u32[]{:S(2)}, u32[]{:S(2)}) collective-permute-start(bf16[4,32,1024]{2,1,0:T(8,128)(2,1)S(1)} %get-tuple-element.12.refs_6_), channel_id=1, source_target_pairs={{0,7},{1,0},{2,1},{3,2},{4,3},{5,4},{6,5},{7,6},{8,15},{9,8},{10,9... | collective-permute-start | bytes 786440 | tf_op jit(solution)/shard_map/ppermute | solution.py:20
  87.0 12.3 %collective-permute-start.12 = (bf16[4,32,1024]{2,1,0:T(8,128)(2,1)S(1)}, bf16[4,32,1024]{2,1,0:T(8,128)(2,1)S(1)}, u32[]{:S(2)}, u32[]{:S(2)}) collective-permute-start(bf16[4,32,1024]{2,1,0:T(8,128)(2,1)S(1)} %get-tuple-element.11.refs_2_), channel_id=1, source_target_pairs={{0,7},{1,0},{2,1},{3,2},{4,3},{5,4},{6,5},{7,6},{8,15},{9,8},{10,9... | collective-permute-start | bytes 786440 | tf_op jit(solution)/shard_map/ppermute | solution.py:20
  87.0 16.0 %collective-permute-start.13 = (bf16[4,32,1024]{2,1,0:T(8,128)(2,1)S(1)}, bf16[4,32,1024]{2,1,0:T(8,128)(2,1)S(1)}, u32[]{:S(2)}, u32[]{:S(2)}) collective-permute-start(bf16[4,32,1024]{2,1,0:T(8,128)(2,1)S(1)} %get-tuple-element.12.refs_6_), channel_id=1, source_target_pairs={{0,1},{1,2},{2,3},{3,4},{4,5},{5,6},{6,7},{7,0},{8,9},{9,10},{10,1... | collective-permute-start | bytes 786440 | tf_op jit(solution)/shard_map/ppermute | solution.py:20
  94.2 10.5 %collective-permute-start.11 = (bf16[4,32,1024]{2,1,0:T(8,128)(2,1)S(1)}, bf16[4,32,1024]{2,1,0:T(8,128)(2,1)S(1)}, u32[]{:S(2)}, u32[]{:S(2)}) collective-permute-start(bf16[4,32,1024]{2,1,0:T(8,128)(2,1)S(1)} %collective-permute-done.10.refs_1_), channel_id=1, source_target_pairs={{0,1},{1,2},{2,3},{3,4},{4,5},{5,6},{6,7},{7,0},{8,9},{9,10},{10,1... | collective-permute-start | bytes 786440 | tf_op jit(solution)/shard_map/ppermute | solution.py:20
  94.2 10.8 %collective-permute-start.20 = (bf16[4,32,1024]{2,1,0:T(8,128)(2,1)S(1)}, bf16[4,32,1024]{2,1,0:T(8,128)(2,1)S(1)}, u32[]{:S(2)}, u32[]{:S(2)}) collective-permute-start(bf16[4,32,1024]{2,1,0:T(8,128)(2,1)S(1)} %collective-permute-done.15.refs_7_), channel_id=1, source_target_pairs={{0,7},{1,0},{2,1},{3,2},{4,3},{5,4},{6,5},{7,6},{8,15},{9,8},{10,9... | collective-permute-start | bytes 786440 | tf_op jit(solution)/shard_map/ppermute | solution.py:20
  99.3 11.2 %collective-permute-start.16 = (bf16[4,32,1024]{2,1,0:T(8,128)(2,1)S(1)}, bf16[4,32,1024]{2,1,0:T(8,128)(2,1)S(1)}, u32[]{:S(2)}, u32[]{:S(2)}) collective-permute-start(bf16[4,32,1024]{2,1,0:T(8,128)(2,1)S(1)} %collective-permute-done.12.refs_3_), channel_id=1, source_target_pairs={{0,7},{1,0},{2,1},{3,2},{4,3},{5,4},{6,5},{7,6},{8,15},{9,8},{10,9... | collective-permute-start | bytes 786440 | tf_op jit(solution)/shard_map/ppermute | solution.py:20
  103.0 11.2 %collective-permute-start.14 = (bf16[4,32,1024]{2,1,0:T(8,128)(2,1)S(1)}, bf16[4,32,1024]{2,1,0:T(8,128)(2,1)S(1)}, u32[]{:S(2)}, u32[]{:S(2)}) collective-permute-start(bf16[4,32,1024]{2,1,0:T(8,128)(2,1)S(1)} %collective-permute-done.13.refs_5_), channel_id=1, source_target_pairs={{0,1},{1,2},{2,3},{3,4},{4,5},{5,6},{6,7},{7,0},{8,9},{9,10},{10,1... | collective-permute-start | bytes 786440 | tf_op jit(solution)/shard_map/ppermute | solution.py:20
  104.7 13.2 %collective-permute-start.18 = (bf16[4,32,1024]{2,1,0:T(8,128)(2,1)S(1)}, bf16[4,32,1024]{2,1,0:T(8,128)(2,1)S(1)}, u32[]{:S(2)}, u32[]{:S(2)}) collective-permute-start(bf16[4,32,1024]{2,1,0:T(8,128)(2,1)S(1)} %collective-permute-done.11.refs_0_), channel_id=1, source_target_pairs={{0,1},{1,2},{2,3},{3,4},{4,5},{5,6},{6,7},{7,0},{8,9},{9,10},{10,1... | collective-permute-start | bytes 786440 | tf_op jit(solution)/shard_map/ppermute | solution.py:20
  105.0 13.0 %collective-permute-start.21 = (bf16[4,32,1024]{2,1,0:T(8,128)(2,1)S(1)}, bf16[4,32,1024]{2,1,0:T(8,128)(2,1)S(1)}, u32[]{:S(2)}, u32[]{:S(2)}) collective-permute-start(bf16[4,32,1024]{2,1,0:T(8,128)(2,1)S(1)} %collective-permute-done.20.refs_4_), channel_id=1, source_target_pairs={{0,7},{1,0},{2,1},{3,2},{4,3},{5,4},{6,5},{7,6},{8,15},{9,8},{10,9... | collective-permute-start | bytes 786440 | tf_op jit(solution)/shard_map/ppermute | solution.py:20
  108.6 12.5 %collective-permute-start.8 = (bf16[32,1024]{1,0:T(8,128)(2,1)S(1)}, bf16[32,1024]{1,0:T(8,128)(2,1)S(1)}, u32[]{:S(2)}, u32[]{:S(2)}) collective-permute-start(bf16[32,1024]{1,0:T(8,128)(2,1)S(1)} %get-tuple-element.10.m0), channel_id=1, source_target_pairs={{0,128},{128,0},{1,129},{129,1},{2,130},{130,2},{3,131},{131,3},{4... | collective-permute-start | bytes 196616 | tf_op jit(solution)/shard_map/ppermute | solution.py:20
  110.6 14.6 %collective-permute-start.17 = (bf16[4,32,1024]{2,1,0:T(8,128)(2,1)S(1)}, bf16[4,32,1024]{2,1,0:T(8,128)(2,1)S(1)}, u32[]{:S(2)}, u32[]{:S(2)}) collective-permute-start(bf16[4,32,1024]{2,1,0:T(8,128)(2,1)S(1)} %collective-permute-done.16.refs_0_), channel_id=1, source_target_pairs={{0,7},{1,0},{2,1},{3,2},{4,3},{5,4},{6,5},{7,6},{8,15},{9,8},{10,9... | collective-permute-start | bytes 786440 | tf_op jit(solution)/shard_map/ppermute | solution.py:20
  114.3 10.9 %collective-permute-start.23 = (bf16[4,32,1024]{2,1,0:T(8,128)(2,1)S(1)}, bf16[4,32,1024]{2,1,0:T(8,128)(2,1)}, u32[]{:S(2)}, u32[]{:S(2)}) collective-permute-start(bf16[4,32,1024]{2,1,0:T(8,128)(2,1)S(1)} %collective-permute-done.14.refs_4_), channel_id=1, source_target_pairs={{0,1},{1,2},{2,3},{3,4},{4,5},{5,6},{6,7},{7,0},{8,9},{9,10},{10,1... | collective-permute-start | bytes 786440 | tf_op jit(solution)/shard_map/ppermute | solution.py:20
  117.9 7.7 %collective-permute-start.19 = (bf16[4,32,1024]{2,1,0:T(8,128)(2,1)S(1)}, bf16[4,32,1024]{2,1,0:T(8,128)(2,1)}, u32[]{:S(2)}, u32[]{:S(2)}) collective-permute-start(bf16[4,32,1024]{2,1,0:T(8,128)(2,1)S(1)} %collective-permute-done.18.refs_3_), channel_id=1, source_target_pairs={{0,1},{1,2},{2,3},{3,4},{4,5},{5,6},{6,7},{7,0},{8,9},{9,10},{10,1... | collective-permute-start | bytes 786440 | tf_op jit(solution)/shard_map/ppermute | solution.py:20
  117.9 7.7 %collective-permute-start.22 = (bf16[4,32,1024]{2,1,0:T(8,128)(2,1)S(1)}, bf16[4,32,1024]{2,1,0:T(8,128)(2,1)}, u32[]{:S(2)}, u32[]{:S(2)}) collective-permute-start(bf16[4,32,1024]{2,1,0:T(8,128)(2,1)S(1)} %collective-permute-done.21.refs_5_), channel_id=1, source_target_pairs={{0,7},{1,0},{2,1},{3,2},{4,3},{5,4},{6,5},{7,6},{8,15},{9,8},{10,9... | collective-permute-start | bytes 786440 | tf_op jit(solution)/shard_map/ppermute | solution.py:20
  121.8 1.7 %collective-permute-start.9 = (bf16[2,32,1024]{2,1,0:T(8,128)(2,1)}, bf16[2,32,1024]{2,1,0:T(8,128)(2,1)}, u32[]{:S(2)}, u32[]{:S(2)}) collective-permute-start(bf16[2,32,1024]{2,1,0:T(8,128)(2,1)} %pad_maximum_fusion.5), channel_id=1, source_target_pairs={{0,64},{64,0},{1,65},{65,1},{2,66},{66,2},{3,67},{67,3},{4,68},{68... | collective-permute-start | bytes 393224 | tf_op jit(solution)/shard_map/ppermute | solution.py:20

commit v5 on v4

v5 whole, which is shorter than its diff:
```python
import jax
import jax.numpy as jnp
from jax import lax
from jax.experimental import pallas as pl
from jax.experimental.pallas import tpu as pltpu
from jax.sharding import Mesh, PartitionSpec as P


FAC = ("yl", "core")
COL = ("yh", "x", "z")
NT = (((1,), (1,)), ((), ()))
BF = jnp.bfloat16
F32 = jnp.float32
LANES = 128
MIB = 1024 * 1024


def shift(a, axis, by=1):
    n = lax.axis_size(axis)
    return lax.ppermute(a, axis, [(i, (i + by) % n) for i in range(n)])


def opposite(a, axes):
    n = lax.axis_size(axes)
    return lax.ppermute(a, axes, [(i, n - 1 - i) for i in range(n)])


def by_index(mine, other, index):
    first = index == 0
    return jnp.stack([jnp.where(first, mine, other), jnp.where(first, other, mine)])


def split(a):
    hi = lax.reduce_precision(a, 8, 7)
    return hi.astype(BF), (a - hi).astype(BF)


def dot(a, b):
    return jnp.dot(a, b, preferred_element_type=F32)


def solve_kernel(pos_ref, own_ref, twin_ref, pack, late, a_ref, b_ref, mine_ref):
    peers, _, lanes = own_ref.shape
    half = peers // 2
    share, w = pack.shape[4:]
    groups = a_ref.shape[0]
    cut = groups * share

    def square(ref, yl, block):
        parts = [
            ref[yl * half : (yl + 1) * half, r : r + 32, :].reshape(half * 32, lanes)
            for r in (64 * block, 64 * block + 32)
        ]
        return jnp.concatenate(parts, axis=1)

    def right(yl, core):
        rows = []
        for yh in range(2):
            rows += [pack[i, yl, yh, core] for i in range(4)]
            rows.append(late[yl, yh, core])
            rows += [pack[i, yl, yh, core] for i in range(4, 7)]
        return jnp.concatenate(rows, axis=0)

    def run(pair):
        solved = []
        for p in range(4):
            yl, core = divmod(p, 2)
            ref = pair[core]
            r = right(yl, core)
            for q in range(p):
                r = r - dot(solved[q], square(ref, yl, 2 + q))
            rhi = r.astype(BF)
            rlo = (r - rhi.astype(F32)).astype(BF)
            dhi = square(ref, yl, 0)
            y = (dot(rlo, dhi) + dot(rhi, square(ref, yl, 1))) + dot(rhi, dhi)
            y = y.astype(BF)
            solved.append(y)
            at = slice(p * w, (p + 1) * w)
            a_ref[:, :, at] = y[:cut].reshape(groups, share, w)
            b_ref[:, :, at] = y[cut:].reshape(groups, share, w)
            mine_ref[:, at] = y[:share]

    @pl.when(pos_ref[0] == 0)
    def _():
        run((own_ref, twin_ref))

    @pl.when(pos_ref[0] == 1)
    def _():
        run((twin_ref, own_ref))


def columns(lhs, block, z):
    nz, share, k = block.shape
    out = lax.dot_general(
        lhs, block[...].reshape(nz * share, k), NT, preferred_element_type=F32
    )
    return pltpu.roll(out, z * share, 1)


def near_kernel(pos_ref, m0, m1, m2, *refs):
    blocks, out_ref, own = refs[:-2], refs[-2], refs[-1]
    yl, core = pos_ref[1], pos_ref[2]
    own[2 * yl + core] = m0[...]
    own[2 * (1 - yl) + core] = m1[...]
    own[2 * yl + (1 - core)] = m2[0]
    own[2 * (1 - yl) + (1 - core)] = m2[1]
    lhs = own[...].reshape(-1, own.shape[2])
    for g, block in enumerate(blocks):
        out_ref[g] = columns(lhs, block, pos_ref[0])


def far_kernel(pos_ref, near, own, last0, last1, out_ref):
    z, yh, x = pos_ref[0], pos_ref[3], pos_ref[4]
    cols = near.shape[2]

    def place(dyh, dx, value):
        at = lax.rem(yh + dyh, 2) * 4 + lax.rem(x + dx, 4)
        out_ref[:, 0, pl.ds(pl.multiple_of(at * cols, cols), cols)] = value

    for dyh in range(2):
        for i, dx in enumerate((0, 1, 3)):
            place(dyh, dx, near[3 * dyh + i])
    lhs = own[...].reshape(-1, own.shape[2])
    for dyh, block in enumerate((last0, last1)):
        place(dyh, 2, columns(lhs, block, z))


def compute(lower_factor, panel_inverse, right_side, fill):
    w, kw = panel_inverse.shape[2:]
    fac = lax.axis_index(FAC)
    yl, core, yh, x, z = (lax.axis_index(a) for a in FAC + COL)
    nx = lax.axis_size("x")
    panels = fill.shape[0]
    halves = w // LANES

    hi, lo = split(panel_inverse[0, 0].T)
    keep = lax.dynamic_slice_in_dim(fill, fac, 1, 0)[0, : panels - 1] == 1
    low = lower_factor[0, 0, : panels - 1].transpose(0, 2, 1)
    low = jnp.where(keep[:, None, None], low, jnp.zeros_like(low))
    rows = jnp.concatenate([hi[None], lo[None], low], axis=0)
    nt = rows.shape[0]
    rows = rows.reshape(nt, kw, halves, LANES).transpose(0, 2, 1, 3)
    rows = rows.reshape(-1, LANES)
    nz = lax.axis_size("z")
    npeer = 2 * 2 * nx
    rows = jnp.broadcast_to(rows[None], (nz,) + rows.shape)
    got = lax.all_to_all(rows, "z", 0, 0, tiled=True)
    got = got.reshape(nz, nt * halves, kw, LANES).transpose(1, 0, 2, 3)
    got = got.reshape(-1, LANES)
    got = jnp.broadcast_to(got[None], (npeer,) + got.shape)
    held = lax.all_to_all(got, ("yl", "yh", "x"), 0, 0, tiled=True)
    twin = shift(held, "core")

    share = right_side.shape[3] // panels
    bt = right_side[0, 0].T
    bo = shift(bt, "core")
    bt = by_index(bt, bo, core)
    bt = bt.reshape(2, 2, 2, share, w)
    bt = lax.dynamic_index_in_dim(bt, core, 2, keepdims=False)
    same = lax.dynamic_index_in_dim(bt, yl, 1, keepdims=False)
    cross = lax.dynamic_index_in_dim(bt, 1 - yl, 1, keepdims=False)
    near = jnp.stack([same, shift(same, "yh")])
    far = jnp.stack([shift(cross, "yl"), opposite(cross, ("yl", "yh"))])
    bt = by_index(near, far, yl)
    ups, downs = [bt], [bt]
    for _ in range(1, 4):
        ups.append(shift(ups[-1], "z", 1))
        downs.append(shift(downs[-1], "z", -1))
    late = shift(ups[-1], "z", 1)
    pack = jnp.stack(downs + ups[:0:-1])

    vm = pl.BlockSpec(memory_space=pltpu.VMEM)
    sm = pl.BlockSpec(memory_space=pltpu.SMEM)
    params = pltpu.CompilerParams(vmem_limit_bytes=16 * MIB)
    pos = jnp.stack([core]).astype(jnp.int32)
    block = jax.ShapeDtypeStruct((nz, share, panels * w), BF)
    one, two, mine = pl.pallas_call(
        solve_kernel,
        out_shape=(block, block, jax.ShapeDtypeStruct((share, panels * w), BF)),
        in_specs=[sm] + [vm] * 4,
        out_specs=(vm, vm, vm),
        compiler_params=params,
        name="solve",
    )(pos, held, twin, pack, late)

    one_before, one_after = shift(one, "x", 1), shift(one, "x", -1)
    two_after, two_before = shift(two, "x", -1), shift(two, "x", 1)
    m1 = shift(mine, "yl")
    m2 = shift(jnp.stack([mine, m1]), "core")
    one_far = shift(one_before, "x", 1)
    two_far = shift(two_after, "x", -1)

    pos = jnp.stack([z, yl, core, yh, x]).astype(jnp.int32)
    cols = panels * share
    part, own = pl.pallas_call(
        near_kernel,
        out_shape=(
            jax.ShapeDtypeStruct((6, cols, nz * share), F32),
            jax.ShapeDtypeStruct((panels, share, panels * w), BF),
        ),
        in_specs=[sm] + [vm] * 9,
        out_specs=(vm, vm),
        compiler_params=params,
        name="near",
    )(pos, mine, m1, m2, one, one_after, one_before, two, two_after, two_before)
    return pl.pallas_call(
        far_kernel,
        out_shape=jax.ShapeDtypeStruct((cols, 1, 2 * nx * nz * share), F32),
        in_specs=[sm] + [vm] * 4,
        out_specs=vm,
        compiler_params=params,
        name="far",
    )(pos, part, own, one_far, two_far)


def solution(mesh):
    fine = Mesh(mesh.devices.reshape(2, 2, 2, 4, 8), FAC + COL)
    return jax.shard_map(
        compute,
        mesh=fine,
        in_specs=(
            P(None, FAC, None, None, COL),
            P(None, FAC, None, COL),
            P(None, FAC, None, COL),
            P(),
        ),
        out_specs=P(COL, FAC, None),
        check_vma=False,
    )
```

time: 130 us -> 120 us (0.923)
  the two profiles are of different devices: /device:TPU:8 before, /device:TPU:6 now
where the time goes in v5:
time: 120 us
  waiting for transfers between devices  64.9 us (54%)
  starting transfers between devices  35.4 us (30%)
  local copies, waits for them, and re-layouts  8.67 us (7%)
  Pallas kernels  8.15 us (7%)
  other arithmetic  2.24 us (2%)
    ppermute x19, waiting for transfers between devices, shift(): return lax.ppermute(a, axis, [(i, (i + by) % n) for i in range(n)])  56.2 us
    ppermute x19, starting transfers between devices, shift(): return lax.ppermute(a, axis, [(i, (i + by) % n) for i in range(n)])  17.5 us
    all_to_all x1, starting transfers between devices, compute(): got = lax.all_to_all(rows, 'z', 0, 0, tiled=True)  8.47 us
    all_to_all x1, waiting for transfers between devices, compute(): got = lax.all_to_all(rows, 'z', 0, 0, tiled=True)  7.45 us
    all_to_all x1, starting transfers between devices, compute(): held = lax.all_to_all(got, ('yl', 'yh', 'x'), 0, 0, tiled=True)  7.42 us
    unnamed x10, local copies, waits for them, and re-layouts  6.53 us
    pallas_call x1, Pallas kernels, compute(): pl.pallas_call(solve_kernel, out_shape=(block, block, jax.ShapeDtypeStruc...  3.3 us
    pallas_call x1, Pallas kernels, compute(): pl.pallas_call(near_kernel, out_shape=(jax.ShapeDtypeStruct((6, cols, nz...  2.49 us
  transfers between devices with their start and end apart: 22, of which 13 were waited for; matrix products, arithmetic and copies ran while one was open for 7% of the time, Pallas kernels for 2%

profile of v5, /device:TPU:6, one launch (start us, length us, event | category | flops | bytes accessed | tf_op | source)
XLA Modules:
  0.0 119.5 jit_solution(10615718903938366697)
XLA Ops:
  0.0 0.0 copy-start
  0.0 0.7 copy-done
  0.7 0.7 fusion.8
  1.4 0.8 fusion.5
  2.2 0.6 broadcast_in_dim.31
  2.8 8.5 %all-to-all-start = ((bf16[8,40,128]{2,1,0:T(8,128)(2,1)}), bf16[8,40,128]{2,1,0:T(8,128)(2,1)S(1)}, u32[]{:S(2)}, u32[]{:S(2)}) async-start(bf16[8,40,128]{2,1,0:T(8,128)(2,1)} %broadcast_in_dim.31), calls=%async_computation | async-start | bytes 163840 | tf_op jit(solution)/shard_map/all_to_all | solution.py:147
  11.3 1.0 copy.21
  12.3 0.1 collective-permute-start.1
  12.4 7.4 %all-to-all-done = bf16[8,40,128]{2,1,0:T(8,128)(2,1)S(1)} async-done(((bf16[8,40,128]{2,1,0:T(8,128)(2,1)}), bf16[8,40,128]{2,1,0:T(8,128)(2,1)S(1)}, u32[]{:S(2)}, u32[]{:S(2)}) %all-to-all-start) | async-done | bytes 81952 | tf_op jit(solution)/shard_map/all_to_all | solution.py:147
  19.9 1.3 %broadcast_in_dim.33 = bf16[16,320,128]{2,1,0:T(8,128)(2,1)} broadcast(bf16[320,128]{1,0:T(8,128)(2,1)S(1)} %bitcast.73), dimensions={1,2} | broadcast | bytes 1392640 | tf_op jit(solution)/shard_map/broadcast_in_dim | solution.py:150
  21.2 7.4 %all-to-all-start.1 = ((bf16[16,320,128]{2,1,0:T(8,128)(2,1)}), bf16[16,320,128]{2,1,0:T(8,128)(2,1)S(1)}, u32[]{:S(2)}, u32[]{:S(2)}) async-start(bf16[16,320,128]{2,1,0:T(8,128)(2,1)} %broadcast_in_dim.33), calls=%async_computation.1 | async-start | bytes 2621440 | tf_op jit(solution)/shard_map/all_to_all | solution.py:151
  28.7 0.0 collective-permute-done.1
  28.7 1.6 %collective-permute-start.3 = (f32[2,32,256]{2,1,0:T(8,128)S(1)}, f32[2,32,256]{2,1,0:T(8,128)S(1)}, u32[]{:S(2)}, u32[]{:S(2)}) collective-permute-start(f32[2,32,256]{2,1,0:T(8,128)S(1)} %get-tuple-element.18), channel_id=1, source_target_pairs={{0,128},{128,0},{1,129},{129,1},{2,130},{130,2},{3,131},{131,3},{4... | collective-permute-start | bytes 196616 | tf_op jit(solution)/shard_map/ppermute | solution.py:20
  30.3 2.1 %collective-permute-start.4 = (f32[2,32,256]{2,1,0:T(8,128)S(1)}, f32[2,32,256]{2,1,0:T(8,128)S(1)}, u32[]{:S(2)}, u32[]{:S(2)}) collective-permute-start(f32[2,32,256]{2,1,0:T(8,128)S(1)} %get-tuple-element.18), channel_id=1, source_target_pairs={{0,160},{32,128},{128,32},{160,0},{1,161},{33,129},{129,33},{161,1... | collective-permute-start | bytes 196616 | tf_op jit(solution)/shard_map/ppermute | solution.py:25
  32.4 0.6 collective-permute-start.2
  33.0 12.3 %collective-permute-done.3 = f32[2,32,256]{2,1,0:T(8,128)S(1)} collective-permute-done((f32[2,32,256]{2,1,0:T(8,128)S(1)}, f32[2,32,256]{2,1,0:T(8,128)S(1)}, u32[]{:S(2)}, u32[]{:S(2)}) %collective-permute-start.3) | collective-permute-done | bytes 65568 | tf_op jit(solution)/shard_map/ppermute | solution.py:20
  45.3 1.2 %collective-permute-done.4 = f32[2,32,256]{2,1,0:T(8,128)S(1)} collective-permute-done((f32[2,32,256]{2,1,0:T(8,128)S(1)}, f32[2,32,256]{2,1,0:T(8,128)S(1)}, u32[]{:S(2)}, u32[]{:S(2)}) %collective-permute-start.4) | collective-permute-done | bytes 65568 | tf_op jit(solution)/shard_map/ppermute | solution.py:25
  46.5 1.0 collective-permute-done.2
  47.5 0.1 collective-permute-start.5
  47.6 2.0 %collective-permute-start.8 = (f32[2,2,2,32,256]{4,3,2,1,0:T(8,128)S(1)}, f32[2,2,2,32,256]{4,3,2,1,0:T(8,128)S(1)}, u32[]{:S(2)}, u32[]{:S(2)}) collective-permute-start(f32[2,2,2,32,256]{4,3,2,1,0:T(8,128)S(1)} %pad_maximum_fusion), channel_id=1, source_target_pairs={{0,1},{1,2},{2,3},{3,4},{4,5},{5,6},{6,7},{7,0},{8,9},{9,10},{10,1... | collective-permute-start | bytes 786440 | tf_op jit(solution)/shard_map/ppermute | solution.py:20
  49.6 4.8 %collective-permute-done.5 = f32[2,2,2,32,256]{4,3,2,1,0:T(8,128)S(1)} collective-permute-done((f32[2,2,2,32,256]{4,3,2,1,0:T(8,128)S(1)}, f32[2,2,2,32,256]{4,3,2,1,0:T(8,128)S(1)}, u32[]{:S(2)}, u32[]{:S(2)}) %collective-permute-start.5) | collective-permute-done | bytes 262176 | tf_op jit(solution)/shard_map/ppermute | solution.py:20
  54.4 0.0 copy-start.1
  54.4 1.1 collective-permute-start.6
  55.5 0.0 collective-permute-done.8
  55.5 1.0 collective-permute-start.9
  56.5 5.7 %collective-permute-done.6 = f32[2,2,2,32,256]{4,3,2,1,0:T(8,128)} collective-permute-done((f32[2,2,2,32,256]{4,3,2,1,0:T(8,128)S(1)}, f32[2,2,2,32,256]{4,3,2,1,0:T(8,128)}, u32[]{:S(2)}, u32[]{:S(2)}) %collective-permute-start.6) | collective-permute-done | bytes 262176 | tf_op jit(solution)/shard_map/ppermute | solution.py:20
  62.1 1.0 collective-permute-start.7
  63.1 0.0 collective-permute-done.9
  63.1 0.0 copy-done.1
  63.2 1.0 collective-permute-start.10
  64.2 0.0 all-to-all-done.1.own_ref
  64.2 0.0 collective-permute-start
  64.2 1.0 bitcast_dynamic-update-slice_fusion.5
  65.1 1.0 bitcast_dynamic-update-slice_fusion.4
  66.1 5.1 %collective-permute-done.10 = f32[2,2,2,32,256]{4,3,2,1,0:T(8,128)} collective-permute-done((f32[2,2,2,32,256]{4,3,2,1,0:T(8,128)}, f32[2,2,2,32,256]{4,3,2,1,0:T(8,128)}, u32[]{:S(2)}, u32[]{:S(2)}) %collective-permute-start.10) | collective-permute-done | bytes 262176 | tf_op jit(solution)/shard_map/ppermute | solution.py:20
  71.3 0.3 collective-permute-start.11
  71.6 0.0 collective-permute-done.7
  71.6 1.0 bitcast_dynamic-update-slice_fusion.3
  72.6 1.0 bitcast_dynamic-update-slice_fusion.2
  73.5 1.0 bitcast_dynamic-update-slice_fusion.1
  74.5 4.5 %collective-permute-done.11.late = f32[2,2,2,32,256]{4,3,2,1,0:T(8,128)S(1)} collective-permute-done((f32[2,2,2,32,256]{4,3,2,1,0:T(8,128)}, f32[2,2,2,32,256]{4,3,2,1,0:T(8,128)S(1)}, u32[]{:S(2)}, u32[]{:S(2)}) %collective-permute-start.11) | collective-permute-done | bytes 262176 | tf_op jit(solution)/shard_map/ppermute | solution.py:20
  79.1 0.0 collective-permute-done.twin_ref
  79.1 3.3 %solve.1 = (bf16[8,32,1024]{2,1,0:T(8,128)(2,1)}, bf16[8,32,1024]{2,1,0:T(8,128)(2,1)}, bf16[32,1024]{1,0:T(8,128)(2,1)S(1)}) custom-call(s32[1]{0:T(128)} %bitcast.2.pos_ref, bf16[16,320,128]{2,1,0:T(8,128)(2,1)S(1)} %all-to-all-done.1.own_ref, bf16[16,320,128]{2,1,0:T(8,128)(2,1)S(1)} %collective-permute-done.twin_ref, ...), custom_call_target="tpu_custom_call" | custom-call | tf_op jit(solution)/shard_map/solve/pallas_call | solution.py:177
  82.4 2.1 %collective-permute-start.15 = (bf16[8,32,1024]{2,1,0:T(8,128)(2,1)}, bf16[8,32,1024]{2,1,0:T(8,128)(2,1)S(1)}, u32[]{:S(2)}, u32[]{:S(2)}) collective-permute-start(bf16[8,32,1024]{2,1,0:T(8,128)(2,1)} %get-tuple-element.11.refs_0_), channel_id=1, source_target_pairs={{0,8},{8,16},{16,24},{24,0},{1,9},{9,17},{17,25},{25,1},{2,10},{10... | collective-permute-start | bytes 1572872 | tf_op jit(solution)/shard_map/ppermute | solution.py:20
  84.5 0.0 collective-permute-start.16
  84.5 1.7 %collective-permute-start.14 = (bf16[8,32,1024]{2,1,0:T(8,128)(2,1)}, bf16[8,32,1024]{2,1,0:T(8,128)(2,1)S(1)}, u32[]{:S(2)}, u32[]{:S(2)}) collective-permute-start(bf16[8,32,1024]{2,1,0:T(8,128)(2,1)} %get-tuple-element.11.refs_0_), channel_id=1, source_target_pairs={{0,24},{8,0},{16,8},{24,16},{1,25},{9,1},{17,9},{25,17},{2,26},{10... | collective-permute-start | bytes 1572872 | tf_op jit(solution)/shard_map/ppermute | solution.py:20
  86.2 1.6 %collective-permute-start.17 = (bf16[8,32,1024]{2,1,0:T(8,128)(2,1)}, bf16[8,32,1024]{2,1,0:T(8,128)(2,1)S(1)}, u32[]{:S(2)}, u32[]{:S(2)}) collective-permute-start(bf16[8,32,1024]{2,1,0:T(8,128)(2,1)} %get-tuple-element.12.refs_3_), channel_id=1, source_target_pairs={{0,8},{8,16},{16,24},{24,0},{1,9},{9,17},{17,25},{25,1},{2,10},{10... | collective-permute-start | bytes 1572872 | tf_op jit(solution)/shard_map/ppermute | solution.py:20
  87.7 9.6 %collective-permute-done.15.refs_2_ = bf16[8,32,1024]{2,1,0:T(8,128)(2,1)S(1)} collective-permute-done((bf16[8,32,1024]{2,1,0:T(8,128)(2,1)}, bf16[8,32,1024]{2,1,0:T(8,128)(2,1)S(1)}, u32[]{:S(2)}, u32[]{:S(2)}) %collective-permute-start.15) | collective-permute-done | bytes 524320 | tf_op jit(solution)/shard_map/ppermute | solution.py:20
  97.4 3.3 %collective-permute-start.18 = (bf16[8,32,1024]{2,1,0:T(8,128)(2,1)S(1)}, bf16[8,32,1024]{2,1,0:T(8,128)(2,1)S(1)}, u32[]{:S(2)}, u32[]{:S(2)}) collective-permute-start(bf16[8,32,1024]{2,1,0:T(8,128)(2,1)S(1)} %collective-permute-done.15.refs_2_), channel_id=1, source_target_pairs={{0,8},{8,16},{16,24},{24,0},{1,9},{9,17},{17,25},{25,1},{2,10},{10... | collective-permute-start | bytes 1572872 | tf_op jit(solution)/shard_map/ppermute | solution.py:20
  100.7 0.0 collective-permute-done.16.refs_4_
  100.7 0.0 collective-permute-start.19
  100.7 0.0 collective-permute-start.12
  100.7 4.3 %collective-permute-done.12.m1 = bf16[32,1024]{1,0:T(8,128)(2,1)S(1)} collective-permute-done((bf16[32,1024]{1,0:T(8,128)(2,1)S(1)}, bf16[32,1024]{1,0:T(8,128)(2,1)S(1)}, u32[]{:S(2)}, u32[]{:S(2)}) %collective-permute-start.12) | collective-permute-done | bytes 65568 | tf_op jit(solution)/shard_map/ppermute | solution.py:20
  105.0 0.7 pad_maximum_fusion.3
  105.6 0.0 collective-permute-start.13
  105.6 0.1 stack.89.pos_ref
  105.7 1.5 %collective-permute-done.13.m2 = bf16[2,32,1024]{2,1,0:T(8,128)(2,1)S(1)} collective-permute-done((bf16[2,32,1024]{2,1,0:T(8,128)(2,1)}, bf16[2,32,1024]{2,1,0:T(8,128)(2,1)S(1)}, u32[]{:S(2)}, u32[]{:S(2)}) %collective-permute-start.13) | collective-permute-done | bytes 131104 | tf_op jit(solution)/shard_map/ppermute | solution.py:20
  107.2 4.4 %collective-permute-done.14.refs_1_ = bf16[8,32,1024]{2,1,0:T(8,128)(2,1)S(1)} collective-permute-done((bf16[8,32,1024]{2,1,0:T(8,128)(2,1)}, bf16[8,32,1024]{2,1,0:T(8,128)(2,1)S(1)}, u32[]{:S(2)}, u32[]{:S(2)}) %collective-permute-start.14) | collective-permute-done | bytes 524320 | tf_op jit(solution)/shard_map/ppermute | solution.py:20
  111.6 0.0 collective-permute-done.17.refs_5_
  111.6 2.5 %near.1 = (f32[6,128,256]{2,1,0:T(8,128)S(1)}, bf16[4,32,1024]{2,1,0:T(8,128)(2,1)S(1)}) custom-call(s32[5]{0:T(128)S(1)} %stack.89.pos_ref, bf16[32,1024]{1,0:T(8,128)(2,1)S(1)} %get-tuple-element.10.m0, bf16[32,1024]{1,0:T(8,128)(2,1)S(1)} %collective-permute-done.12.m1, bf16[2,32,1024]{2,1,0:T(8,128)(2,1)S(1)} %collective-permute-done.13.m2, ...), custom_call_target="tpu_custom_call" | custom-call | tf_op jit(solution)/shard_map/near/pallas_call | solution.py:195
  114.1 0.0 collective-permute-done.18.last0
  114.1 3.1 %collective-permute-done.19.last1 = bf16[8,32,1024]{2,1,0:T(8,128)(2,1)S(1)} collective-permute-done((bf16[8,32,1024]{2,1,0:T(8,128)(2,1)S(1)}, bf16[8,32,1024]{2,1,0:T(8,128)(2,1)S(1)}, u32[]{:S(2)}, u32[]{:S(2)}) %collective-permute-start.19) | collective-permute-done | bytes 524320 | tf_op jit(solution)/shard_map/ppermute | solution.py:20
  117.2 2.4 %far.1 = f32[128,1,2048]{2,1,0:T(1,128)} custom-call(s32[5]{0:T(128)S(1)} %stack.89.pos_ref, f32[6,128,256]{2,1,0:T(8,128)S(1)} %get-tuple-element.13.near, bf16[4,32,1024]{2,1,0:T(8,128)(2,1)S(1)} %get-tuple-element.14.own, bf16[8,32,1024]{2,1,0:T(8,128)(2,1)S(1)} %collective-permute-done.18.last0, bf16[8,32,1024]{2,1,0:T(8,128)(2,1)S(1)} %collective-permute-done.19.last1), custom_call_target="tpu_custom_call" | custom-call | tf_op jit(solution)/shard_map/far/pallas_call | solution.py:206
  (11 shorter events, 0.2 us)
Async XLA Ops:
  0.0 0.7 copy-start
  2.8 17.0 %all-to-all-start = ((bf16[8,40,128]{2,1,0:T(8,128)(2,1)}), bf16[8,40,128]{2,1,0:T(8,128)(2,1)S(1)}, u32[]{:S(2)}, u32[]{:S(2)}) async-start(bf16[8,40,128]{2,1,0:T(8,128)(2,1)} %broadcast_in_dim.31), calls=%async_computation | async-start | bytes 163840 | tf_op jit(solution)/shard_map/all_to_all | solution.py:147
  12.3 16.4 %collective-permute-start.1 = (f32[128,256]{1,0:T(8,128)S(1)}, f32[128,256]{1,0:T(8,128)S(1)}, u32[]{:S(2)}, u32[]{:S(2)}) collective-permute-start(f32[128,256]{1,0:T(8,128)S(1)} %bitcast.69), channel_id=1, source_target_pairs={{0,64},{64,0},{1,65},{65,1},{2,66},{66,2},{3,67},{67,3},{4,68},{68... | collective-permute-start | bytes 393224 | tf_op jit(solution)/shard_map/ppermute | solution.py:20
  21.2 42.9 %all-to-all-start.1 = ((bf16[16,320,128]{2,1,0:T(8,128)(2,1)}), bf16[16,320,128]{2,1,0:T(8,128)(2,1)S(1)}, u32[]{:S(2)}, u32[]{:S(2)}) async-start(bf16[16,320,128]{2,1,0:T(8,128)(2,1)} %broadcast_in_dim.33), calls=%async_computation.1 | async-start | bytes 2621440 | tf_op jit(solution)/shard_map/all_to_all | solution.py:151
  28.7 16.5 %collective-permute-start.3 = (f32[2,32,256]{2,1,0:T(8,128)S(1)}, f32[2,32,256]{2,1,0:T(8,128)S(1)}, u32[]{:S(2)}, u32[]{:S(2)}) collective-permute-start(f32[2,32,256]{2,1,0:T(8,128)S(1)} %get-tuple-element.18), channel_id=1, source_target_pairs={{0,128},{128,0},{1,129},{129,1},{2,130},{130,2},{3,131},{131,3},{4... | collective-permute-start | bytes 196616 | tf_op jit(solution)/shard_map/ppermute | solution.py:20
  30.3 16.2 %collective-permute-start.4 = (f32[2,32,256]{2,1,0:T(8,128)S(1)}, f32[2,32,256]{2,1,0:T(8,128)S(1)}, u32[]{:S(2)}, u32[]{:S(2)}) collective-permute-start(f32[2,32,256]{2,1,0:T(8,128)S(1)} %get-tuple-element.18), channel_id=1, source_target_pairs={{0,160},{32,128},{128,32},{160,0},{1,161},{33,129},{129,33},{161,1... | collective-permute-start | bytes 196616 | tf_op jit(solution)/shard_map/ppermute | solution.py:25
  32.4 15.1 %collective-permute-start.2 = (f32[2,32,256]{2,1,0:T(8,128)S(1)}, f32[2,32,256]{2,1,0:T(8,128)S(1)}, u32[]{:S(2)}, u32[]{:S(2)}) collective-permute-start(f32[2,32,256]{2,1,0:T(8,128)S(1)} %get-tuple-element.19), channel_id=1, source_target_pairs={{0,32},{32,0},{1,33},{33,1},{2,34},{34,2},{3,35},{35,3},{4,36},{36... | collective-permute-start | bytes 196616 | tf_op jit(solution)/shard_map/ppermute | solution.py:20
  47.5 6.9 %collective-permute-start.5 = (f32[2,2,2,32,256]{4,3,2,1,0:T(8,128)S(1)}, f32[2,2,2,32,256]{4,3,2,1,0:T(8,128)S(1)}, u32[]{:S(2)}, u32[]{:S(2)}) collective-permute-start(f32[2,2,2,32,256]{4,3,2,1,0:T(8,128)S(1)} %pad_maximum_fusion), channel_id=1, source_target_pairs={{0,7},{1,0},{2,1},{3,2},{4,3},{5,4},{6,5},{7,6},{8,15},{9,8},{10,9... | collective-permute-start | bytes 786440 | tf_op jit(solution)/shard_map/ppermute | solution.py:20
  47.6 7.8 %collective-permute-start.8 = (f32[2,2,2,32,256]{4,3,2,1,0:T(8,128)S(1)}, f32[2,2,2,32,256]{4,3,2,1,0:T(8,128)S(1)}, u32[]{:S(2)}, u32[]{:S(2)}) collective-permute-start(f32[2,2,2,32,256]{4,3,2,1,0:T(8,128)S(1)} %pad_maximum_fusion), channel_id=1, source_target_pairs={{0,1},{1,2},{2,3},{3,4},{4,5},{5,6},{6,7},{7,0},{8,9},{9,10},{10,1... | collective-permute-start | bytes 786440 | tf_op jit(solution)/shard_map/ppermute | solution.py:20
  54.4 8.8 %copy-start.1 = (f32[2,2,2,32,256]{4,3,2,1,0:T(8,128)}, f32[2,2,2,32,256]{4,3,2,1,0:T(8,128)S(1)}, u32[]{:S(2)}) copy-start(f32[2,2,2,32,256]{4,3,2,1,0:T(8,128)S(1)} %collective-permute-done.5) | copy-start | bytes 786436
  54.4 7.7 %collective-permute-start.6 = (f32[2,2,2,32,256]{4,3,2,1,0:T(8,128)S(1)}, f32[2,2,2,32,256]{4,3,2,1,0:T(8,128)}, u32[]{:S(2)}, u32[]{:S(2)}) collective-permute-start(f32[2,2,2,32,256]{4,3,2,1,0:T(8,128)S(1)} %collective-permute-done.5), channel_id=1, source_target_pairs={{0,7},{1,0},{2,1},{3,2},{4,3},{5,4},{6,5},{7,6},{8,15},{9,8},{10,9... | collective-permute-start | bytes 786440 | tf_op jit(solution)/shard_map/ppermute | solution.py:20
  55.5 7.7 %collective-permute-start.9 = (f32[2,2,2,32,256]{4,3,2,1,0:T(8,128)S(1)}, f32[2,2,2,32,256]{4,3,2,1,0:T(8,128)}, u32[]{:S(2)}, u32[]{:S(2)}) collective-permute-start(f32[2,2,2,32,256]{4,3,2,1,0:T(8,128)S(1)} %collective-permute-done.8), channel_id=1, source_target_pairs={{0,1},{1,2},{2,3},{3,4},{4,5},{5,6},{6,7},{7,0},{8,9},{9,10},{10,1... | collective-permute-start | bytes 786440 | tf_op jit(solution)/shard_map/ppermute | solution.py:20
  62.1 9.4 %collective-permute-start.7 = (f32[2,2,2,32,256]{4,3,2,1,0:T(8,128)}, f32[2,2,2,32,256]{4,3,2,1,0:T(8,128)}, u32[]{:S(2)}, u32[]{:S(2)}) collective-permute-start(f32[2,2,2,32,256]{4,3,2,1,0:T(8,128)} %collective-permute-done.6), channel_id=1, source_target_pairs={{0,7},{1,0},{2,1},{3,2},{4,3},{5,4},{6,5},{7,6},{8,15},{9,8},{10,9... | collective-permute-start | bytes 786440 | tf_op jit(solution)/shard_map/ppermute | solution.py:20
  63.2 8.1 %collective-permute-start.10 = (f32[2,2,2,32,256]{4,3,2,1,0:T(8,128)}, f32[2,2,2,32,256]{4,3,2,1,0:T(8,128)}, u32[]{:S(2)}, u32[]{:S(2)}) collective-permute-start(f32[2,2,2,32,256]{4,3,2,1,0:T(8,128)} %collective-permute-done.9), channel_id=1, source_target_pairs={{0,1},{1,2},{2,3},{3,4},{4,5},{5,6},{6,7},{7,0},{8,9},{9,10},{10,1... | collective-permute-start | bytes 786440 | tf_op jit(solution)/shard_map/ppermute | solution.py:20
  64.2 14.9 %collective-permute-start = (bf16[16,320,128]{2,1,0:T(8,128)(2,1)S(1)}, bf16[16,320,128]{2,1,0:T(8,128)(2,1)S(1)}, u32[]{:S(2)}, u32[]{:S(2)}) collective-permute-start(bf16[16,320,128]{2,1,0:T(8,128)(2,1)S(1)} %all-to-all-done.1.own_ref), channel_id=1, source_target_pairs={{0,64},{64,0},{1,65},{65,1},{2,66},{66,2},{3,67},{67,3},{4,68},{68... | collective-permute-start | bytes 3932168 | tf_op jit(solution)/shard_map/ppermute | solution.py:20
  71.3 7.8 %collective-permute-start.11 = (f32[2,2,2,32,256]{4,3,2,1,0:T(8,128)}, f32[2,2,2,32,256]{4,3,2,1,0:T(8,128)S(1)}, u32[]{:S(2)}, u32[]{:S(2)}) collective-permute-start(f32[2,2,2,32,256]{4,3,2,1,0:T(8,128)} %collective-permute-done.10), channel_id=1, source_target_pairs={{0,1},{1,2},{2,3},{3,4},{4,5},{5,6},{6,7},{7,0},{8,9},{9,10},{10,1... | collective-permute-start | bytes 786440 | tf_op jit(solution)/shard_map/ppermute | solution.py:20
  82.4 15.0 %collective-permute-start.15 = (bf16[8,32,1024]{2,1,0:T(8,128)(2,1)}, bf16[8,32,1024]{2,1,0:T(8,128)(2,1)S(1)}, u32[]{:S(2)}, u32[]{:S(2)}) collective-permute-start(bf16[8,32,1024]{2,1,0:T(8,128)(2,1)} %get-tuple-element.11.refs_0_), channel_id=1, source_target_pairs={{0,8},{8,16},{16,24},{24,0},{1,9},{9,17},{17,25},{25,1},{2,10},{10... | collective-permute-start | bytes 1572872 | tf_op jit(solution)/shard_map/ppermute | solution.py:20
  84.5 16.2 %collective-permute-start.16 = (bf16[8,32,1024]{2,1,0:T(8,128)(2,1)}, bf16[8,32,1024]{2,1,0:T(8,128)(2,1)S(1)}, u32[]{:S(2)}, u32[]{:S(2)}) collective-permute-start(bf16[8,32,1024]{2,1,0:T(8,128)(2,1)} %get-tuple-element.12.refs_3_), channel_id=1, source_target_pairs={{0,24},{8,0},{16,8},{24,16},{1,25},{9,1},{17,9},{25,17},{2,26},{10... | collective-permute-start | bytes 1572872 | tf_op jit(solution)/shard_map/ppermute | solution.py:20
  84.5 27.1 %collective-permute-start.14 = (bf16[8,32,1024]{2,1,0:T(8,128)(2,1)}, bf16[8,32,1024]{2,1,0:T(8,128)(2,1)S(1)}, u32[]{:S(2)}, u32[]{:S(2)}) collective-permute-start(bf16[8,32,1024]{2,1,0:T(8,128)(2,1)} %get-tuple-element.11.refs_0_), channel_id=1, source_target_pairs={{0,24},{8,0},{16,8},{24,16},{1,25},{9,1},{17,9},{25,17},{2,26},{10... | collective-permute-start | bytes 1572872 | tf_op jit(solution)/shard_map/ppermute | solution.py:20
  86.2 25.4 %collective-permute-start.17 = (bf16[8,32,1024]{2,1,0:T(8,128)(2,1)}, bf16[8,32,1024]{2,1,0:T(8,128)(2,1)S(1)}, u32[]{:S(2)}, u32[]{:S(2)}) collective-permute-start(bf16[8,32,1024]{2,1,0:T(8,128)(2,1)} %get-tuple-element.12.refs_3_), channel_id=1, source_target_pairs={{0,8},{8,16},{16,24},{24,0},{1,9},{9,17},{17,25},{25,1},{2,10},{10... | collective-permute-start | bytes 1572872 | tf_op jit(solution)/shard_map/ppermute | solution.py:20
  97.4 16.7 %collective-permute-start.18 = (bf16[8,32,1024]{2,1,0:T(8,128)(2,1)S(1)}, bf16[8,32,1024]{2,1,0:T(8,128)(2,1)S(1)}, u32[]{:S(2)}, u32[]{:S(2)}) collective-permute-start(bf16[8,32,1024]{2,1,0:T(8,128)(2,1)S(1)} %collective-permute-done.15.refs_2_), channel_id=1, source_target_pairs={{0,8},{8,16},{16,24},{24,0},{1,9},{9,17},{17,25},{25,1},{2,10},{10... | collective-permute-start | bytes 1572872 | tf_op jit(solution)/shard_map/ppermute | solution.py:20
  100.7 16.5 %collective-permute-start.19 = (bf16[8,32,1024]{2,1,0:T(8,128)(2,1)S(1)}, bf16[8,32,1024]{2,1,0:T(8,128)(2,1)S(1)}, u32[]{:S(2)}, u32[]{:S(2)}) collective-permute-start(bf16[8,32,1024]{2,1,0:T(8,128)(2,1)S(1)} %collective-permute-done.16.refs_4_), channel_id=1, source_target_pairs={{0,24},{8,0},{16,8},{24,16},{1,25},{9,1},{17,9},{25,17},{2,26},{10... | collective-permute-start | bytes 1572872 | tf_op jit(solution)/shard_map/ppermute | solution.py:20
  100.7 4.3 %collective-permute-start.12 = (bf16[32,1024]{1,0:T(8,128)(2,1)S(1)}, bf16[32,1024]{1,0:T(8,128)(2,1)S(1)}, u32[]{:S(2)}, u32[]{:S(2)}) collective-permute-start(bf16[32,1024]{1,0:T(8,128)(2,1)S(1)} %get-tuple-element.10.m0), channel_id=1, source_target_pairs={{0,128},{128,0},{1,129},{129,1},{2,130},{130,2},{3,131},{131,3},{4... | collective-permute-start | bytes 196616 | tf_op jit(solution)/shard_map/ppermute | solution.py:20
  105.6 1.6 %collective-permute-start.13 = (bf16[2,32,1024]{2,1,0:T(8,128)(2,1)}, bf16[2,32,1024]{2,1,0:T(8,128)(2,1)S(1)}, u32[]{:S(2)}, u32[]{:S(2)}) collective-permute-start(bf16[2,32,1024]{2,1,0:T(8,128)(2,1)} %pad_maximum_fusion.3), channel_id=1, source_target_pairs={{0,64},{64,0},{1,65},{65,1},{2,66},{66,2},{3,67},{67,3},{4,68},{68... | collective-permute-start | bytes 393224 | tf_op jit(solution)/shard_map/ppermute | solution.py:20

commit v6 on v5

v6 whole, which is shorter than its diff:
```python
import functools

import jax
import jax.numpy as jnp
from jax import lax
from jax.experimental import pallas as pl
from jax.experimental.pallas import tpu as pltpu
from jax.sharding import Mesh, PartitionSpec as P


FAC = ("yl", "core")
COL = ("yh", "x", "z")
NT = (((1,), (1,)), ((), ()))
BF = jnp.bfloat16
F32 = jnp.float32
LANES = 128
MIB = 1024 * 1024


def shift(a, axis, by=1):
    n = lax.axis_size(axis)
    return lax.ppermute(a, axis, [(i, (i + by) % n) for i in range(n)])


def by_index(mine, other, index):
    first = index == 0
    return jnp.stack([jnp.where(first, mine, other), jnp.where(first, other, mine)])


def split(a):
    hi = lax.reduce_precision(a, 8, 7)
    return hi.astype(BF), (a - hi).astype(BF)


def dot(a, b):
    return jnp.dot(a, b, preferred_element_type=F32)


def solve_kernel(pos_ref, own_ref, twin_ref, *refs):
    rights, late, outs = refs[:7], refs[7:9], refs[9:]
    peers, _, lanes = own_ref.shape
    half = peers // 2
    share, w = rights[0].shape[2:]

    def square(ref, yl, block):
        parts = [
            ref[yl * half : (yl + 1) * half, r : r + 32, :].reshape(half * 32, lanes)
            for r in (64 * block, 64 * block + 32)
        ]
        return jnp.concatenate(parts, axis=1)

    def right(yl, core):
        rows = [b[yl, core] for b in rights]
        rows.insert(4, late[yl][core])
        return jnp.concatenate(rows, axis=0)

    def factor(p, q):
        return ((0, 3) if q == 2 else (p // 2, 2 + q))

    def run(pair):
        solved = []
        for p in range(4):
            yl, core = divmod(p, 2)
            ref = pair[core]
            r = right(yl, core)
            for q in range(p):
                r = r - dot(solved[q], square(ref, *factor(p, q)))
            rhi = r.astype(BF)
            rlo = (r - rhi.astype(F32)).astype(BF)
            dhi = square(ref, yl, 0)
            y = (dot(rlo, dhi) + dot(rhi, square(ref, yl, 1))) + dot(rhi, dhi)
            y = y.astype(BF)
            solved.append(y)
            at = slice(p * w, (p + 1) * w)
            parts = y.reshape((2, -1, share, w))
            for i in range(2):
                outs[i][:, :, at] = parts[i]
            outs[2][:, at] = y[:share]

    @pl.when(pos_ref[0] == 0)
    def _():
        run((own_ref, twin_ref))

    @pl.when(pos_ref[0] == 1)
    def _():
        run((twin_ref, own_ref))


def columns(lhs, parts, z):
    nz, share, k = parts[0].shape
    rhs = jnp.concatenate([p[...].reshape(nz * share, k) for p in parts], axis=0)
    out = lax.dot_general(lhs, rhs, NT, preferred_element_type=F32)
    return pltpu.roll(out, z * share, 1)


NEAR = ((0, 0), (0, 1), (0, 3), (0, 2), (1, 0))
NEXT = ((1, 1), (1, 3))
LAST = ((1, 2),)


def near_kernel(pos_ref, m0, m1, m2, *refs):
    blocks, out_ref, own = refs[:-2], refs[-2], refs[-1]
    yl, core = pos_ref[1], pos_ref[2]
    own[2 * yl + core] = m0[...]
    own[2 * (1 - yl) + core] = m1[...]
    own[2 * yl + (1 - core)] = m2[0]
    own[2 * (1 - yl) + (1 - core)] = m2[1]
    lhs = own[...].reshape(-1, own.shape[2])
    for i, (dyh, dx) in enumerate(NEAR):
        value = columns(lhs, blocks[2 * i : 2 * i + 2], pos_ref[0])
        out_ref[:, 0, unit(pos_ref, dyh, dx, value.shape[1])] = value


def unit(pos_ref, dyh, dx, cols):
    at = lax.rem(pos_ref[3] + dyh, 2) * 4 + lax.rem(pos_ref[4] + dx, 4)
    return pl.ds(pl.multiple_of(at * cols, cols), cols)


def more_kernel(offsets, pos_ref, before, own, *refs):
    blocks, out_ref, stage, sems = refs[:-3], refs[-3], refs[-2], refs[-1]
    lhs = own[...].reshape(-1, own.shape[2])
    copies = []
    for i, (dyh, dx) in enumerate(offsets):
        stage[i, :, 0, :] = columns(lhs, blocks[2 * i : 2 * i + 2], pos_ref[0])
        at = unit(pos_ref, dyh, dx, stage.shape[3])
        copies.append(
            pltpu.make_async_copy(stage.at[i], out_ref.at[:, :, at], sems.at[i])
        )
        copies[-1].start()
    for copy in copies:
        copy.wait()


def y_shift(a, by):
    pairs = []
    for yl in range(2):
        for yh in range(2):
            y = (2 * yh + yl + by) % 4
            pairs.append((2 * yl + yh, 2 * (y % 2) + y // 2))
    return lax.ppermute(a, ("yl", "yh"), pairs)


def x_ring(halves):
    found = {0: halves}
    found[3] = [shift(h, "x", 1) for h in halves]
    found[1] = [shift(h, "x", -1) for h in halves]
    up = shift(found[3][0], "x", 1)
    down = shift(found[1][1], "x", -1)
    found[2] = [up, down]
    return found


def compute(lower_factor, panel_inverse, right_side, fill):
    w, kw = panel_inverse.shape[2:]
    fac = lax.axis_index(FAC)
    yl, core, yh, x, z = (lax.axis_index(a) for a in FAC + COL)
    nx = lax.axis_size("x")
    panels = fill.shape[0]
    halves = w // LANES

    hi, lo = split(panel_inverse[0, 0].T)
    keep = lax.dynamic_slice_in_dim(fill, fac, 1, 0)[0, : panels - 1] == 1
    low = lower_factor[0, 0, : panels - 1].transpose(0, 2, 1)
    low = jnp.where(keep[:, None, None], low, jnp.zeros_like(low))
    moved = shift(low[2], "yl")
    extra = jnp.where(yl == 0, moved, low[1])
    rows = jnp.stack([hi, lo, low[0], extra])
    nt = rows.shape[0]
    rows = rows.reshape(nt, kw, halves, LANES).transpose(0, 2, 1, 3)
    rows = rows.reshape(-1, LANES)
    nz = lax.axis_size("z")
    npeer = 2 * 2 * nx
    rows = jnp.broadcast_to(rows[None], (nz,) + rows.shape)
    got = lax.all_to_all(rows, "z", 0, 0, tiled=True)
    got = got.reshape(nz, nt * halves, kw, LANES).transpose(1, 0, 2, 3)
    got = got.reshape(-1, LANES)
    got = jnp.broadcast_to(got[None], (npeer,) + got.shape)
    held = lax.all_to_all(got, ("yl", "yh", "x"), 0, 0, tiled=True)
    twin = shift(held, "core")

    share = right_side.shape[3] // panels
    bt = right_side[0, 0].T
    bo = shift(bt, "core")
    bt = by_index(bt, bo, core)
    bt = bt.reshape(2, 2, 2, share, w)
    bt = lax.dynamic_index_in_dim(bt, core, 2, keepdims=False)
    same = lax.dynamic_index_in_dim(bt, yl, 1, keepdims=False)
    cross = lax.dynamic_index_in_dim(bt, 1 - yl, 1, keepdims=False)
    cross = shift(cross, "yl")
    bt = by_index(same, cross, yl)
    ups, downs = [bt], [bt]
    for _ in range(1, 4):
        ups.append(shift(ups[-1], "z", 1))
        downs.append(shift(downs[-1], "z", -1))
    late = shift(ups[-1][0], "z", 1), shift(downs[-1][1], "z", -1)
    rights = downs + ups[:0:-1]

    vm = pl.BlockSpec(memory_space=pltpu.VMEM)
    sm = pl.BlockSpec(memory_space=pltpu.SMEM)
    hbm = pl.BlockSpec(memory_space=pl.ANY)
    params = pltpu.CompilerParams(vmem_limit_bytes=16 * MIB)
    pos = jnp.stack([core]).astype(jnp.int32)
    part = jax.ShapeDtypeStruct((nz // 2, share, panels * w), BF)
    *solved, mine = pl.pallas_call(
        solve_kernel,
        out_shape=[part] * 2 + [jax.ShapeDtypeStruct((share, panels * w), BF)],
        in_specs=[sm] + [vm] * 11,
        out_specs=[vm] * 3,
        compiler_params=params,
        name="solve",
    )(pos, held, twin, *rights, *late)

    there = y_shift(solved[0], 1), y_shift(solved[1], -1)
    there = y_shift(there[0], 1), y_shift(there[1], -1)
    blocks = [x_ring(solved), x_ring(list(there))]
    m1 = shift(mine, "yl")
    m2 = shift(jnp.stack([mine, m1]), "core")

    def halves(offsets):
        return [half for dyh, dx in offsets for half in blocks[dyh][dx]]

    near = halves(NEAR)

    pos = jnp.stack([z, yl, core, yh, x]).astype(jnp.int32)
    cols = panels * share
    full = jax.ShapeDtypeStruct((cols, 1, 2 * nx * nz * share), F32)
    done, own = pl.pallas_call(
        near_kernel,
        out_shape=(full, jax.ShapeDtypeStruct((panels, share, panels * w), BF)),
        in_specs=[sm] + [vm] * (3 + len(near)),
        out_specs=(vm, vm),
        compiler_params=params,
        name="near",
    )(pos, mine, m1, m2, *near)

    def more(done, offsets):
        found = halves(offsets)
        n = len(offsets)
        return pl.pallas_call(
            functools.partial(more_kernel, offsets),
            out_shape=full,
            in_specs=[sm, hbm] + [vm] * (1 + len(found)),
            out_specs=hbm,
            input_output_aliases={1: 0},
            scratch_shapes=[
                pltpu.VMEM((n, cols, 1, nz * share), F32),
                pltpu.SemaphoreType.DMA((n,)),
            ],
            compiler_params=params,
        )(pos, done, own, *found)

    done = more(done, NEXT)
    return more(done, LAST)


def solution(mesh):
    fine = Mesh(mesh.devices.reshape(2, 2, 2, 4, 8), FAC + COL)
    return jax.shard_map(
        compute,
        mesh=fine,
        in_specs=(
            P(None, FAC, None, None, COL),
            P(None, FAC, None, COL),
            P(None, FAC, None, COL),
            P(),
        ),
        out_specs=P(COL, FAC, None),
        check_vma=False,
    )
```

time: 120 us -> 121 us (level)
  the two profiles are of different devices: /device:TPU:6 before, /device:TPU:1 now
where the time goes in v6:
time: 121 us
  starting transfers between devices  54.7 us (45%)
  waiting for transfers between devices  37.7 us (31%)
  blocking collectives  15.4 us (13%)
  Pallas kernels  8.9 us (7%)
  local copies, waits for them, and re-layouts  3.7 us (3%)
    ppermute x26, starting transfers between devices, shift(): return lax.ppermute(a, axis, [(i, (i + by) % n) for i in range(n)])  42.4 us
    ppermute x26, waiting for transfers between devices, shift(): return lax.ppermute(a, axis, [(i, (i + by) % n) for i in range(n)])  28.9 us
    all_to_all x1, blocking collectives, compute(): got = lax.all_to_all(rows, 'z', 0, 0, tiled=True)  15.4 us
    all_to_all x1, waiting for transfers between devices, compute(): held = lax.all_to_all(got, ('yl', 'yh', 'x'), 0, 0, tiled=True)  7.69 us
    all_to_all x1, starting transfers between devices, compute(): held = lax.all_to_all(got, ('yl', 'yh', 'x'), 0, 0, tiled=True)  6.89 us
    ppermute x4, starting transfers between devices, y_shift(): return lax.ppermute(a, ('yl', 'yh'), pairs)  5.43 us
    pallas_call x2, Pallas kernels, more(): pl.pallas_call(functools.partial(more_kernel, offsets), out_shape=full, i...  4.3 us
    pallas_call x1, Pallas kernels, compute(): pl.pallas_call(near_kernel, out_shape=(full, jax.ShapeDtypeStruct((panels...  3.12 us
  transfers between devices with their start and end apart: 31, of which 13 were waited for; matrix products, arithmetic and copies ran while one was open for 0% of the time, Pallas kernels for 4%

profile of v6, /device:TPU:1, one launch (start us, length us, event | category | flops | bytes accessed | tf_op | source)
XLA Modules:
  0.0 120.8 jit_solution(4134797158050460268)
XLA Ops:
  0.0 0.7 copy-done
  0.7 0.0 copy-done.4
  0.7 0.1 fusion.4
  0.8 2.2 %collective-permute-start = (bf16[4,256]{1,0:T(4,128)(2,1)S(1)}, bf16[4,256]{1,0:T(4,128)(2,1)S(1)}, u32[]{:S(2)}, u32[]{:S(2)}) collective-permute-start(bf16[4,256]{1,0:T(4,128)(2,1)S(1)} %get-tuple-element.20), channel_id=1, source_target_pairs={{0,128},{128,0},{1,129},{129,1},{2,130},{130,2},{3,131},{131,3},{4... | collective-permute-start | bytes 6152 | tf_op jit(solution)/shard_map/ppermute | solution.py:22
  3.0 1.0 collective-permute-done
  4.0 15.4 %all_to_all.10 = bf16[8,32,128]{2,1,0:T(8,128)(2,1)S(1)} all-to-all(bf16[8,32,128]{2,1,0:T(8,128)(2,1)S(1)} %broadcast_in_dim.29), channel_id=1, replica_groups=mesh['yl'=2,'core'=2,'yh'=2,'x'=4,'z'=8] {'z'}, dimensions={0} | all-to-all | bytes 131072 | tf_op jit(solution)/shard_map/all_to_all | solution.py:174
  19.5 1.2 broadcast_in_dim.31
  20.6 6.9 %all-to-all-start.1 = ((bf16[16,256,128]{2,1,0:T(8,128)(2,1)}), bf16[16,256,128]{2,1,0:T(8,128)(2,1)S(1)}, u32[]{:S(2)}, u32[]{:S(2)}) async-start(bf16[16,256,128]{2,1,0:T(8,128)(2,1)} %broadcast_in_dim.31), calls=%async_computation.1 | async-start | bytes 2097152 | tf_op jit(solution)/shard_map/all_to_all | solution.py:178
  27.5 0.1 copy.26
  27.6 3.6 %collective-permute-start.2 = (f32[128,256]{1,0:T(8,128)S(1)}, f32[128,256]{1,0:T(8,128)S(1)}, u32[]{:S(2)}, u32[]{:S(2)}) collective-permute-start(f32[128,256]{1,0:T(8,128)S(1)} %bitcast.76), channel_id=1, source_target_pairs={{0,64},{64,0},{1,65},{65,1},{2,66},{66,2},{3,67},{67,3},{4,68},{68... | collective-permute-start | bytes 393224 | tf_op jit(solution)/shard_map/ppermute | solution.py:22
  31.3 1.0 collective-permute-done.2
  32.3 1.7 %collective-permute-start.3 = (f32[2,32,256]{2,1,0:T(8,128)S(1)}, f32[2,32,256]{2,1,0:T(8,128)S(1)}, u32[]{:S(2)}, u32[]{:S(2)}) collective-permute-start(f32[2,32,256]{2,1,0:T(8,128)S(1)} %fusion.1), channel_id=1, source_target_pairs={{0,128},{128,0},{1,129},{129,1},{2,130},{130,2},{3,131},{131,3},{4... | collective-permute-start | bytes 196616 | tf_op jit(solution)/shard_map/ppermute | solution.py:22
  34.0 7.7 %all-to-all-done.1.own_ref = bf16[16,256,128]{2,1,0:T(8,128)(2,1)S(1)} async-done(((bf16[16,256,128]{2,1,0:T(8,128)(2,1)}), bf16[16,256,128]{2,1,0:T(8,128)(2,1)S(1)}, u32[]{:S(2)}, u32[]{:S(2)}) %all-to-all-start.1) | async-done | bytes 1048608 | tf_op jit(solution)/shard_map/all_to_all | solution.py:178
  41.7 4.4 %collective-permute-start.1 = (bf16[16,256,128]{2,1,0:T(8,128)(2,1)S(1)}, bf16[16,256,128]{2,1,0:T(8,128)(2,1)S(1)}, u32[]{:S(2)}, u32[]{:S(2)}) collective-permute-start(bf16[16,256,128]{2,1,0:T(8,128)(2,1)S(1)} %all-to-all-done.1.own_ref), channel_id=1, source_target_pairs={{0,64},{64,0},{1,65},{65,1},{2,66},{66,2},{3,67},{67,3},{4,68},{68... | collective-permute-start | bytes 3145736 | tf_op jit(solution)/shard_map/ppermute | solution.py:22
  46.1 0.0 collective-permute-done.3
  46.1 0.5 collective-permute-start.7
  46.6 2.3 %collective-permute-start.4 = (f32[2,2,32,256]{3,2,1,0:T(8,128)S(1)}, f32[2,2,32,256]{3,2,1,0:T(8,128)S(1)}, u32[]{:S(2)}, u32[]{:S(2)}) collective-permute-start(f32[2,2,32,256]{3,2,1,0:T(8,128)S(1)} %pad_maximum_fusion.refs_0_), channel_id=1, source_target_pairs={{0,7},{1,0},{2,1},{3,2},{4,3},{5,4},{6,5},{7,6},{8,15},{9,8},{10,9... | collective-permute-start | bytes 393224 | tf_op jit(solution)/shard_map/ppermute | solution.py:22
  48.9 3.6 %collective-permute-done.7.refs_6_ = f32[2,2,32,256]{3,2,1,0:T(8,128)S(1)} collective-permute-done((f32[2,2,32,256]{3,2,1,0:T(8,128)S(1)}, f32[2,2,32,256]{3,2,1,0:T(8,128)S(1)}, u32[]{:S(2)}, u32[]{:S(2)}) %collective-permute-start.7) | collective-permute-done | bytes 131104 | tf_op jit(solution)/shard_map/ppermute | solution.py:22
  52.5 0.0 collective-permute-start.8
  52.5 0.0 collective-permute-done.4.refs_1_
  52.5 2.7 %collective-permute-start.5 = (f32[2,2,32,256]{3,2,1,0:T(8,128)S(1)}, f32[2,2,32,256]{3,2,1,0:T(8,128)S(1)}, u32[]{:S(2)}, u32[]{:S(2)}) collective-permute-start(f32[2,2,32,256]{3,2,1,0:T(8,128)S(1)} %collective-permute-done.4.refs_1_), channel_id=1, source_target_pairs={{0,7},{1,0},{2,1},{3,2},{4,3},{5,4},{6,5},{7,6},{8,15},{9,8},{10,9... | collective-permute-start | bytes 393224 | tf_op jit(solution)/shard_map/ppermute | solution.py:22
  55.1 2.7 %collective-permute-done.8.refs_5_ = f32[2,2,32,256]{3,2,1,0:T(8,128)S(1)} collective-permute-done((f32[2,2,32,256]{3,2,1,0:T(8,128)S(1)}, f32[2,2,32,256]{3,2,1,0:T(8,128)S(1)}, u32[]{:S(2)}, u32[]{:S(2)}) %collective-permute-start.8) | collective-permute-done | bytes 131104 | tf_op jit(solution)/shard_map/ppermute | solution.py:22
  57.9 0.0 collective-permute-start.9
  57.9 0.0 collective-permute-done.5.refs_2_
  57.9 2.7 %collective-permute-start.6 = (f32[2,2,32,256]{3,2,1,0:T(8,128)S(1)}, f32[2,2,32,256]{3,2,1,0:T(8,128)S(1)}, u32[]{:S(2)}, u32[]{:S(2)}) collective-permute-start(f32[2,2,32,256]{3,2,1,0:T(8,128)S(1)} %collective-permute-done.5.refs_2_), channel_id=1, source_target_pairs={{0,7},{1,0},{2,1},{3,2},{4,3},{5,4},{6,5},{7,6},{8,15},{9,8},{10,9... | collective-permute-start | bytes 393224 | tf_op jit(solution)/shard_map/ppermute | solution.py:22
  60.5 2.3 %collective-permute-done.9.refs_4_ = f32[2,2,32,256]{3,2,1,0:T(8,128)S(1)} collective-permute-done((f32[2,2,32,256]{3,2,1,0:T(8,128)S(1)}, f32[2,2,32,256]{3,2,1,0:T(8,128)S(1)}, u32[]{:S(2)}, u32[]{:S(2)}) %collective-permute-start.9) | collective-permute-done | bytes 131104 | tf_op jit(solution)/shard_map/ppermute | solution.py:22
  62.9 0.0 collective-permute-start.10
  62.9 2.7 %collective-permute-start.11 = (f32[2,32,256]{2,1,0:T(8,128)S(1)}, f32[2,32,256]{2,1,0:T(8,128)S(1)}, u32[]{:S(2)}, u32[]{:S(2)}) collective-permute-start(f32[2,32,256]{2,1,0:T(8,128)S(1)} %slice_bitcast_fusion), channel_id=1, source_target_pairs={{0,7},{1,0},{2,1},{3,2},{4,3},{5,4},{6,5},{7,6},{8,15},{9,8},{10,9... | collective-permute-start | bytes 196616 | tf_op jit(solution)/shard_map/ppermute | solution.py:22
  65.7 1.6 %collective-permute-done.10.refs_7_ = f32[2,32,256]{2,1,0:T(8,128)S(1)} collective-permute-done((f32[2,32,256]{2,1,0:T(8,128)S(1)}, f32[2,32,256]{2,1,0:T(8,128)S(1)}, u32[]{:S(2)}, u32[]{:S(2)}) %collective-permute-start.10) | collective-permute-done | bytes 65568 | tf_op jit(solution)/shard_map/ppermute | solution.py:22
  67.2 0.0 collective-permute-done.11.refs_8_
  67.2 0.0 collective-permute-done.1.twin_ref
  67.2 1.5 %solve.1 = (bf16[4,32,1024]{2,1,0:T(8,128)(2,1)S(1)}, bf16[4,32,1024]{2,1,0:T(8,128)(2,1)S(1)}, bf16[32,1024]{1,0:T(8,128)(2,1)S(1)}) custom-call(s32[1]{0:T(128)} %bitcast.2.pos_ref, bf16[16,256,128]{2,1,0:T(8,128)(2,1)S(1)} %all-to-all-done.1.own_ref, bf16[16,256,128]{2,1,0:T(8,128)(2,1)S(1)} %collective-permute-done.1.twin_ref, ...), custom_call_target="tpu_custom_call" | custom-call | tf_op jit(solution)/shard_map/solve/pallas_call | solution.py:204
  68.7 0.3 collective-permute-start.20
  69.0 2.5 %collective-permute-start.22 = (bf16[4,32,1024]{2,1,0:T(8,128)(2,1)S(1)}, bf16[4,32,1024]{2,1,0:T(8,128)(2,1)S(1)}, u32[]{:S(2)}, u32[]{:S(2)}) collective-permute-start(bf16[4,32,1024]{2,1,0:T(8,128)(2,1)S(1)} %get-tuple-element.12.refs_1_), channel_id=1, source_target_pairs={{0,160},{32,128},{128,0},{160,32},{1,161},{33,129},{129,1},{161,33... | collective-permute-start | bytes 786440 | tf_op jit(solution)/shard_map/ppermute | solution.py:140
  71.5 0.0 collective-permute-start.12
  71.5 0.7 collective-permute-start.16
  72.2 1.9 %collective-permute-start.15 = (bf16[4,32,1024]{2,1,0:T(8,128)(2,1)S(1)}, bf16[4,32,1024]{2,1,0:T(8,128)(2,1)S(1)}, u32[]{:S(2)}, u32[]{:S(2)}) collective-permute-start(bf16[4,32,1024]{2,1,0:T(8,128)(2,1)S(1)} %get-tuple-element.12.refs_1_), channel_id=1, source_target_pairs={{0,24},{8,0},{16,8},{24,16},{1,25},{9,1},{17,9},{25,17},{2,26},{10... | collective-permute-start | bytes 786440 | tf_op jit(solution)/shard_map/ppermute | solution.py:22
  74.2 1.1 collective-permute-done.20
  75.2 0.4 collective-permute-start.21
  75.6 0.0 collective-permute-done.22
  75.6 2.3 %collective-permute-start.23 = (bf16[4,32,1024]{2,1,0:T(8,128)(2,1)S(1)}, bf16[4,32,1024]{2,1,0:T(8,128)(2,1)S(1)}, u32[]{:S(2)}, u32[]{:S(2)}) collective-permute-start(bf16[4,32,1024]{2,1,0:T(8,128)(2,1)S(1)} %collective-permute-done.22), channel_id=1, source_target_pairs={{0,160},{32,128},{128,0},{160,32},{1,161},{33,129},{129,1},{161,33... | collective-permute-start | bytes 786440 | tf_op jit(solution)/shard_map/ppermute | solution.py:140
  77.9 6.9 %collective-permute-start.13 = (bf16[2,32,1024]{2,1,0:T(8,128)(2,1)S(1)}, bf16[2,32,1024]{2,1,0:T(8,128)(2,1)S(1)}, u32[]{:S(2)}, u32[]{:S(2)}) collective-permute-start(bf16[2,32,1024]{2,1,0:T(8,128)(2,1)S(1)} %pad_maximum_fusion.1), channel_id=1, source_target_pairs={{0,64},{64,0},{1,65},{65,1},{2,66},{66,2},{3,67},{67,3},{4,68},{68... | collective-permute-start | bytes 393224 | tf_op jit(solution)/shard_map/ppermute | solution.py:22
  84.9 1.0 collective-permute-done.13.m2
  85.9 0.7 copy-done.1
  86.5 1.2 collective-permute-start.14
  87.7 0.0 collective-permute-done.16.refs_4_
  87.7 0.3 collective-permute-start.17
  88.0 0.7 collective-permute-start.18
  88.7 0.4 collective-permute-start.26
  89.1 2.3 %collective-permute-start.25 = (bf16[4,32,1024]{2,1,0:T(8,128)(2,1)S(1)}, bf16[4,32,1024]{2,1,0:T(8,128)(2,1)S(1)}, u32[]{:S(2)}, u32[]{:S(2)}) collective-permute-start(bf16[4,32,1024]{2,1,0:T(8,128)(2,1)S(1)} %collective-permute-done.23.refs_9_), channel_id=1, source_target_pairs={{0,24},{8,0},{16,8},{24,16},{1,25},{9,1},{17,9},{25,17},{2,26},{10... | collective-permute-start | bytes 786440 | tf_op jit(solution)/shard_map/ppermute | solution.py:22
  91.4 2.6 %collective-permute-done.14.refs_2_ = bf16[4,32,1024]{2,1,0:T(8,128)(2,1)S(1)} collective-permute-done((bf16[4,32,1024]{2,1,0:T(8,128)(2,1)S(1)}, bf16[4,32,1024]{2,1,0:T(8,128)(2,1)S(1)}, u32[]{:S(2)}, u32[]{:S(2)}) %collective-permute-start.14) | collective-permute-done | bytes 262176 | tf_op jit(solution)/shard_map/ppermute | solution.py:22
  94.0 2.4 %collective-permute-start.19 = (bf16[4,32,1024]{2,1,0:T(8,128)(2,1)S(1)}, bf16[4,32,1024]{2,1,0:T(8,128)(2,1)}, u32[]{:S(2)}, u32[]{:S(2)}) collective-permute-start(bf16[4,32,1024]{2,1,0:T(8,128)(2,1)S(1)} %collective-permute-done.15.refs_3_), channel_id=1, source_target_pairs={{0,24},{8,0},{16,8},{24,16},{1,25},{9,1},{17,9},{25,17},{2,26},{10... | collective-permute-start | bytes 786440 | tf_op jit(solution)/shard_map/ppermute | solution.py:22
  96.4 0.0 collective-permute-done.17.refs_5_
  96.4 0.0 collective-permute-start.24
  96.5 5.3 %collective-permute-done.18.refs_6_ = bf16[4,32,1024]{2,1,0:T(8,128)(2,1)S(1)} collective-permute-done((bf16[4,32,1024]{2,1,0:T(8,128)(2,1)S(1)}, bf16[4,32,1024]{2,1,0:T(8,128)(2,1)S(1)}, u32[]{:S(2)}, u32[]{:S(2)}) %collective-permute-start.18) | collective-permute-done | bytes 262176 | tf_op jit(solution)/shard_map/ppermute | solution.py:22
  101.8 0.0 collective-permute-start.27
  101.8 5.6 %collective-permute-done.26.refs_2_ = bf16[4,32,1024]{2,1,0:T(8,128)(2,1)S(1)} collective-permute-done((bf16[4,32,1024]{2,1,0:T(8,128)(2,1)S(1)}, bf16[4,32,1024]{2,1,0:T(8,128)(2,1)S(1)}, u32[]{:S(2)}, u32[]{:S(2)}) %collective-permute-start.26) | collective-permute-done | bytes 262176 | tf_op jit(solution)/shard_map/ppermute | solution.py:22
  107.4 2.7 %collective-permute-start.29 = (bf16[4,32,1024]{2,1,0:T(8,128)(2,1)S(1)}, bf16[4,32,1024]{2,1,0:T(8,128)(2,1)}, u32[]{:S(2)}, u32[]{:S(2)}) collective-permute-start(bf16[4,32,1024]{2,1,0:T(8,128)(2,1)S(1)} %collective-permute-done.25.refs_1_), channel_id=1, source_target_pairs={{0,24},{8,0},{16,8},{24,16},{1,25},{9,1},{17,9},{25,17},{2,26},{10... | collective-permute-start | bytes 786440 | tf_op jit(solution)/shard_map/ppermute | solution.py:22
  110.1 0.1 stack.65.pos_ref
  110.2 0.9 copy-done.2
  111.1 3.1 %near.1 = (f32[128,1,2048]{2,1,0:T(1,128)}, bf16[4,32,1024]{2,1,0:T(8,128)(2,1)S(1)}) custom-call(s32[5]{0:T(128)S(1)} %stack.65.pos_ref, bf16[32,1024]{1,0:T(8,128)(2,1)S(1)} %get-tuple-element.10.m0, bf16[32,1024]{1,0:T(8,128)(2,1)S(1)} %collective-permute-done.12.m1, bf16[2,32,1024]{2,1,0:T(8,128)(2,1)S(1)} %copy-done.2, ...), custom_call_target="tpu_custom_call" | custom-call | tf_op jit(solution)/shard_map/near/pallas_call | solution.py:227
  114.2 2.3 %shard_map.46.before = f32[128,1,2048]{2,1,0:T(1,128)} custom-call(s32[5]{0:T(128)S(1)} %stack.65.pos_ref, f32[128,1,2048]{2,1,0:T(1,128)} %get-tuple-element.13.before, bf16[4,32,1024]{2,1,0:T(8,128)(2,1)S(1)} %get-tuple-element.14.own, bf16[4,32,1024]{2,1,0:T(8,128)(2,1)S(1)} %collective-permute-done.24.refs_0_, ...), custom_call_target="tpu_custom_call", output_to_operand_aliasing={{}: (1, {})} | custom-call | tf_op jit(solution)/shard_map/pallas_call | solution.py:239
  116.5 2.1 %collective-permute-done.28.refs_0_ = bf16[4,32,1024]{2,1,0:T(8,128)(2,1)S(1)} collective-permute-done((bf16[4,32,1024]{2,1,0:T(8,128)(2,1)S(1)}, bf16[4,32,1024]{2,1,0:T(8,128)(2,1)S(1)}, u32[]{:S(2)}, u32[]{:S(2)}) %collective-permute-start.28) | collective-permute-done | bytes 262176 | tf_op jit(solution)/shard_map/ppermute | solution.py:22
  118.6 2.0 %shard_map.47 = f32[128,1,2048]{2,1,0:T(1,128)} custom-call(s32[5]{0:T(128)S(1)} %stack.65.pos_ref, f32[128,1,2048]{2,1,0:T(1,128)} %shard_map.46.before, bf16[4,32,1024]{2,1,0:T(8,128)(2,1)S(1)} %get-tuple-element.14.own, bf16[4,32,1024]{2,1,0:T(8,128)(2,1)S(1)} %collective-permute-done.28.refs_0_, ...), custom_call_target="tpu_custom_call", output_to_operand_aliasing={{}: (1, {})} | custom-call | tf_op jit(solution)/shard_map/pallas_call | solution.py:239
  (35 shorter events, 0.2 us)
Async XLA Ops:
  0.0 0.7 copy-start
  0.0 0.7 copy-start.4
  0.8 2.2 %copy-start.5 = (f32[1,1,256,4]{2,3,1,0:T(4,128)S(1)}, f32[1,1,256,4]{2,3,1,0:T(4,128)}, u32[]{:S(2)}) copy-start(f32[1,1,256,4]{2,3,1,0:T(4,128)} %param.5) | copy-start | bytes 12292
  0.8 3.2 %collective-permute-start = (bf16[4,256]{1,0:T(4,128)(2,1)S(1)}, bf16[4,256]{1,0:T(4,128)(2,1)S(1)}, u32[]{:S(2)}, u32[]{:S(2)}) collective-permute-start(bf16[4,256]{1,0:T(4,128)(2,1)S(1)} %get-tuple-element.20), channel_id=1, source_target_pairs={{0,128},{128,0},{1,129},{129,1},{2,130},{130,2},{3,131},{131,3},{4... | collective-permute-start | bytes 6152 | tf_op jit(solution)/shard_map/ppermute | solution.py:22
  20.6 6.9 %copy-start.3 = (f32[1,1,256,128]{3,2,1,0:T(8,128)S(1)}, f32[1,1,256,128]{3,2,1,0:T(8,128)}, u32[]{:S(2)}) copy-start(f32[1,1,256,128]{3,2,1,0:T(8,128)} %param.6) | copy-start | bytes 393220
  20.6 21.1 %all-to-all-start.1 = ((bf16[16,256,128]{2,1,0:T(8,128)(2,1)}), bf16[16,256,128]{2,1,0:T(8,128)(2,1)S(1)}, u32[]{:S(2)}, u32[]{:S(2)}) async-start(bf16[16,256,128]{2,1,0:T(8,128)(2,1)} %broadcast_in_dim.31), calls=%async_computation.1 | async-start | bytes 2097152 | tf_op jit(solution)/shard_map/all_to_all | solution.py:178
  27.6 4.6 %collective-permute-start.2 = (f32[128,256]{1,0:T(8,128)S(1)}, f32[128,256]{1,0:T(8,128)S(1)}, u32[]{:S(2)}, u32[]{:S(2)}) collective-permute-start(f32[128,256]{1,0:T(8,128)S(1)} %bitcast.76), channel_id=1, source_target_pairs={{0,64},{64,0},{1,65},{65,1},{2,66},{66,2},{3,67},{67,3},{4,68},{68... | collective-permute-start | bytes 393224 | tf_op jit(solution)/shard_map/ppermute | solution.py:22
  32.3 13.8 %collective-permute-start.3 = (f32[2,32,256]{2,1,0:T(8,128)S(1)}, f32[2,32,256]{2,1,0:T(8,128)S(1)}, u32[]{:S(2)}, u32[]{:S(2)}) collective-permute-start(f32[2,32,256]{2,1,0:T(8,128)S(1)} %fusion.1), channel_id=1, source_target_pairs={{0,128},{128,0},{1,129},{129,1},{2,130},{130,2},{3,131},{131,3},{4... | collective-permute-start | bytes 196616 | tf_op jit(solution)/shard_map/ppermute | solution.py:22
  41.7 25.5 %collective-permute-start.1 = (bf16[16,256,128]{2,1,0:T(8,128)(2,1)S(1)}, bf16[16,256,128]{2,1,0:T(8,128)(2,1)S(1)}, u32[]{:S(2)}, u32[]{:S(2)}) collective-permute-start(bf16[16,256,128]{2,1,0:T(8,128)(2,1)S(1)} %all-to-all-done.1.own_ref), channel_id=1, source_target_pairs={{0,64},{64,0},{1,65},{65,1},{2,66},{66,2},{3,67},{67,3},{4,68},{68... | collective-permute-start | bytes 3145736 | tf_op jit(solution)/shard_map/ppermute | solution.py:22
  46.1 6.3 %collective-permute-start.7 = (f32[2,2,32,256]{3,2,1,0:T(8,128)S(1)}, f32[2,2,32,256]{3,2,1,0:T(8,128)S(1)}, u32[]{:S(2)}, u32[]{:S(2)}) collective-permute-start(f32[2,2,32,256]{3,2,1,0:T(8,128)S(1)} %pad_maximum_fusion.refs_0_), channel_id=1, source_target_pairs={{0,1},{1,2},{2,3},{3,4},{4,5},{5,6},{6,7},{7,0},{8,9},{9,10},{10,1... | collective-permute-start | bytes 393224 | tf_op jit(solution)/shard_map/ppermute | solution.py:22
  46.6 5.9 %collective-permute-start.4 = (f32[2,2,32,256]{3,2,1,0:T(8,128)S(1)}, f32[2,2,32,256]{3,2,1,0:T(8,128)S(1)}, u32[]{:S(2)}, u32[]{:S(2)}) collective-permute-start(f32[2,2,32,256]{3,2,1,0:T(8,128)S(1)} %pad_maximum_fusion.refs_0_), channel_id=1, source_target_pairs={{0,7},{1,0},{2,1},{3,2},{4,3},{5,4},{6,5},{7,6},{8,15},{9,8},{10,9... | collective-permute-start | bytes 393224 | tf_op jit(solution)/shard_map/ppermute | solution.py:22
  52.5 5.4 %collective-permute-start.8 = (f32[2,2,32,256]{3,2,1,0:T(8,128)S(1)}, f32[2,2,32,256]{3,2,1,0:T(8,128)S(1)}, u32[]{:S(2)}, u32[]{:S(2)}) collective-permute-start(f32[2,2,32,256]{3,2,1,0:T(8,128)S(1)} %collective-permute-done.7.refs_6_), channel_id=1, source_target_pairs={{0,1},{1,2},{2,3},{3,4},{4,5},{5,6},{6,7},{7,0},{8,9},{9,10},{10,1... | collective-permute-start | bytes 393224 | tf_op jit(solution)/shard_map/ppermute | solution.py:22
  52.5 5.4 %collective-permute-start.5 = (f32[2,2,32,256]{3,2,1,0:T(8,128)S(1)}, f32[2,2,32,256]{3,2,1,0:T(8,128)S(1)}, u32[]{:S(2)}, u32[]{:S(2)}) collective-permute-start(f32[2,2,32,256]{3,2,1,0:T(8,128)S(1)} %collective-permute-done.4.refs_1_), channel_id=1, source_target_pairs={{0,7},{1,0},{2,1},{3,2},{4,3},{5,4},{6,5},{7,6},{8,15},{9,8},{10,9... | collective-permute-start | bytes 393224 | tf_op jit(solution)/shard_map/ppermute | solution.py:22
  57.9 5.0 %collective-permute-start.9 = (f32[2,2,32,256]{3,2,1,0:T(8,128)S(1)}, f32[2,2,32,256]{3,2,1,0:T(8,128)S(1)}, u32[]{:S(2)}, u32[]{:S(2)}) collective-permute-start(f32[2,2,32,256]{3,2,1,0:T(8,128)S(1)} %collective-permute-done.8.refs_5_), channel_id=1, source_target_pairs={{0,1},{1,2},{2,3},{3,4},{4,5},{5,6},{6,7},{7,0},{8,9},{9,10},{10,1... | collective-permute-start | bytes 393224 | tf_op jit(solution)/shard_map/ppermute | solution.py:22
  57.9 5.0 %collective-permute-start.6 = (f32[2,2,32,256]{3,2,1,0:T(8,128)S(1)}, f32[2,2,32,256]{3,2,1,0:T(8,128)S(1)}, u32[]{:S(2)}, u32[]{:S(2)}) collective-permute-start(f32[2,2,32,256]{3,2,1,0:T(8,128)S(1)} %collective-permute-done.5.refs_2_), channel_id=1, source_target_pairs={{0,7},{1,0},{2,1},{3,2},{4,3},{5,4},{6,5},{7,6},{8,15},{9,8},{10,9... | collective-permute-start | bytes 393224 | tf_op jit(solution)/shard_map/ppermute | solution.py:22
  62.9 4.3 %collective-permute-start.10 = (f32[2,32,256]{2,1,0:T(8,128)S(1)}, f32[2,32,256]{2,1,0:T(8,128)S(1)}, u32[]{:S(2)}, u32[]{:S(2)}) collective-permute-start(f32[2,32,256]{2,1,0:T(8,128)S(1)} %slice_bitcast_fusion.1), channel_id=1, source_target_pairs={{0,1},{1,2},{2,3},{3,4},{4,5},{5,6},{6,7},{7,0},{8,9},{9,10},{10,1... | collective-permute-start | bytes 196616 | tf_op jit(solution)/shard_map/ppermute | solution.py:22
  62.9 4.3 %collective-permute-start.11 = (f32[2,32,256]{2,1,0:T(8,128)S(1)}, f32[2,32,256]{2,1,0:T(8,128)S(1)}, u32[]{:S(2)}, u32[]{:S(2)}) collective-permute-start(f32[2,32,256]{2,1,0:T(8,128)S(1)} %slice_bitcast_fusion), channel_id=1, source_target_pairs={{0,7},{1,0},{2,1},{3,2},{4,3},{5,4},{6,5},{7,6},{8,15},{9,8},{10,9... | collective-permute-start | bytes 196616 | tf_op jit(solution)/shard_map/ppermute | solution.py:22
  68.7 6.5 %collective-permute-start.20 = (bf16[4,32,1024]{2,1,0:T(8,128)(2,1)S(1)}, bf16[4,32,1024]{2,1,0:T(8,128)(2,1)S(1)}, u32[]{:S(2)}, u32[]{:S(2)}) collective-permute-start(bf16[4,32,1024]{2,1,0:T(8,128)(2,1)S(1)} %get-tuple-element.11.refs_0_), channel_id=1, source_target_pairs={{0,128},{32,160},{128,32},{160,0},{1,129},{33,161},{129,33},{161,1... | collective-permute-start | bytes 786440 | tf_op jit(solution)/shard_map/ppermute | solution.py:140
  69.0 6.6 %collective-permute-start.22 = (bf16[4,32,1024]{2,1,0:T(8,128)(2,1)S(1)}, bf16[4,32,1024]{2,1,0:T(8,128)(2,1)S(1)}, u32[]{:S(2)}, u32[]{:S(2)}) collective-permute-start(bf16[4,32,1024]{2,1,0:T(8,128)(2,1)S(1)} %get-tuple-element.12.refs_1_), channel_id=1, source_target_pairs={{0,160},{32,128},{128,0},{160,32},{1,161},{33,129},{129,1},{161,33... | collective-permute-start | bytes 786440 | tf_op jit(solution)/shard_map/ppermute | solution.py:140
  71.5 6.4 %collective-permute-start.12 = (bf16[32,1024]{1,0:T(8,128)(2,1)S(1)}, bf16[32,1024]{1,0:T(8,128)(2,1)S(1)}, u32[]{:S(2)}, u32[]{:S(2)}) collective-permute-start(bf16[32,1024]{1,0:T(8,128)(2,1)S(1)} %get-tuple-element.10.m0), channel_id=1, source_target_pairs={{0,128},{128,0},{1,129},{129,1},{2,130},{130,2},{3,131},{131,3},{4... | collective-permute-start | bytes 196616 | tf_op jit(solution)/shard_map/ppermute | solution.py:22
  71.5 16.3 %collective-permute-start.16 = (bf16[4,32,1024]{2,1,0:T(8,128)(2,1)S(1)}, bf16[4,32,1024]{2,1,0:T(8,128)(2,1)S(1)}, u32[]{:S(2)}, u32[]{:S(2)}) collective-permute-start(bf16[4,32,1024]{2,1,0:T(8,128)(2,1)S(1)} %get-tuple-element.11.refs_0_), channel_id=1, source_target_pairs={{0,8},{8,16},{16,24},{24,0},{1,9},{9,17},{17,25},{25,1},{2,10},{10... | collective-permute-start | bytes 786440 | tf_op jit(solution)/shard_map/ppermute | solution.py:22
  72.2 15.8 %collective-permute-start.15 = (bf16[4,32,1024]{2,1,0:T(8,128)(2,1)S(1)}, bf16[4,32,1024]{2,1,0:T(8,128)(2,1)S(1)}, u32[]{:S(2)}, u32[]{:S(2)}) collective-permute-start(bf16[4,32,1024]{2,1,0:T(8,128)(2,1)S(1)} %get-tuple-element.12.refs_1_), channel_id=1, source_target_pairs={{0,24},{8,0},{16,8},{24,16},{1,25},{9,1},{17,9},{25,17},{2,26},{10... | collective-permute-start | bytes 786440 | tf_op jit(solution)/shard_map/ppermute | solution.py:22
  75.2 13.5 %collective-permute-start.21 = (bf16[4,32,1024]{2,1,0:T(8,128)(2,1)S(1)}, bf16[4,32,1024]{2,1,0:T(8,128)(2,1)S(1)}, u32[]{:S(2)}, u32[]{:S(2)}) collective-permute-start(bf16[4,32,1024]{2,1,0:T(8,128)(2,1)S(1)} %collective-permute-done.20), channel_id=1, source_target_pairs={{0,128},{32,160},{128,32},{160,0},{1,129},{33,161},{129,33},{161,1... | collective-permute-start | bytes 786440 | tf_op jit(solution)/shard_map/ppermute | solution.py:140
  75.6 13.5 %collective-permute-start.23 = (bf16[4,32,1024]{2,1,0:T(8,128)(2,1)S(1)}, bf16[4,32,1024]{2,1,0:T(8,128)(2,1)S(1)}, u32[]{:S(2)}, u32[]{:S(2)}) collective-permute-start(bf16[4,32,1024]{2,1,0:T(8,128)(2,1)S(1)} %collective-permute-done.22), channel_id=1, source_target_pairs={{0,160},{32,128},{128,0},{160,32},{1,161},{33,129},{129,1},{161,33... | collective-permute-start | bytes 786440 | tf_op jit(solution)/shard_map/ppermute | solution.py:140
  77.9 7.9 %collective-permute-start.13 = (bf16[2,32,1024]{2,1,0:T(8,128)(2,1)S(1)}, bf16[2,32,1024]{2,1,0:T(8,128)(2,1)S(1)}, u32[]{:S(2)}, u32[]{:S(2)}) collective-permute-start(bf16[2,32,1024]{2,1,0:T(8,128)(2,1)S(1)} %pad_maximum_fusion.1), channel_id=1, source_target_pairs={{0,64},{64,0},{1,65},{65,1},{2,66},{66,2},{3,67},{67,3},{4,68},{68... | collective-permute-start | bytes 393224 | tf_op jit(solution)/shard_map/ppermute | solution.py:22
  85.9 0.7 copy-start.1
  86.5 7.5 %collective-permute-start.14 = (bf16[4,32,1024]{2,1,0:T(8,128)(2,1)S(1)}, bf16[4,32,1024]{2,1,0:T(8,128)(2,1)S(1)}, u32[]{:S(2)}, u32[]{:S(2)}) collective-permute-start(bf16[4,32,1024]{2,1,0:T(8,128)(2,1)S(1)} %get-tuple-element.11.refs_0_), channel_id=1, source_target_pairs={{0,24},{8,0},{16,8},{24,16},{1,25},{9,1},{17,9},{25,17},{2,26},{10... | collective-permute-start | bytes 786440 | tf_op jit(solution)/shard_map/ppermute | solution.py:22
  87.7 8.7 %collective-permute-start.17 = (bf16[4,32,1024]{2,1,0:T(8,128)(2,1)S(1)}, bf16[4,32,1024]{2,1,0:T(8,128)(2,1)S(1)}, u32[]{:S(2)}, u32[]{:S(2)}) collective-permute-start(bf16[4,32,1024]{2,1,0:T(8,128)(2,1)S(1)} %get-tuple-element.12.refs_1_), channel_id=1, source_target_pairs={{0,8},{8,16},{16,24},{24,0},{1,9},{9,17},{17,25},{25,1},{2,10},{10... | collective-permute-start | bytes 786440 | tf_op jit(solution)/shard_map/ppermute | solution.py:22
  88.0 13.8 %collective-permute-start.18 = (bf16[4,32,1024]{2,1,0:T(8,128)(2,1)S(1)}, bf16[4,32,1024]{2,1,0:T(8,128)(2,1)S(1)}, u32[]{:S(2)}, u32[]{:S(2)}) collective-permute-start(bf16[4,32,1024]{2,1,0:T(8,128)(2,1)S(1)} %collective-permute-done.16.refs_4_), channel_id=1, source_target_pairs={{0,8},{8,16},{16,24},{24,0},{1,9},{9,17},{17,25},{25,1},{2,10},{10... | collective-permute-start | bytes 786440 | tf_op jit(solution)/shard_map/ppermute | solution.py:22
  88.7 18.7 %collective-permute-start.26 = (bf16[4,32,1024]{2,1,0:T(8,128)(2,1)S(1)}, bf16[4,32,1024]{2,1,0:T(8,128)(2,1)S(1)}, u32[]{:S(2)}, u32[]{:S(2)}) collective-permute-start(bf16[4,32,1024]{2,1,0:T(8,128)(2,1)S(1)} %collective-permute-done.21.refs_8_), channel_id=1, source_target_pairs={{0,8},{8,16},{16,24},{24,0},{1,9},{9,17},{17,25},{25,1},{2,10},{10... | collective-permute-start | bytes 786440 | tf_op jit(solution)/shard_map/ppermute | solution.py:22
  89.1 18.3 %collective-permute-start.25 = (bf16[4,32,1024]{2,1,0:T(8,128)(2,1)S(1)}, bf16[4,32,1024]{2,1,0:T(8,128)(2,1)S(1)}, u32[]{:S(2)}, u32[]{:S(2)}) collective-permute-start(bf16[4,32,1024]{2,1,0:T(8,128)(2,1)S(1)} %collective-permute-done.23.refs_9_), channel_id=1, source_target_pairs={{0,24},{8,0},{16,8},{24,16},{1,25},{9,1},{17,9},{25,17},{2,26},{10... | collective-permute-start | bytes 786440 | tf_op jit(solution)/shard_map/ppermute | solution.py:22
  94.0 16.1 %collective-permute-start.19 = (bf16[4,32,1024]{2,1,0:T(8,128)(2,1)S(1)}, bf16[4,32,1024]{2,1,0:T(8,128)(2,1)}, u32[]{:S(2)}, u32[]{:S(2)}) collective-permute-start(bf16[4,32,1024]{2,1,0:T(8,128)(2,1)S(1)} %collective-permute-done.15.refs_3_), channel_id=1, source_target_pairs={{0,24},{8,0},{16,8},{24,16},{1,25},{9,1},{17,9},{25,17},{2,26},{10... | collective-permute-start | bytes 786440 | tf_op jit(solution)/shard_map/ppermute | solution.py:22
  96.4 17.8 %collective-permute-start.24 = (bf16[4,32,1024]{2,1,0:T(8,128)(2,1)S(1)}, bf16[4,32,1024]{2,1,0:T(8,128)(2,1)S(1)}, u32[]{:S(2)}, u32[]{:S(2)}) collective-permute-start(bf16[4,32,1024]{2,1,0:T(8,128)(2,1)S(1)} %collective-permute-done.21.refs_8_), channel_id=1, source_target_pairs={{0,24},{8,0},{16,8},{24,16},{1,25},{9,1},{17,9},{25,17},{2,26},{10... | collective-permute-start | bytes 786440 | tf_op jit(solution)/shard_map/ppermute | solution.py:22
  101.8 12.4 %collective-permute-start.27 = (bf16[4,32,1024]{2,1,0:T(8,128)(2,1)S(1)}, bf16[4,32,1024]{2,1,0:T(8,128)(2,1)}, u32[]{:S(2)}, u32[]{:S(2)}) collective-permute-start(bf16[4,32,1024]{2,1,0:T(8,128)(2,1)S(1)} %collective-permute-done.23.refs_9_), channel_id=1, source_target_pairs={{0,8},{8,16},{16,24},{24,0},{1,9},{9,17},{17,25},{25,1},{2,10},{10... | collective-permute-start | bytes 786440 | tf_op jit(solution)/shard_map/ppermute | solution.py:22
  107.4 11.2 %collective-permute-start.28 = (bf16[4,32,1024]{2,1,0:T(8,128)(2,1)S(1)}, bf16[4,32,1024]{2,1,0:T(8,128)(2,1)S(1)}, u32[]{:S(2)}, u32[]{:S(2)}) collective-permute-start(bf16[4,32,1024]{2,1,0:T(8,128)(2,1)S(1)} %collective-permute-done.26.refs_2_), channel_id=1, source_target_pairs={{0,8},{8,16},{16,24},{24,0},{1,9},{9,17},{17,25},{25,1},{2,10},{10... | collective-permute-start | bytes 786440 | tf_op jit(solution)/shard_map/ppermute | solution.py:22
  107.4 11.2 %collective-permute-start.29 = (bf16[4,32,1024]{2,1,0:T(8,128)(2,1)S(1)}, bf16[4,32,1024]{2,1,0:T(8,128)(2,1)}, u32[]{:S(2)}, u32[]{:S(2)}) collective-permute-start(bf16[4,32,1024]{2,1,0:T(8,128)(2,1)S(1)} %collective-permute-done.25.refs_1_), channel_id=1, source_target_pairs={{0,24},{8,0},{16,8},{24,16},{1,25},{9,1},{17,9},{25,17},{2,26},{10... | collective-permute-start | bytes 786440 | tf_op jit(solution)/shard_map/ppermute | solution.py:22
  110.2 0.9 copy-start.2

commit v7 on v6

--- a/solution.py
+++ b/solution.py
@@ -37,7 +37,7 @@
 
 
 def solve_kernel(pos_ref, own_ref, twin_ref, *refs):
-    rights, late, outs = refs[:7], refs[7:9], refs[9:]
+    rights, late, outs = refs[:7], refs[7], refs[8:]
     peers, _, lanes = own_ref.shape
     half = peers // 2
     share, w = rights[0].shape[2:]
@@ -51,7 +51,7 @@
 
     def right(yl, core):
         rows = [b[yl, core] for b in rights]
-        rows.insert(4, late[yl][core])
+        rows.insert(4, late[yl, core])
         return jnp.concatenate(rows, axis=0)
 
     def factor(p, q):
@@ -192,7 +192,7 @@
     for _ in range(1, 4):
         ups.append(shift(ups[-1], "z", 1))
         downs.append(shift(downs[-1], "z", -1))
-    late = shift(ups[-1][0], "z", 1), shift(downs[-1][1], "z", -1)
+    late = shift(ups[-1], "z", 1)
     rights = downs + ups[:0:-1]
 
     vm = pl.BlockSpec(memory_space=pltpu.VMEM)
@@ -204,11 +204,11 @@
     *solved, mine = pl.pallas_call(
         solve_kernel,
         out_shape=[part] * 2 + [jax.ShapeDtypeStruct((share, panels * w), BF)],
-        in_specs=[sm] + [vm] * 11,
+        in_specs=[sm] + [vm] * 10,
         out_specs=[vm] * 3,
         compiler_params=params,
         name="solve",
-    )(pos, held, twin, *rights, *late)
+    )(pos, held, twin, *rights, late)
 
     there = y_shift(solved[0], 1), y_shift(solved[1], -1)
     there = y_shift(there[0], 1), y_shift(there[1], -1)

time: 121 us -> 126 us (1.041)
  waiting for transfers between devices: 37.7 us -> 46.2 us
  starting transfers between devices: 54.7 us -> 51 us
    ppermute x26 -> x25, waiting for transfers between devices: 28.9 us -> 34.1 us  [shift(): return lax.ppermute(a, axis, [(i, (i + by) % n) for i in range(n)])]
    ppermute x26 -> x25, starting transfers between devices: 42.4 us -> 38.7 us  [shift(): return lax.ppermute(a, axis, [(i, (i + by) % n) for i in range(n)])]
    all_to_all x1, waiting for transfers between devices: 7.69 us -> 11 us  [compute(): held = lax.all_to_all(got, ('yl', 'yh', 'x'), 0, 0, tiled=True)]
  transfers between devices with their start and end apart: 31 -> 30, of which waited for: 13 -> 13; matrix products, arithmetic and copies ran while one was open for 0% -> 0% of each run, Pallas kernels for 4% -> 4%
where the time goes in v7:
time: 126 us
  starting transfers between devices  51 us (40%)
  waiting for transfers between devices  46.2 us (37%)
  blocking collectives  15.4 us (12%)
  Pallas kernels  8.9 us (7%)
  local copies, waits for them, and re-layouts  3.69 us (3%)
    ppermute x25, starting transfers between devices, shift(): return lax.ppermute(a, axis, [(i, (i + by) % n) for i in range(n)])  38.7 us
    ppermute x25, waiting for transfers between devices, shift(): return lax.ppermute(a, axis, [(i, (i + by) % n) for i in range(n)])  34.1 us
    all_to_all x1, blocking collectives, compute(): got = lax.all_to_all(rows, 'z', 0, 0, tiled=True)  15.4 us
    all_to_all x1, waiting for transfers between devices, compute(): held = lax.all_to_all(got, ('yl', 'yh', 'x'), 0, 0, tiled=True)  11 us
    all_to_all x1, starting transfers between devices, compute(): held = lax.all_to_all(got, ('yl', 'yh', 'x'), 0, 0, tiled=True)  6.89 us
    ppermute x4, starting transfers between devices, y_shift(): return lax.ppermute(a, ('yl', 'yh'), pairs)  5.43 us
    pallas_call x2, Pallas kernels, more(): pl.pallas_call(functools.partial(more_kernel, offsets), out_shape=full, i...  4.29 us
    pallas_call x1, Pallas kernels, compute(): pl.pallas_call(near_kernel, out_shape=(full, jax.ShapeDtypeStruct((panels...  3.13 us
  transfers between devices with their start and end apart: 30, of which 13 were waited for; matrix products, arithmetic and copies ran while one was open for 0% of the time, Pallas kernels for 4%

profile of v7, /device:TPU:1, one launch (start us, length us, event | category | flops | bytes accessed | tf_op | source)
XLA Modules:
  0.0 125.7 jit_solution(6653506084390450835)
XLA Ops:
  0.0 0.7 copy-done
  0.7 0.0 copy-done.4
  0.7 0.1 fusion.4
  0.8 2.2 %collective-permute-start = (bf16[4,256]{1,0:T(4,128)(2,1)S(1)}, bf16[4,256]{1,0:T(4,128)(2,1)S(1)}, u32[]{:S(2)}, u32[]{:S(2)}) collective-permute-start(bf16[4,256]{1,0:T(4,128)(2,1)S(1)} %get-tuple-element.20), channel_id=1, source_target_pairs={{0,128},{128,0},{1,129},{129,1},{2,130},{130,2},{3,131},{131,3},{4... | collective-permute-start | bytes 6152 | tf_op jit(solution)/shard_map/ppermute | solution.py:22
  3.0 1.0 collective-permute-done
  4.0 15.4 %all_to_all.10 = bf16[8,32,128]{2,1,0:T(8,128)(2,1)S(1)} all-to-all(bf16[8,32,128]{2,1,0:T(8,128)(2,1)S(1)} %broadcast_in_dim.29), channel_id=1, replica_groups=mesh['yl'=2,'core'=2,'yh'=2,'x'=4,'z'=8] {'z'}, dimensions={0} | all-to-all | bytes 131072 | tf_op jit(solution)/shard_map/all_to_all | solution.py:174
  19.5 1.2 broadcast_in_dim.31
  20.6 6.9 %all-to-all-start.1 = ((bf16[16,256,128]{2,1,0:T(8,128)(2,1)}), bf16[16,256,128]{2,1,0:T(8,128)(2,1)S(1)}, u32[]{:S(2)}, u32[]{:S(2)}) async-start(bf16[16,256,128]{2,1,0:T(8,128)(2,1)} %broadcast_in_dim.31), calls=%async_computation.1 | async-start | bytes 2097152 | tf_op jit(solution)/shard_map/all_to_all | solution.py:178
  27.5 0.1 copy.26
  27.6 3.6 %collective-permute-start.2 = (f32[128,256]{1,0:T(8,128)S(1)}, f32[128,256]{1,0:T(8,128)S(1)}, u32[]{:S(2)}, u32[]{:S(2)}) collective-permute-start(f32[128,256]{1,0:T(8,128)S(1)} %bitcast.72), channel_id=1, source_target_pairs={{0,64},{64,0},{1,65},{65,1},{2,66},{66,2},{3,67},{67,3},{4,68},{68... | collective-permute-start | bytes 393224 | tf_op jit(solution)/shard_map/ppermute | solution.py:22
  31.3 11.0 %all-to-all-done.1.own_ref = bf16[16,256,128]{2,1,0:T(8,128)(2,1)S(1)} async-done(((bf16[16,256,128]{2,1,0:T(8,128)(2,1)}), bf16[16,256,128]{2,1,0:T(8,128)(2,1)S(1)}, u32[]{:S(2)}, u32[]{:S(2)}) %all-to-all-start.1) | async-done | bytes 1048608 | tf_op jit(solution)/shard_map/all_to_all | solution.py:178
  42.3 3.8 %collective-permute-start.1 = (bf16[16,256,128]{2,1,0:T(8,128)(2,1)S(1)}, bf16[16,256,128]{2,1,0:T(8,128)(2,1)S(1)}, u32[]{:S(2)}, u32[]{:S(2)}) collective-permute-start(bf16[16,256,128]{2,1,0:T(8,128)(2,1)S(1)} %all-to-all-done.1.own_ref), channel_id=1, source_target_pairs={{0,64},{64,0},{1,65},{65,1},{2,66},{66,2},{3,67},{67,3},{4,68},{68... | collective-permute-start | bytes 3145736 | tf_op jit(solution)/shard_map/ppermute | solution.py:22
  46.1 0.0 collective-permute-done.2
  46.1 0.1 collective-permute-start.3
  46.2 3.6 %collective-permute-done.3 = f32[2,32,256]{2,1,0:T(8,128)S(1)} collective-permute-done((f32[2,32,256]{2,1,0:T(8,128)S(1)}, f32[2,32,256]{2,1,0:T(8,128)S(1)}, u32[]{:S(2)}, u32[]{:S(2)}) %collective-permute-start.3) | collective-permute-done | bytes 65568 | tf_op jit(solution)/shard_map/ppermute | solution.py:22
  49.9 0.5 collective-permute-start.7
  50.4 2.3 %collective-permute-start.4 = (f32[2,2,32,256]{3,2,1,0:T(8,128)S(1)}, f32[2,2,32,256]{3,2,1,0:T(8,128)S(1)}, u32[]{:S(2)}, u32[]{:S(2)}) collective-permute-start(f32[2,2,32,256]{3,2,1,0:T(8,128)S(1)} %pad_maximum_fusion.refs_0_), channel_id=1, source_target_pairs={{0,7},{1,0},{2,1},{3,2},{4,3},{5,4},{6,5},{7,6},{8,15},{9,8},{10,9... | collective-permute-start | bytes 393224 | tf_op jit(solution)/shard_map/ppermute | solution.py:22
  52.7 2.7 %collective-permute-done.7.refs_6_ = f32[2,2,32,256]{3,2,1,0:T(8,128)S(1)} collective-permute-done((f32[2,2,32,256]{3,2,1,0:T(8,128)S(1)}, f32[2,2,32,256]{3,2,1,0:T(8,128)S(1)}, u32[]{:S(2)}, u32[]{:S(2)}) %collective-permute-start.7) | collective-permute-done | bytes 131104 | tf_op jit(solution)/shard_map/ppermute | solution.py:22
  55.4 0.0 collective-permute-start.8
  55.4 0.0 collective-permute-done.4.refs_1_
  55.4 2.7 %collective-permute-start.5 = (f32[2,2,32,256]{3,2,1,0:T(8,128)S(1)}, f32[2,2,32,256]{3,2,1,0:T(8,128)S(1)}, u32[]{:S(2)}, u32[]{:S(2)}) collective-permute-start(f32[2,2,32,256]{3,2,1,0:T(8,128)S(1)} %collective-permute-done.4.refs_1_), channel_id=1, source_target_pairs={{0,7},{1,0},{2,1},{3,2},{4,3},{5,4},{6,5},{7,6},{8,15},{9,8},{10,9... | collective-permute-start | bytes 393224 | tf_op jit(solution)/shard_map/ppermute | solution.py:22
  58.1 2.3 %collective-permute-done.8.refs_5_ = f32[2,2,32,256]{3,2,1,0:T(8,128)S(1)} collective-permute-done((f32[2,2,32,256]{3,2,1,0:T(8,128)S(1)}, f32[2,2,32,256]{3,2,1,0:T(8,128)S(1)}, u32[]{:S(2)}, u32[]{:S(2)}) %collective-permute-start.8) | collective-permute-done | bytes 131104 | tf_op jit(solution)/shard_map/ppermute | solution.py:22
  60.4 0.0 collective-permute-start.9
  60.4 0.0 collective-permute-done.5.refs_2_
  60.4 2.7 %collective-permute-start.6 = (f32[2,2,32,256]{3,2,1,0:T(8,128)S(1)}, f32[2,2,32,256]{3,2,1,0:T(8,128)S(1)}, u32[]{:S(2)}, u32[]{:S(2)}) collective-permute-start(f32[2,2,32,256]{3,2,1,0:T(8,128)S(1)} %collective-permute-done.5.refs_2_), channel_id=1, source_target_pairs={{0,7},{1,0},{2,1},{3,2},{4,3},{5,4},{6,5},{7,6},{8,15},{9,8},{10,9... | collective-permute-start | bytes 393224 | tf_op jit(solution)/shard_map/ppermute | solution.py:22
  63.1 2.3 %collective-permute-done.9.refs_4_ = f32[2,2,32,256]{3,2,1,0:T(8,128)S(1)} collective-permute-done((f32[2,2,32,256]{3,2,1,0:T(8,128)S(1)}, f32[2,2,32,256]{3,2,1,0:T(8,128)S(1)}, u32[]{:S(2)}, u32[]{:S(2)}) %collective-permute-start.9) | collective-permute-done | bytes 131104 | tf_op jit(solution)/shard_map/ppermute | solution.py:22
  65.5 5.0 %collective-permute-done.10.refs_7_ = f32[2,2,32,256]{3,2,1,0:T(8,128)S(1)} collective-permute-done((f32[2,2,32,256]{3,2,1,0:T(8,128)S(1)}, f32[2,2,32,256]{3,2,1,0:T(8,128)S(1)}, u32[]{:S(2)}, u32[]{:S(2)}) %collective-permute-start.10) | collective-permute-done | bytes 131104 | tf_op jit(solution)/shard_map/ppermute | solution.py:22
  70.5 1.5 %solve.1 = (bf16[4,32,1024]{2,1,0:T(8,128)(2,1)S(1)}, bf16[4,32,1024]{2,1,0:T(8,128)(2,1)S(1)}, bf16[32,1024]{1,0:T(8,128)(2,1)S(1)}) custom-call(s32[1]{0:T(128)} %bitcast.2.pos_ref, bf16[16,256,128]{2,1,0:T(8,128)(2,1)S(1)} %all-to-all-done.1.own_ref, bf16[16,256,128]{2,1,0:T(8,128)(2,1)S(1)} %collective-permute-done.1.twin_ref, ...), custom_call_target="tpu_custom_call" | custom-call | tf_op jit(solution)/shard_map/solve/pallas_call | solution.py:204
  72.0 0.2 collective-permute-start.19
  72.1 2.6 %collective-permute-start.21 = (bf16[4,32,1024]{2,1,0:T(8,128)(2,1)S(1)}, bf16[4,32,1024]{2,1,0:T(8,128)(2,1)S(1)}, u32[]{:S(2)}, u32[]{:S(2)}) collective-permute-start(bf16[4,32,1024]{2,1,0:T(8,128)(2,1)S(1)} %get-tuple-element.12.refs_1_), channel_id=1, source_target_pairs={{0,160},{32,128},{128,0},{160,32},{1,161},{33,129},{129,1},{161,33... | collective-permute-start | bytes 786440 | tf_op jit(solution)/shard_map/ppermute | solution.py:140
  74.7 0.0 collective-permute-start.11
  74.7 0.4 collective-permute-start.15
  75.1 2.2 %collective-permute-start.14 = (bf16[4,32,1024]{2,1,0:T(8,128)(2,1)S(1)}, bf16[4,32,1024]{2,1,0:T(8,128)(2,1)S(1)}, u32[]{:S(2)}, u32[]{:S(2)}) collective-permute-start(bf16[4,32,1024]{2,1,0:T(8,128)(2,1)S(1)} %get-tuple-element.12.refs_1_), channel_id=1, source_target_pairs={{0,24},{8,0},{16,8},{24,16},{1,25},{9,1},{17,9},{25,17},{2,26},{10... | collective-permute-start | bytes 786440 | tf_op jit(solution)/shard_map/ppermute | solution.py:22
  77.4 1.1 collective-permute-done.19
  78.5 0.4 collective-permute-start.20
  78.9 0.0 collective-permute-done.21
  78.9 2.3 %collective-permute-start.22 = (bf16[4,32,1024]{2,1,0:T(8,128)(2,1)S(1)}, bf16[4,32,1024]{2,1,0:T(8,128)(2,1)S(1)}, u32[]{:S(2)}, u32[]{:S(2)}) collective-permute-start(bf16[4,32,1024]{2,1,0:T(8,128)(2,1)S(1)} %collective-permute-done.21), channel_id=1, source_target_pairs={{0,160},{32,128},{128,0},{160,32},{1,161},{33,129},{129,1},{161,33... | collective-permute-start | bytes 786440 | tf_op jit(solution)/shard_map/ppermute | solution.py:140
  81.2 9.2 %collective-permute-start.12 = (bf16[2,32,1024]{2,1,0:T(8,128)(2,1)S(1)}, bf16[2,32,1024]{2,1,0:T(8,128)(2,1)S(1)}, u32[]{:S(2)}, u32[]{:S(2)}) collective-permute-start(bf16[2,32,1024]{2,1,0:T(8,128)(2,1)S(1)} %pad_maximum_fusion.1), channel_id=1, source_target_pairs={{0,64},{64,0},{1,65},{65,1},{2,66},{66,2},{3,67},{67,3},{4,68},{68... | collective-permute-start | bytes 393224 | tf_op jit(solution)/shard_map/ppermute | solution.py:22
  90.4 1.0 collective-permute-done.12.m2
  91.4 0.7 copy-done.1
  92.1 0.5 collective-permute-start.13
  92.6 0.0 collective-permute-done.15.refs_4_
  92.6 1.0 collective-permute-start.16
  93.5 0.4 collective-permute-start.17
  94.0 0.0 collective-permute-done.20.refs_8_
  94.0 0.1 collective-permute-start.25
  94.1 2.6 %collective-permute-start.24 = (bf16[4,32,1024]{2,1,0:T(8,128)(2,1)S(1)}, bf16[4,32,1024]{2,1,0:T(8,128)(2,1)S(1)}, u32[]{:S(2)}, u32[]{:S(2)}) collective-permute-start(bf16[4,32,1024]{2,1,0:T(8,128)(2,1)S(1)} %collective-permute-done.22.refs_9_), channel_id=1, source_target_pairs={{0,24},{8,0},{16,8},{24,16},{1,25},{9,1},{17,9},{25,17},{2,26},{10... | collective-permute-start | bytes 786440 | tf_op jit(solution)/shard_map/ppermute | solution.py:22
  96.7 2.9 %collective-permute-done.13.refs_2_ = bf16[4,32,1024]{2,1,0:T(8,128)(2,1)S(1)} collective-permute-done((bf16[4,32,1024]{2,1,0:T(8,128)(2,1)S(1)}, bf16[4,32,1024]{2,1,0:T(8,128)(2,1)S(1)}, u32[]{:S(2)}, u32[]{:S(2)}) %collective-permute-start.13) | collective-permute-done | bytes 262176 | tf_op jit(solution)/shard_map/ppermute | solution.py:22
  99.6 1.7 %collective-permute-start.18 = (bf16[4,32,1024]{2,1,0:T(8,128)(2,1)S(1)}, bf16[4,32,1024]{2,1,0:T(8,128)(2,1)}, u32[]{:S(2)}, u32[]{:S(2)}) collective-permute-start(bf16[4,32,1024]{2,1,0:T(8,128)(2,1)S(1)} %collective-permute-done.14.refs_3_), channel_id=1, source_target_pairs={{0,24},{8,0},{16,8},{24,16},{1,25},{9,1},{17,9},{25,17},{2,26},{10... | collective-permute-start | bytes 786440 | tf_op jit(solution)/shard_map/ppermute | solution.py:22
  101.3 0.0 collective-permute-done.16.refs_5_
  101.3 0.0 collective-permute-start.23
  101.3 5.3 %collective-permute-done.17.refs_6_ = bf16[4,32,1024]{2,1,0:T(8,128)(2,1)S(1)} collective-permute-done((bf16[4,32,1024]{2,1,0:T(8,128)(2,1)S(1)}, bf16[4,32,1024]{2,1,0:T(8,128)(2,1)S(1)}, u32[]{:S(2)}, u32[]{:S(2)}) %collective-permute-start.17) | collective-permute-done | bytes 262176 | tf_op jit(solution)/shard_map/ppermute | solution.py:22
  106.6 5.6 %collective-permute-done.25.refs_2_ = bf16[4,32,1024]{2,1,0:T(8,128)(2,1)S(1)} collective-permute-done((bf16[4,32,1024]{2,1,0:T(8,128)(2,1)S(1)}, bf16[4,32,1024]{2,1,0:T(8,128)(2,1)S(1)}, u32[]{:S(2)}, u32[]{:S(2)}) %collective-permute-start.25) | collective-permute-done | bytes 262176 | tf_op jit(solution)/shard_map/ppermute | solution.py:22
  112.2 0.0 collective-permute-start.27
  112.2 0.0 collective-permute-done.24.refs_1_
  112.2 2.7 %collective-permute-start.28 = (bf16[4,32,1024]{2,1,0:T(8,128)(2,1)S(1)}, bf16[4,32,1024]{2,1,0:T(8,128)(2,1)}, u32[]{:S(2)}, u32[]{:S(2)}) collective-permute-start(bf16[4,32,1024]{2,1,0:T(8,128)(2,1)S(1)} %collective-permute-done.24.refs_1_), channel_id=1, source_target_pairs={{0,24},{8,0},{16,8},{24,16},{1,25},{9,1},{17,9},{25,17},{2,26},{10... | collective-permute-start | bytes 786440 | tf_op jit(solution)/shard_map/ppermute | solution.py:22
  114.9 0.1 stack.65.pos_ref
  115.0 0.0 collective-permute-done.18.refs_7_
  115.0 0.9 copy-done.2
  115.9 3.1 %near.1 = (f32[128,1,2048]{2,1,0:T(1,128)}, bf16[4,32,1024]{2,1,0:T(8,128)(2,1)S(1)}) custom-call(s32[5]{0:T(128)S(1)} %stack.65.pos_ref, bf16[32,1024]{1,0:T(8,128)(2,1)S(1)} %get-tuple-element.10.m0, bf16[32,1024]{1,0:T(8,128)(2,1)S(1)} %collective-permute-done.11.m1, bf16[2,32,1024]{2,1,0:T(8,128)(2,1)S(1)} %copy-done.2, ...), custom_call_target="tpu_custom_call" | custom-call | tf_op jit(solution)/shard_map/near/pallas_call | solution.py:227
  119.0 0.0 collective-permute-done.23.refs_0_
  119.0 2.3 %shard_map.46.before = f32[128,1,2048]{2,1,0:T(1,128)} custom-call(s32[5]{0:T(128)S(1)} %stack.65.pos_ref, f32[128,1,2048]{2,1,0:T(1,128)} %get-tuple-element.13.before, bf16[4,32,1024]{2,1,0:T(8,128)(2,1)S(1)} %get-tuple-element.14.own, bf16[4,32,1024]{2,1,0:T(8,128)(2,1)S(1)} %collective-permute-done.23.refs_0_, ...), custom_call_target="tpu_custom_call", output_to_operand_aliasing={{}: (1, {})} | custom-call | tf_op jit(solution)/shard_map/pallas_call | solution.py:239
  121.3 2.1 %collective-permute-done.27.refs_0_ = bf16[4,32,1024]{2,1,0:T(8,128)(2,1)S(1)} collective-permute-done((bf16[4,32,1024]{2,1,0:T(8,128)(2,1)S(1)}, bf16[4,32,1024]{2,1,0:T(8,128)(2,1)S(1)}, u32[]{:S(2)}, u32[]{:S(2)}) %collective-permute-start.27) | collective-permute-done | bytes 262176 | tf_op jit(solution)/shard_map/ppermute | solution.py:22
  123.5 2.0 %shard_map.47 = f32[128,1,2048]{2,1,0:T(1,128)} custom-call(s32[5]{0:T(128)S(1)} %stack.65.pos_ref, f32[128,1,2048]{2,1,0:T(1,128)} %shard_map.46.before, bf16[4,32,1024]{2,1,0:T(8,128)(2,1)S(1)} %get-tuple-element.14.own, bf16[4,32,1024]{2,1,0:T(8,128)(2,1)S(1)} %collective-permute-done.27.refs_0_, ...), custom_call_target="tpu_custom_call", output_to_operand_aliasing={{}: (1, {})} | custom-call | tf_op jit(solution)/shard_map/pallas_call | solution.py:239
  (31 shorter events, 0.2 us)
Async XLA Ops:
  0.0 0.7 copy-start
  0.0 0.7 copy-start.4
  0.8 2.2 %copy-start.5 = (f32[1,1,256,4]{2,3,1,0:T(4,128)S(1)}, f32[1,1,256,4]{2,3,1,0:T(4,128)}, u32[]{:S(2)}) copy-start(f32[1,1,256,4]{2,3,1,0:T(4,128)} %param.5) | copy-start | bytes 12292
  0.8 3.2 %collective-permute-start = (bf16[4,256]{1,0:T(4,128)(2,1)S(1)}, bf16[4,256]{1,0:T(4,128)(2,1)S(1)}, u32[]{:S(2)}, u32[]{:S(2)}) collective-permute-start(bf16[4,256]{1,0:T(4,128)(2,1)S(1)} %get-tuple-element.20), channel_id=1, source_target_pairs={{0,128},{128,0},{1,129},{129,1},{2,130},{130,2},{3,131},{131,3},{4... | collective-permute-start | bytes 6152 | tf_op jit(solution)/shard_map/ppermute | solution.py:22
  20.6 6.9 %copy-start.3 = (f32[1,1,256,128]{3,2,1,0:T(8,128)S(1)}, f32[1,1,256,128]{3,2,1,0:T(8,128)}, u32[]{:S(2)}) copy-start(f32[1,1,256,128]{3,2,1,0:T(8,128)} %param.6) | copy-start | bytes 393220
  20.6 21.7 %all-to-all-start.1 = ((bf16[16,256,128]{2,1,0:T(8,128)(2,1)}), bf16[16,256,128]{2,1,0:T(8,128)(2,1)S(1)}, u32[]{:S(2)}, u32[]{:S(2)}) async-start(bf16[16,256,128]{2,1,0:T(8,128)(2,1)} %broadcast_in_dim.31), calls=%async_computation.1 | async-start | bytes 2097152 | tf_op jit(solution)/shard_map/all_to_all | solution.py:178
  27.6 18.4 %collective-permute-start.2 = (f32[128,256]{1,0:T(8,128)S(1)}, f32[128,256]{1,0:T(8,128)S(1)}, u32[]{:S(2)}, u32[]{:S(2)}) collective-permute-start(f32[128,256]{1,0:T(8,128)S(1)} %bitcast.72), channel_id=1, source_target_pairs={{0,64},{64,0},{1,65},{65,1},{2,66},{66,2},{3,67},{67,3},{4,68},{68... | collective-permute-start | bytes 393224 | tf_op jit(solution)/shard_map/ppermute | solution.py:22
  42.3 28.2 %collective-permute-start.1 = (bf16[16,256,128]{2,1,0:T(8,128)(2,1)S(1)}, bf16[16,256,128]{2,1,0:T(8,128)(2,1)S(1)}, u32[]{:S(2)}, u32[]{:S(2)}) collective-permute-start(bf16[16,256,128]{2,1,0:T(8,128)(2,1)S(1)} %all-to-all-done.1.own_ref), channel_id=1, source_target_pairs={{0,64},{64,0},{1,65},{65,1},{2,66},{66,2},{3,67},{67,3},{4,68},{68... | collective-permute-start | bytes 3145736 | tf_op jit(solution)/shard_map/ppermute | solution.py:22
  46.1 3.7 %collective-permute-start.3 = (f32[2,32,256]{2,1,0:T(8,128)S(1)}, f32[2,32,256]{2,1,0:T(8,128)S(1)}, u32[]{:S(2)}, u32[]{:S(2)}) collective-permute-start(f32[2,32,256]{2,1,0:T(8,128)S(1)} %fusion.1), channel_id=1, source_target_pairs={{0,128},{128,0},{1,129},{129,1},{2,130},{130,2},{3,131},{131,3},{4... | collective-permute-start | bytes 196616 | tf_op jit(solution)/shard_map/ppermute | solution.py:22
  49.9 5.5 %collective-permute-start.7 = (f32[2,2,32,256]{3,2,1,0:T(8,128)S(1)}, f32[2,2,32,256]{3,2,1,0:T(8,128)S(1)}, u32[]{:S(2)}, u32[]{:S(2)}) collective-permute-start(f32[2,2,32,256]{3,2,1,0:T(8,128)S(1)} %pad_maximum_fusion.refs_0_), channel_id=1, source_target_pairs={{0,1},{1,2},{2,3},{3,4},{4,5},{5,6},{6,7},{7,0},{8,9},{9,10},{10,1... | collective-permute-start | bytes 393224 | tf_op jit(solution)/shard_map/ppermute | solution.py:22
  50.4 5.0 %collective-permute-start.4 = (f32[2,2,32,256]{3,2,1,0:T(8,128)S(1)}, f32[2,2,32,256]{3,2,1,0:T(8,128)S(1)}, u32[]{:S(2)}, u32[]{:S(2)}) collective-permute-start(f32[2,2,32,256]{3,2,1,0:T(8,128)S(1)} %pad_maximum_fusion.refs_0_), channel_id=1, source_target_pairs={{0,7},{1,0},{2,1},{3,2},{4,3},{5,4},{6,5},{7,6},{8,15},{9,8},{10,9... | collective-permute-start | bytes 393224 | tf_op jit(solution)/shard_map/ppermute | solution.py:22
  55.4 5.0 %collective-permute-start.8 = (f32[2,2,32,256]{3,2,1,0:T(8,128)S(1)}, f32[2,2,32,256]{3,2,1,0:T(8,128)S(1)}, u32[]{:S(2)}, u32[]{:S(2)}) collective-permute-start(f32[2,2,32,256]{3,2,1,0:T(8,128)S(1)} %collective-permute-done.7.refs_6_), channel_id=1, source_target_pairs={{0,1},{1,2},{2,3},{3,4},{4,5},{5,6},{6,7},{7,0},{8,9},{9,10},{10,1... | collective-permute-start | bytes 393224 | tf_op jit(solution)/shard_map/ppermute | solution.py:22
  55.4 5.0 %collective-permute-start.5 = (f32[2,2,32,256]{3,2,1,0:T(8,128)S(1)}, f32[2,2,32,256]{3,2,1,0:T(8,128)S(1)}, u32[]{:S(2)}, u32[]{:S(2)}) collective-permute-start(f32[2,2,32,256]{3,2,1,0:T(8,128)S(1)} %collective-permute-done.4.refs_1_), channel_id=1, source_target_pairs={{0,7},{1,0},{2,1},{3,2},{4,3},{5,4},{6,5},{7,6},{8,15},{9,8},{10,9... | collective-permute-start | bytes 393224 | tf_op jit(solution)/shard_map/ppermute | solution.py:22
  60.4 5.0 %collective-permute-start.9 = (f32[2,2,32,256]{3,2,1,0:T(8,128)S(1)}, f32[2,2,32,256]{3,2,1,0:T(8,128)S(1)}, u32[]{:S(2)}, u32[]{:S(2)}) collective-permute-start(f32[2,2,32,256]{3,2,1,0:T(8,128)S(1)} %collective-permute-done.8.refs_5_), channel_id=1, source_target_pairs={{0,1},{1,2},{2,3},{3,4},{4,5},{5,6},{6,7},{7,0},{8,9},{9,10},{10,1... | collective-permute-start | bytes 393224 | tf_op jit(solution)/shard_map/ppermute | solution.py:22
  60.4 5.0 %collective-permute-start.6 = (f32[2,2,32,256]{3,2,1,0:T(8,128)S(1)}, f32[2,2,32,256]{3,2,1,0:T(8,128)S(1)}, u32[]{:S(2)}, u32[]{:S(2)}) collective-permute-start(f32[2,2,32,256]{3,2,1,0:T(8,128)S(1)} %collective-permute-done.5.refs_2_), channel_id=1, source_target_pairs={{0,7},{1,0},{2,1},{3,2},{4,3},{5,4},{6,5},{7,6},{8,15},{9,8},{10,9... | collective-permute-start | bytes 393224 | tf_op jit(solution)/shard_map/ppermute | solution.py:22
  65.4 5.0 %collective-permute-start.10 = (f32[2,2,32,256]{3,2,1,0:T(8,128)S(1)}, f32[2,2,32,256]{3,2,1,0:T(8,128)S(1)}, u32[]{:S(2)}, u32[]{:S(2)}) collective-permute-start(f32[2,2,32,256]{3,2,1,0:T(8,128)S(1)} %collective-permute-done.9.refs_4_), channel_id=1, source_target_pairs={{0,1},{1,2},{2,3},{3,4},{4,5},{5,6},{6,7},{7,0},{8,9},{9,10},{10,1... | collective-permute-start | bytes 393224 | tf_op jit(solution)/shard_map/ppermute | solution.py:22
  72.0 6.5 %collective-permute-start.19 = (bf16[4,32,1024]{2,1,0:T(8,128)(2,1)S(1)}, bf16[4,32,1024]{2,1,0:T(8,128)(2,1)S(1)}, u32[]{:S(2)}, u32[]{:S(2)}) collective-permute-start(bf16[4,32,1024]{2,1,0:T(8,128)(2,1)S(1)} %get-tuple-element.11.refs_0_), channel_id=1, source_target_pairs={{0,128},{32,160},{128,32},{160,0},{1,129},{33,161},{129,33},{161,1... | collective-permute-start | bytes 786440 | tf_op jit(solution)/shard_map/ppermute | solution.py:140
  72.1 6.7 %collective-permute-start.21 = (bf16[4,32,1024]{2,1,0:T(8,128)(2,1)S(1)}, bf16[4,32,1024]{2,1,0:T(8,128)(2,1)S(1)}, u32[]{:S(2)}, u32[]{:S(2)}) collective-permute-start(bf16[4,32,1024]{2,1,0:T(8,128)(2,1)S(1)} %get-tuple-element.12.refs_1_), channel_id=1, source_target_pairs={{0,160},{32,128},{128,0},{160,32},{1,161},{33,129},{129,1},{161,33... | collective-permute-start | bytes 786440 | tf_op jit(solution)/shard_map/ppermute | solution.py:140
  74.7 6.4 %collective-permute-start.11 = (bf16[32,1024]{1,0:T(8,128)(2,1)S(1)}, bf16[32,1024]{1,0:T(8,128)(2,1)S(1)}, u32[]{:S(2)}, u32[]{:S(2)}) collective-permute-start(bf16[32,1024]{1,0:T(8,128)(2,1)S(1)} %get-tuple-element.10.m0), channel_id=1, source_target_pairs={{0,128},{128,0},{1,129},{129,1},{2,130},{130,2},{3,131},{131,3},{4... | collective-permute-start | bytes 196616 | tf_op jit(solution)/shard_map/ppermute | solution.py:22
  74.7 17.9 %collective-permute-start.15 = (bf16[4,32,1024]{2,1,0:T(8,128)(2,1)S(1)}, bf16[4,32,1024]{2,1,0:T(8,128)(2,1)S(1)}, u32[]{:S(2)}, u32[]{:S(2)}) collective-permute-start(bf16[4,32,1024]{2,1,0:T(8,128)(2,1)S(1)} %get-tuple-element.11.refs_0_), channel_id=1, source_target_pairs={{0,8},{8,16},{16,24},{24,0},{1,9},{9,17},{17,25},{25,1},{2,10},{10... | collective-permute-start | bytes 786440 | tf_op jit(solution)/shard_map/ppermute | solution.py:22
  75.1 18.4 %collective-permute-start.14 = (bf16[4,32,1024]{2,1,0:T(8,128)(2,1)S(1)}, bf16[4,32,1024]{2,1,0:T(8,128)(2,1)S(1)}, u32[]{:S(2)}, u32[]{:S(2)}) collective-permute-start(bf16[4,32,1024]{2,1,0:T(8,128)(2,1)S(1)} %get-tuple-element.12.refs_1_), channel_id=1, source_target_pairs={{0,24},{8,0},{16,8},{24,16},{1,25},{9,1},{17,9},{25,17},{2,26},{10... | collective-permute-start | bytes 786440 | tf_op jit(solution)/shard_map/ppermute | solution.py:22
  78.5 15.5 %collective-permute-start.20 = (bf16[4,32,1024]{2,1,0:T(8,128)(2,1)S(1)}, bf16[4,32,1024]{2,1,0:T(8,128)(2,1)S(1)}, u32[]{:S(2)}, u32[]{:S(2)}) collective-permute-start(bf16[4,32,1024]{2,1,0:T(8,128)(2,1)S(1)} %collective-permute-done.19), channel_id=1, source_target_pairs={{0,128},{32,160},{128,32},{160,0},{1,129},{33,161},{129,33},{161,1... | collective-permute-start | bytes 786440 | tf_op jit(solution)/shard_map/ppermute | solution.py:140
  78.9 15.2 %collective-permute-start.22 = (bf16[4,32,1024]{2,1,0:T(8,128)(2,1)S(1)}, bf16[4,32,1024]{2,1,0:T(8,128)(2,1)S(1)}, u32[]{:S(2)}, u32[]{:S(2)}) collective-permute-start(bf16[4,32,1024]{2,1,0:T(8,128)(2,1)S(1)} %collective-permute-done.21), channel_id=1, source_target_pairs={{0,160},{32,128},{128,0},{160,32},{1,161},{33,129},{129,1},{161,33... | collective-permute-start | bytes 786440 | tf_op jit(solution)/shard_map/ppermute | solution.py:140
  81.2 10.2 %collective-permute-start.12 = (bf16[2,32,1024]{2,1,0:T(8,128)(2,1)S(1)}, bf16[2,32,1024]{2,1,0:T(8,128)(2,1)S(1)}, u32[]{:S(2)}, u32[]{:S(2)}) collective-permute-start(bf16[2,32,1024]{2,1,0:T(8,128)(2,1)S(1)} %pad_maximum_fusion.1), channel_id=1, source_target_pairs={{0,64},{64,0},{1,65},{65,1},{2,66},{66,2},{3,67},{67,3},{4,68},{68... | collective-permute-start | bytes 393224 | tf_op jit(solution)/shard_map/ppermute | solution.py:22
  91.4 0.7 copy-start.1
  92.1 7.5 %collective-permute-start.13 = (bf16[4,32,1024]{2,1,0:T(8,128)(2,1)S(1)}, bf16[4,32,1024]{2,1,0:T(8,128)(2,1)S(1)}, u32[]{:S(2)}, u32[]{:S(2)}) collective-permute-start(bf16[4,32,1024]{2,1,0:T(8,128)(2,1)S(1)} %get-tuple-element.11.refs_0_), channel_id=1, source_target_pairs={{0,24},{8,0},{16,8},{24,16},{1,25},{9,1},{17,9},{25,17},{2,26},{10... | collective-permute-start | bytes 786440 | tf_op jit(solution)/shard_map/ppermute | solution.py:22
  92.6 8.7 %collective-permute-start.16 = (bf16[4,32,1024]{2,1,0:T(8,128)(2,1)S(1)}, bf16[4,32,1024]{2,1,0:T(8,128)(2,1)S(1)}, u32[]{:S(2)}, u32[]{:S(2)}) collective-permute-start(bf16[4,32,1024]{2,1,0:T(8,128)(2,1)S(1)} %get-tuple-element.12.refs_1_), channel_id=1, source_target_pairs={{0,8},{8,16},{16,24},{24,0},{1,9},{9,17},{17,25},{25,1},{2,10},{10... | collective-permute-start | bytes 786440 | tf_op jit(solution)/shard_map/ppermute | solution.py:22
  93.5 13.1 %collective-permute-start.17 = (bf16[4,32,1024]{2,1,0:T(8,128)(2,1)S(1)}, bf16[4,32,1024]{2,1,0:T(8,128)(2,1)S(1)}, u32[]{:S(2)}, u32[]{:S(2)}) collective-permute-start(bf16[4,32,1024]{2,1,0:T(8,128)(2,1)S(1)} %collective-permute-done.15.refs_4_), channel_id=1, source_target_pairs={{0,8},{8,16},{16,24},{24,0},{1,9},{9,17},{17,25},{25,1},{2,10},{10... | collective-permute-start | bytes 786440 | tf_op jit(solution)/shard_map/ppermute | solution.py:22
  94.0 18.3 %collective-permute-start.25 = (bf16[4,32,1024]{2,1,0:T(8,128)(2,1)S(1)}, bf16[4,32,1024]{2,1,0:T(8,128)(2,1)S(1)}, u32[]{:S(2)}, u32[]{:S(2)}) collective-permute-start(bf16[4,32,1024]{2,1,0:T(8,128)(2,1)S(1)} %collective-permute-done.20.refs_8_), channel_id=1, source_target_pairs={{0,8},{8,16},{16,24},{24,0},{1,9},{9,17},{17,25},{25,1},{2,10},{10... | collective-permute-start | bytes 786440 | tf_op jit(solution)/shard_map/ppermute | solution.py:22
  94.1 18.2 %collective-permute-start.24 = (bf16[4,32,1024]{2,1,0:T(8,128)(2,1)S(1)}, bf16[4,32,1024]{2,1,0:T(8,128)(2,1)S(1)}, u32[]{:S(2)}, u32[]{:S(2)}) collective-permute-start(bf16[4,32,1024]{2,1,0:T(8,128)(2,1)S(1)} %collective-permute-done.22.refs_9_), channel_id=1, source_target_pairs={{0,24},{8,0},{16,8},{24,16},{1,25},{9,1},{17,9},{25,17},{2,26},{10... | collective-permute-start | bytes 786440 | tf_op jit(solution)/shard_map/ppermute | solution.py:22
  99.6 15.4 %collective-permute-start.18 = (bf16[4,32,1024]{2,1,0:T(8,128)(2,1)S(1)}, bf16[4,32,1024]{2,1,0:T(8,128)(2,1)}, u32[]{:S(2)}, u32[]{:S(2)}) collective-permute-start(bf16[4,32,1024]{2,1,0:T(8,128)(2,1)S(1)} %collective-permute-done.14.refs_3_), channel_id=1, source_target_pairs={{0,24},{8,0},{16,8},{24,16},{1,25},{9,1},{17,9},{25,17},{2,26},{10... | collective-permute-start | bytes 786440 | tf_op jit(solution)/shard_map/ppermute | solution.py:22
  101.3 17.8 %collective-permute-start.23 = (bf16[4,32,1024]{2,1,0:T(8,128)(2,1)S(1)}, bf16[4,32,1024]{2,1,0:T(8,128)(2,1)S(1)}, u32[]{:S(2)}, u32[]{:S(2)}) collective-permute-start(bf16[4,32,1024]{2,1,0:T(8,128)(2,1)S(1)} %collective-permute-done.20.refs_8_), channel_id=1, source_target_pairs={{0,24},{8,0},{16,8},{24,16},{1,25},{9,1},{17,9},{25,17},{2,26},{10... | collective-permute-start | bytes 786440 | tf_op jit(solution)/shard_map/ppermute | solution.py:22
  106.6 12.4 %collective-permute-start.26 = (bf16[4,32,1024]{2,1,0:T(8,128)(2,1)S(1)}, bf16[4,32,1024]{2,1,0:T(8,128)(2,1)}, u32[]{:S(2)}, u32[]{:S(2)}) collective-permute-start(bf16[4,32,1024]{2,1,0:T(8,128)(2,1)S(1)} %collective-permute-done.22.refs_9_), channel_id=1, source_target_pairs={{0,8},{8,16},{16,24},{24,0},{1,9},{9,17},{17,25},{25,1},{2,10},{10... | collective-permute-start | bytes 786440 | tf_op jit(solution)/shard_map/ppermute | solution.py:22
  112.2 11.2 %collective-permute-start.27 = (bf16[4,32,1024]{2,1,0:T(8,128)(2,1)S(1)}, bf16[4,32,1024]{2,1,0:T(8,128)(2,1)S(1)}, u32[]{:S(2)}, u32[]{:S(2)}) collective-permute-start(bf16[4,32,1024]{2,1,0:T(8,128)(2,1)S(1)} %collective-permute-done.25.refs_2_), channel_id=1, source_target_pairs={{0,8},{8,16},{16,24},{24,0},{1,9},{9,17},{17,25},{25,1},{2,10},{10... | collective-permute-start | bytes 786440 | tf_op jit(solution)/shard_map/ppermute | solution.py:22
  112.2 11.2 %collective-permute-start.28 = (bf16[4,32,1024]{2,1,0:T(8,128)(2,1)S(1)}, bf16[4,32,1024]{2,1,0:T(8,128)(2,1)}, u32[]{:S(2)}, u32[]{:S(2)}) collective-permute-start(bf16[4,32,1024]{2,1,0:T(8,128)(2,1)S(1)} %collective-permute-done.24.refs_1_), channel_id=1, source_target_pairs={{0,24},{8,0},{16,8},{24,16},{1,25},{9,1},{17,9},{25,17},{2,26},{10... | collective-permute-start | bytes 786440 | tf_op jit(solution)/shard_map/ppermute | solution.py:22
  115.0 0.9 copy-start.2

commit v8 on v7

--- a/solution.py
+++ b/solution.py
@@ -98,13 +98,13 @@
 LAST = ((1, 2),)
 
 
-def near_kernel(pos_ref, m0, m1, m2, *refs):
+def near_kernel(pos_ref, m0, m1, m2, m3, *refs):
     blocks, out_ref, own = refs[:-2], refs[-2], refs[-1]
     yl, core = pos_ref[1], pos_ref[2]
     own[2 * yl + core] = m0[...]
     own[2 * (1 - yl) + core] = m1[...]
-    own[2 * yl + (1 - core)] = m2[0]
-    own[2 * (1 - yl) + (1 - core)] = m2[1]
+    own[2 * yl + (1 - core)] = m2[...]
+    own[2 * (1 - yl) + (1 - core)] = m3[...]
     lhs = own[...].reshape(-1, own.shape[2])
     for i, (dyh, dx) in enumerate(NEAR):
         value = columns(lhs, blocks[2 * i : 2 * i + 2], pos_ref[0])
@@ -214,7 +214,7 @@
     there = y_shift(there[0], 1), y_shift(there[1], -1)
     blocks = [x_ring(solved), x_ring(list(there))]
     m1 = shift(mine, "yl")
-    m2 = shift(jnp.stack([mine, m1]), "core")
+    m2, m3 = shift(mine, "core"), shift(m1, "core")
 
     def halves(offsets):
         return [half for dyh, dx in offsets for half in blocks[dyh][dx]]
@@ -227,11 +227,11 @@
     done, own = pl.pallas_call(
         near_kernel,
         out_shape=(full, jax.ShapeDtypeStruct((panels, share, panels * w), BF)),
-        in_specs=[sm] + [vm] * (3 + len(near)),
+        in_specs=[sm] + [vm] * (4 + len(near)),
         out_specs=(vm, vm),
         compiler_params=params,
         name="near",
-    )(pos, mine, m1, m2, *near)
+    )(pos, mine, m1, m2, m3, *near)
 
     def more(done, offsets):
         found = halves(offsets)

time: 126 us -> 132 us (1.048)
  the two profiles are of different devices: /device:TPU:1 before, /device:TPU:8 now
where the time goes in v8:
time: 132 us; the launch traced here: 130 us
  waiting for transfers between devices  54.7 us (41%)
  starting transfers between devices  44.7 us (34%)
  blocking collectives  16.5 us (12%)
  Pallas kernels  8.91 us (7%)
  local copies, waits for them, and re-layouts  5.06 us (4%)
    ppermute x26, waiting for transfers between devices, shift(): return lax.ppermute(a, axis, [(i, (i + by) % n) for i in range(n)])  38.4 us
    ppermute x26, starting transfers between devices, shift(): return lax.ppermute(a, axis, [(i, (i + by) % n) for i in range(n)])  32.2 us
    all_to_all x1, blocking collectives, compute(): got = lax.all_to_all(rows, 'z', 0, 0, tiled=True)  16.5 us
    all_to_all x1, waiting for transfers between devices, compute(): held = lax.all_to_all(got, ('yl', 'yh', 'x'), 0, 0, tiled=True)  13.1 us
    all_to_all x1, starting transfers between devices, compute(): held = lax.all_to_all(got, ('yl', 'yh', 'x'), 0, 0, tiled=True)  7.53 us
    ppermute x4, starting transfers between devices, y_shift(): return lax.ppermute(a, ('yl', 'yh'), pairs)  4.98 us
    pallas_call x2, Pallas kernels, more(): pl.pallas_call(functools.partial(more_kernel, offsets), out_shape=full, i...  4.3 us
    unnamed x17, local copies, waits for them, and re-layouts  3.73 us
  transfers between devices with their start and end apart: 31, of which 14 were waited for; matrix products, arithmetic and copies ran while one was open for 0% of the time, Pallas kernels for 4%

profile of v8, /device:TPU:8, one launch (start us, length us, event | category | flops | bytes accessed | tf_op | source)
XLA Modules:
  0.0 130.3 jit_solution(8557566517425874069)
XLA Ops:
  0.0 0.7 copy-done
  0.7 0.0 copy-done.6
  0.7 0.1 fusion.4
  0.8 2.2 %collective-permute-start = (bf16[4,256]{1,0:T(4,128)(2,1)S(1)}, bf16[4,256]{1,0:T(4,128)(2,1)S(1)}, u32[]{:S(2)}, u32[]{:S(2)}) collective-permute-start(bf16[4,256]{1,0:T(4,128)(2,1)S(1)} %get-tuple-element.20), channel_id=1, source_target_pairs={{0,128},{128,0},{1,129},{129,1},{2,130},{130,2},{3,131},{131,3},{4... | collective-permute-start | bytes 6152 | tf_op jit(solution)/shard_map/ppermute | solution.py:22
  3.1 1.6 %collective-permute-done = bf16[4,256]{1,0:T(4,128)(2,1)S(1)} collective-permute-done((bf16[4,256]{1,0:T(4,128)(2,1)S(1)}, bf16[4,256]{1,0:T(4,128)(2,1)S(1)}, u32[]{:S(2)}, u32[]{:S(2)}) %collective-permute-start) | collective-permute-done | bytes 2080 | tf_op jit(solution)/shard_map/ppermute | solution.py:22
  4.7 16.5 %all_to_all.10 = bf16[8,32,128]{2,1,0:T(8,128)(2,1)S(1)} all-to-all(bf16[8,32,128]{2,1,0:T(8,128)(2,1)S(1)} %broadcast_in_dim.29), channel_id=1, replica_groups=mesh['yl'=2,'core'=2,'yh'=2,'x'=4,'z'=8] {'z'}, dimensions={0} | all-to-all | bytes 131072 | tf_op jit(solution)/shard_map/all_to_all | solution.py:174
  21.2 1.2 broadcast_in_dim.31
  22.4 7.5 %all-to-all-start.1 = ((bf16[16,256,128]{2,1,0:T(8,128)(2,1)}), bf16[16,256,128]{2,1,0:T(8,128)(2,1)S(1)}, u32[]{:S(2)}, u32[]{:S(2)}) async-start(bf16[16,256,128]{2,1,0:T(8,128)(2,1)} %broadcast_in_dim.31), calls=%async_computation.1 | async-start | bytes 2097152 | tf_op jit(solution)/shard_map/all_to_all | solution.py:178
  29.9 0.1 copy.26
  30.0 0.1 collective-permute-start.2
  30.2 13.1 %all-to-all-done.1.own_ref = bf16[16,256,128]{2,1,0:T(8,128)(2,1)S(1)} async-done(((bf16[16,256,128]{2,1,0:T(8,128)(2,1)}), bf16[16,256,128]{2,1,0:T(8,128)(2,1)S(1)}, u32[]{:S(2)}, u32[]{:S(2)}) %all-to-all-start.1) | async-done | bytes 1048608 | tf_op jit(solution)/shard_map/all_to_all | solution.py:178
  43.3 0.0 collective-permute-start.1
  43.3 1.9 %collective-permute-start.3 = (f32[2,32,256]{2,1,0:T(8,128)S(1)}, f32[2,32,256]{2,1,0:T(8,128)S(1)}, u32[]{:S(2)}, u32[]{:S(2)}) collective-permute-start(f32[2,32,256]{2,1,0:T(8,128)S(1)} %fusion.1), channel_id=1, source_target_pairs={{0,128},{128,0},{1,129},{129,1},{2,130},{130,2},{3,131},{131,3},{4... | collective-permute-start | bytes 196616 | tf_op jit(solution)/shard_map/ppermute | solution.py:22
  45.2 2.8 %collective-permute-done.3 = f32[2,32,256]{2,1,0:T(8,128)S(1)} collective-permute-done((f32[2,32,256]{2,1,0:T(8,128)S(1)}, f32[2,32,256]{2,1,0:T(8,128)S(1)}, u32[]{:S(2)}, u32[]{:S(2)}) %collective-permute-start.3) | collective-permute-done | bytes 65568 | tf_op jit(solution)/shard_map/ppermute | solution.py:22
  48.0 0.7 collective-permute-start.7
  48.7 2.6 %collective-permute-start.4 = (f32[2,2,32,256]{3,2,1,0:T(8,128)S(1)}, f32[2,2,32,256]{3,2,1,0:T(8,128)S(1)}, u32[]{:S(2)}, u32[]{:S(2)}) collective-permute-start(f32[2,2,32,256]{3,2,1,0:T(8,128)S(1)} %pad_maximum_fusion.refs_0_), channel_id=1, source_target_pairs={{0,7},{1,0},{2,1},{3,2},{4,3},{5,4},{6,5},{7,6},{8,15},{9,8},{10,9... | collective-permute-start | bytes 393224 | tf_op jit(solution)/shard_map/ppermute | solution.py:22
  51.3 3.1 %collective-permute-done.7.refs_6_ = f32[2,2,32,256]{3,2,1,0:T(8,128)S(1)} collective-permute-done((f32[2,2,32,256]{3,2,1,0:T(8,128)S(1)}, f32[2,2,32,256]{3,2,1,0:T(8,128)S(1)}, u32[]{:S(2)}, u32[]{:S(2)}) %collective-permute-start.7) | collective-permute-done | bytes 131104 | tf_op jit(solution)/shard_map/ppermute | solution.py:22
  54.4 0.0 collective-permute-start.8
  54.4 0.0 collective-permute-done.4.refs_1_
  54.4 3.2 %collective-permute-start.5 = (f32[2,2,32,256]{3,2,1,0:T(8,128)S(1)}, f32[2,2,32,256]{3,2,1,0:T(8,128)S(1)}, u32[]{:S(2)}, u32[]{:S(2)}) collective-permute-start(f32[2,2,32,256]{3,2,1,0:T(8,128)S(1)} %collective-permute-done.4.refs_1_), channel_id=1, source_target_pairs={{0,7},{1,0},{2,1},{3,2},{4,3},{5,4},{6,5},{7,6},{8,15},{9,8},{10,9... | collective-permute-start | bytes 393224 | tf_op jit(solution)/shard_map/ppermute | solution.py:22
  57.6 2.9 %collective-permute-done.8.refs_5_ = f32[2,2,32,256]{3,2,1,0:T(8,128)S(1)} collective-permute-done((f32[2,2,32,256]{3,2,1,0:T(8,128)S(1)}, f32[2,2,32,256]{3,2,1,0:T(8,128)S(1)}, u32[]{:S(2)}, u32[]{:S(2)}) %collective-permute-start.8) | collective-permute-done | bytes 131104 | tf_op jit(solution)/shard_map/ppermute | solution.py:22
  60.5 3.2 %collective-permute-start.6 = (f32[2,2,32,256]{3,2,1,0:T(8,128)S(1)}, f32[2,2,32,256]{3,2,1,0:T(8,128)S(1)}, u32[]{:S(2)}, u32[]{:S(2)}) collective-permute-start(f32[2,2,32,256]{3,2,1,0:T(8,128)S(1)} %collective-permute-done.5.refs_2_), channel_id=1, source_target_pairs={{0,7},{1,0},{2,1},{3,2},{4,3},{5,4},{6,5},{7,6},{8,15},{9,8},{10,9... | collective-permute-start | bytes 393224 | tf_op jit(solution)/shard_map/ppermute | solution.py:22
  63.8 2.9 %collective-permute-done.9.refs_4_ = f32[2,2,32,256]{3,2,1,0:T(8,128)S(1)} collective-permute-done((f32[2,2,32,256]{3,2,1,0:T(8,128)S(1)}, f32[2,2,32,256]{3,2,1,0:T(8,128)S(1)}, u32[]{:S(2)}, u32[]{:S(2)}) %collective-permute-start.9) | collective-permute-done | bytes 131104 | tf_op jit(solution)/shard_map/ppermute | solution.py:22
  66.7 0.0 collective-permute-start.10
  66.7 0.0 collective-permute-done.6.refs_3_
  66.7 6.2 %collective-permute-done.10.refs_7_ = f32[2,2,32,256]{3,2,1,0:T(8,128)S(1)} collective-permute-done((f32[2,2,32,256]{3,2,1,0:T(8,128)S(1)}, f32[2,2,32,256]{3,2,1,0:T(8,128)S(1)}, u32[]{:S(2)}, u32[]{:S(2)}) %collective-permute-start.10) | collective-permute-done | bytes 131104 | tf_op jit(solution)/shard_map/ppermute | solution.py:22
  72.9 0.0 collective-permute-done.1.twin_ref
  72.9 1.5 %solve.1 = (bf16[4,32,1024]{2,1,0:T(8,128)(2,1)S(1)}, bf16[4,32,1024]{2,1,0:T(8,128)(2,1)S(1)}, bf16[32,1024]{1,0:T(8,128)(2,1)S(1)}) custom-call(s32[1]{0:T(128)} %bitcast.2.pos_ref, bf16[16,256,128]{2,1,0:T(8,128)(2,1)S(1)} %all-to-all-done.1.own_ref, bf16[16,256,128]{2,1,0:T(8,128)(2,1)S(1)} %collective-permute-done.1.twin_ref, ...), custom_call_target="tpu_custom_call" | custom-call | tf_op jit(solution)/shard_map/solve/pallas_call | solution.py:204
  74.4 1.1 collective-permute-start.20
  75.5 1.0 collective-permute-start.22
  76.5 0.8 collective-permute-start.16
  77.3 2.4 %collective-permute-start.15 = (bf16[4,32,1024]{2,1,0:T(8,128)(2,1)S(1)}, bf16[4,32,1024]{2,1,0:T(8,128)(2,1)S(1)}, u32[]{:S(2)}, u32[]{:S(2)}) collective-permute-start(bf16[4,32,1024]{2,1,0:T(8,128)(2,1)S(1)} %get-tuple-element.12.refs_1_), channel_id=1, source_target_pairs={{0,24},{8,0},{16,8},{24,16},{1,25},{9,1},{17,9},{25,17},{2,26},{10... | collective-permute-start | bytes 786440 | tf_op jit(solution)/shard_map/ppermute | solution.py:22
  79.7 3.2 %collective-permute-done.20 = bf16[4,32,1024]{2,1,0:T(8,128)(2,1)S(1)} collective-permute-done((bf16[4,32,1024]{2,1,0:T(8,128)(2,1)S(1)}, bf16[4,32,1024]{2,1,0:T(8,128)(2,1)S(1)}, u32[]{:S(2)}, u32[]{:S(2)}) %collective-permute-start.20) | collective-permute-done | bytes 262176 | tf_op jit(solution)/shard_map/ppermute | solution.py:140
  82.9 1.6 %collective-permute-start.21 = (bf16[4,32,1024]{2,1,0:T(8,128)(2,1)S(1)}, bf16[4,32,1024]{2,1,0:T(8,128)(2,1)S(1)}, u32[]{:S(2)}, u32[]{:S(2)}) collective-permute-start(bf16[4,32,1024]{2,1,0:T(8,128)(2,1)S(1)} %collective-permute-done.20), channel_id=1, source_target_pairs={{0,128},{32,160},{128,32},{160,0},{1,129},{33,161},{129,33},{161,1... | collective-permute-start | bytes 786440 | tf_op jit(solution)/shard_map/ppermute | solution.py:140
  84.5 0.0 collective-permute-done.22
  84.5 1.3 collective-permute-start.23
  85.8 3.5 %collective-permute-start.11 = (bf16[32,1024]{1,0:T(8,128)(2,1)S(1)}, bf16[32,1024]{1,0:T(8,128)(2,1)S(1)}, u32[]{:S(2)}, u32[]{:S(2)}) collective-permute-start(bf16[32,1024]{1,0:T(8,128)(2,1)S(1)} %get-tuple-element.10.m0), channel_id=1, source_target_pairs={{0,128},{128,0},{1,129},{129,1},{2,130},{130,2},{3,131},{131,3},{4... | collective-permute-start | bytes 196616 | tf_op jit(solution)/shard_map/ppermute | solution.py:22
  89.3 2.2 %collective-permute-done.11.m1 = bf16[32,1024]{1,0:T(8,128)(2,1)S(1)} collective-permute-done((bf16[32,1024]{1,0:T(8,128)(2,1)S(1)}, bf16[32,1024]{1,0:T(8,128)(2,1)S(1)}, u32[]{:S(2)}, u32[]{:S(2)}) %collective-permute-start.11) | collective-permute-done | bytes 65568 | tf_op jit(solution)/shard_map/ppermute | solution.py:22
  91.5 1.3 collective-permute-done.12.m2
  92.8 0.6 copy-done.1
  93.4 0.2 collective-permute-start.13
  93.6 1.1 collective-permute-done.13.m3
  94.7 0.6 copy-done.3
  95.3 0.8 collective-permute-start.14
  96.1 0.0 collective-permute-done.16.refs_4_
  96.1 1.2 collective-permute-start.17
  97.3 0.0 collective-permute-done.15.refs_3_
  97.3 0.7 collective-permute-start.18
  98.0 0.3 collective-permute-start.26
  98.3 2.9 %collective-permute-start.25 = (bf16[4,32,1024]{2,1,0:T(8,128)(2,1)S(1)}, bf16[4,32,1024]{2,1,0:T(8,128)(2,1)S(1)}, u32[]{:S(2)}, u32[]{:S(2)}) collective-permute-start(bf16[4,32,1024]{2,1,0:T(8,128)(2,1)S(1)} %collective-permute-done.23.refs_9_), channel_id=1, source_target_pairs={{0,24},{8,0},{16,8},{24,16},{1,25},{9,1},{17,9},{25,17},{2,26},{10... | collective-permute-start | bytes 786440 | tf_op jit(solution)/shard_map/ppermute | solution.py:22
  101.3 3.2 %collective-permute-done.14.refs_2_ = bf16[4,32,1024]{2,1,0:T(8,128)(2,1)S(1)} collective-permute-done((bf16[4,32,1024]{2,1,0:T(8,128)(2,1)S(1)}, bf16[4,32,1024]{2,1,0:T(8,128)(2,1)S(1)}, u32[]{:S(2)}, u32[]{:S(2)}) %collective-permute-start.14) | collective-permute-done | bytes 262176 | tf_op jit(solution)/shard_map/ppermute | solution.py:22
  104.5 2.0 %collective-permute-start.19 = (bf16[4,32,1024]{2,1,0:T(8,128)(2,1)S(1)}, bf16[4,32,1024]{2,1,0:T(8,128)(2,1)}, u32[]{:S(2)}, u32[]{:S(2)}) collective-permute-start(bf16[4,32,1024]{2,1,0:T(8,128)(2,1)S(1)} %collective-permute-done.15.refs_3_), channel_id=1, source_target_pairs={{0,24},{8,0},{16,8},{24,16},{1,25},{9,1},{17,9},{25,17},{2,26},{10... | collective-permute-start | bytes 786440 | tf_op jit(solution)/shard_map/ppermute | solution.py:22
  106.5 0.0 collective-permute-start.24
  106.5 5.6 %collective-permute-done.18.refs_6_ = bf16[4,32,1024]{2,1,0:T(8,128)(2,1)S(1)} collective-permute-done((bf16[4,32,1024]{2,1,0:T(8,128)(2,1)S(1)}, bf16[4,32,1024]{2,1,0:T(8,128)(2,1)S(1)}, u32[]{:S(2)}, u32[]{:S(2)}) %collective-permute-start.18) | collective-permute-done | bytes 262176 | tf_op jit(solution)/shard_map/ppermute | solution.py:22
  112.1 0.0 collective-permute-start.27
  112.1 5.6 %collective-permute-done.26.refs_2_ = bf16[4,32,1024]{2,1,0:T(8,128)(2,1)S(1)} collective-permute-done((bf16[4,32,1024]{2,1,0:T(8,128)(2,1)S(1)}, bf16[4,32,1024]{2,1,0:T(8,128)(2,1)S(1)}, u32[]{:S(2)}, u32[]{:S(2)}) %collective-permute-start.26) | collective-permute-done | bytes 262176 | tf_op jit(solution)/shard_map/ppermute | solution.py:22
  117.7 0.0 collective-permute-start.28
  117.7 3.2 %collective-permute-start.29 = (bf16[4,32,1024]{2,1,0:T(8,128)(2,1)S(1)}, bf16[4,32,1024]{2,1,0:T(8,128)(2,1)}, u32[]{:S(2)}, u32[]{:S(2)}) collective-permute-start(bf16[4,32,1024]{2,1,0:T(8,128)(2,1)S(1)} %collective-permute-done.25.refs_1_), channel_id=1, source_target_pairs={{0,24},{8,0},{16,8},{24,16},{1,25},{9,1},{17,9},{25,17},{2,26},{10... | collective-permute-start | bytes 786440 | tf_op jit(solution)/shard_map/ppermute | solution.py:22
  120.9 0.1 stack.56.pos_ref
  121.0 0.8 copy-done.2
  121.9 0.8 copy-done.4
  122.7 3.1 %near.1 = (f32[128,1,2048]{2,1,0:T(1,128)}, bf16[4,32,1024]{2,1,0:T(8,128)(2,1)S(1)}) custom-call(s32[5]{0:T(128)S(1)} %stack.56.pos_ref, bf16[32,1024]{1,0:T(8,128)(2,1)S(1)} %get-tuple-element.10.m0, bf16[32,1024]{1,0:T(8,128)(2,1)S(1)} %collective-permute-done.11.m1, bf16[32,1024]{1,0:T(8,128)(2,1)S(1)} %copy-done.2, bf16[32,1024]{1,0:T(8,128)(2,1)S(1)} %copy-done.4, ...), custom_call_target="tpu_custom_call" | custom-call | tf_op jit(solution)/shard_map/near/pallas_call | solution.py:227
  125.8 2.3 %shard_map.46.before = f32[128,1,2048]{2,1,0:T(1,128)} custom-call(s32[5]{0:T(128)S(1)} %stack.56.pos_ref, f32[128,1,2048]{2,1,0:T(1,128)} %get-tuple-element.13.before, bf16[4,32,1024]{2,1,0:T(8,128)(2,1)S(1)} %get-tuple-element.14.own, bf16[4,32,1024]{2,1,0:T(8,128)(2,1)S(1)} %collective-permute-done.24.refs_0_, ...), custom_call_target="tpu_custom_call", output_to_operand_aliasing={{}: (1, {})} | custom-call | tf_op jit(solution)/shard_map/pallas_call | solution.py:239
  128.1 2.0 %shard_map.47 = f32[128,1,2048]{2,1,0:T(1,128)} custom-call(s32[5]{0:T(128)S(1)} %stack.56.pos_ref, f32[128,1,2048]{2,1,0:T(1,128)} %shard_map.46.before, bf16[4,32,1024]{2,1,0:T(8,128)(2,1)S(1)} %get-tuple-element.14.own, bf16[4,32,1024]{2,1,0:T(8,128)(2,1)S(1)} %collective-permute-done.28.refs_0_, ...), custom_call_target="tpu_custom_call", output_to_operand_aliasing={{}: (1, {})} | custom-call | tf_op jit(solution)/shard_map/pallas_call | solution.py:239
  (36 shorter events, 0.2 us)
Async XLA Ops:
  0.0 0.7 copy-start
  0.0 0.7 copy-start.6
  0.8 2.3 %copy-start.7 = (f32[1,1,256,4]{2,3,1,0:T(4,128)S(1)}, f32[1,1,256,4]{2,3,1,0:T(4,128)}, u32[]{:S(2)}) copy-start(f32[1,1,256,4]{2,3,1,0:T(4,128)} %param.5) | copy-start | bytes 12292
  0.8 3.8 %collective-permute-start = (bf16[4,256]{1,0:T(4,128)(2,1)S(1)}, bf16[4,256]{1,0:T(4,128)(2,1)S(1)}, u32[]{:S(2)}, u32[]{:S(2)}) collective-permute-start(bf16[4,256]{1,0:T(4,128)(2,1)S(1)} %get-tuple-element.20), channel_id=1, source_target_pairs={{0,128},{128,0},{1,129},{129,1},{2,130},{130,2},{3,131},{131,3},{4... | collective-permute-start | bytes 6152 | tf_op jit(solution)/shard_map/ppermute | solution.py:22
  22.4 7.5 %copy-start.5 = (f32[1,1,256,128]{3,2,1,0:T(8,128)S(1)}, f32[1,1,256,128]{3,2,1,0:T(8,128)}, u32[]{:S(2)}) copy-start(f32[1,1,256,128]{3,2,1,0:T(8,128)} %param.6) | copy-start | bytes 393220
  22.4 20.9 %all-to-all-start.1 = ((bf16[16,256,128]{2,1,0:T(8,128)(2,1)}), bf16[16,256,128]{2,1,0:T(8,128)(2,1)S(1)}, u32[]{:S(2)}, u32[]{:S(2)}) async-start(bf16[16,256,128]{2,1,0:T(8,128)(2,1)} %broadcast_in_dim.31), calls=%async_computation.1 | async-start | bytes 2097152 | tf_op jit(solution)/shard_map/all_to_all | solution.py:178
  30.0 13.2 %collective-permute-start.2 = (f32[128,256]{1,0:T(8,128)S(1)}, f32[128,256]{1,0:T(8,128)S(1)}, u32[]{:S(2)}, u32[]{:S(2)}) collective-permute-start(f32[128,256]{1,0:T(8,128)S(1)} %bitcast.68), channel_id=1, source_target_pairs={{0,64},{64,0},{1,65},{65,1},{2,66},{66,2},{3,67},{67,3},{4,68},{68... | collective-permute-start | bytes 393224 | tf_op jit(solution)/shard_map/ppermute | solution.py:22
  43.3 29.6 %collective-permute-start.1 = (bf16[16,256,128]{2,1,0:T(8,128)(2,1)S(1)}, bf16[16,256,128]{2,1,0:T(8,128)(2,1)S(1)}, u32[]{:S(2)}, u32[]{:S(2)}) collective-permute-start(bf16[16,256,128]{2,1,0:T(8,128)(2,1)S(1)} %all-to-all-done.1.own_ref), channel_id=1, source_target_pairs={{0,64},{64,0},{1,65},{65,1},{2,66},{66,2},{3,67},{67,3},{4,68},{68... | collective-permute-start | bytes 3145736 | tf_op jit(solution)/shard_map/ppermute | solution.py:22
  43.3 4.6 %collective-permute-start.3 = (f32[2,32,256]{2,1,0:T(8,128)S(1)}, f32[2,32,256]{2,1,0:T(8,128)S(1)}, u32[]{:S(2)}, u32[]{:S(2)}) collective-permute-start(f32[2,32,256]{2,1,0:T(8,128)S(1)} %fusion.1), channel_id=1, source_target_pairs={{0,128},{128,0},{1,129},{129,1},{2,130},{130,2},{3,131},{131,3},{4... | collective-permute-start | bytes 196616 | tf_op jit(solution)/shard_map/ppermute | solution.py:22
  48.0 6.4 %collective-permute-start.7 = (f32[2,2,32,256]{3,2,1,0:T(8,128)S(1)}, f32[2,2,32,256]{3,2,1,0:T(8,128)S(1)}, u32[]{:S(2)}, u32[]{:S(2)}) collective-permute-start(f32[2,2,32,256]{3,2,1,0:T(8,128)S(1)} %pad_maximum_fusion.refs_0_), channel_id=1, source_target_pairs={{0,1},{1,2},{2,3},{3,4},{4,5},{5,6},{6,7},{7,0},{8,9},{9,10},{10,1... | collective-permute-start | bytes 393224 | tf_op jit(solution)/shard_map/ppermute | solution.py:22
  48.7 5.6 %collective-permute-start.4 = (f32[2,2,32,256]{3,2,1,0:T(8,128)S(1)}, f32[2,2,32,256]{3,2,1,0:T(8,128)S(1)}, u32[]{:S(2)}, u32[]{:S(2)}) collective-permute-start(f32[2,2,32,256]{3,2,1,0:T(8,128)S(1)} %pad_maximum_fusion.refs_0_), channel_id=1, source_target_pairs={{0,7},{1,0},{2,1},{3,2},{4,3},{5,4},{6,5},{7,6},{8,15},{9,8},{10,9... | collective-permute-start | bytes 393224 | tf_op jit(solution)/shard_map/ppermute | solution.py:22
  54.4 6.2 %collective-permute-start.8 = (f32[2,2,32,256]{3,2,1,0:T(8,128)S(1)}, f32[2,2,32,256]{3,2,1,0:T(8,128)S(1)}, u32[]{:S(2)}, u32[]{:S(2)}) collective-permute-start(f32[2,2,32,256]{3,2,1,0:T(8,128)S(1)} %collective-permute-done.7.refs_6_), channel_id=1, source_target_pairs={{0,1},{1,2},{2,3},{3,4},{4,5},{5,6},{6,7},{7,0},{8,9},{9,10},{10,1... | collective-permute-start | bytes 393224 | tf_op jit(solution)/shard_map/ppermute | solution.py:22
  54.4 6.2 %collective-permute-start.5 = (f32[2,2,32,256]{3,2,1,0:T(8,128)S(1)}, f32[2,2,32,256]{3,2,1,0:T(8,128)S(1)}, u32[]{:S(2)}, u32[]{:S(2)}) collective-permute-start(f32[2,2,32,256]{3,2,1,0:T(8,128)S(1)} %collective-permute-done.4.refs_1_), channel_id=1, source_target_pairs={{0,7},{1,0},{2,1},{3,2},{4,3},{5,4},{6,5},{7,6},{8,15},{9,8},{10,9... | collective-permute-start | bytes 393224 | tf_op jit(solution)/shard_map/ppermute | solution.py:22
  60.5 6.2 %collective-permute-start.9 = (f32[2,2,32,256]{3,2,1,0:T(8,128)S(1)}, f32[2,2,32,256]{3,2,1,0:T(8,128)S(1)}, u32[]{:S(2)}, u32[]{:S(2)}) collective-permute-start(f32[2,2,32,256]{3,2,1,0:T(8,128)S(1)} %collective-permute-done.8.refs_5_), channel_id=1, source_target_pairs={{0,1},{1,2},{2,3},{3,4},{4,5},{5,6},{6,7},{7,0},{8,9},{9,10},{10,1... | collective-permute-start | bytes 393224 | tf_op jit(solution)/shard_map/ppermute | solution.py:22
  60.5 6.2 %collective-permute-start.6 = (f32[2,2,32,256]{3,2,1,0:T(8,128)S(1)}, f32[2,2,32,256]{3,2,1,0:T(8,128)S(1)}, u32[]{:S(2)}, u32[]{:S(2)}) collective-permute-start(f32[2,2,32,256]{3,2,1,0:T(8,128)S(1)} %collective-permute-done.5.refs_2_), channel_id=1, source_target_pairs={{0,7},{1,0},{2,1},{3,2},{4,3},{5,4},{6,5},{7,6},{8,15},{9,8},{10,9... | collective-permute-start | bytes 393224 | tf_op jit(solution)/shard_map/ppermute | solution.py:22
  66.7 6.2 %collective-permute-start.10 = (f32[2,2,32,256]{3,2,1,0:T(8,128)S(1)}, f32[2,2,32,256]{3,2,1,0:T(8,128)S(1)}, u32[]{:S(2)}, u32[]{:S(2)}) collective-permute-start(f32[2,2,32,256]{3,2,1,0:T(8,128)S(1)} %collective-permute-done.9.refs_4_), channel_id=1, source_target_pairs={{0,1},{1,2},{2,3},{3,4},{4,5},{5,6},{6,7},{7,0},{8,9},{9,10},{10,1... | collective-permute-start | bytes 393224 | tf_op jit(solution)/shard_map/ppermute | solution.py:22
  74.4 8.5 %collective-permute-start.20 = (bf16[4,32,1024]{2,1,0:T(8,128)(2,1)S(1)}, bf16[4,32,1024]{2,1,0:T(8,128)(2,1)S(1)}, u32[]{:S(2)}, u32[]{:S(2)}) collective-permute-start(bf16[4,32,1024]{2,1,0:T(8,128)(2,1)S(1)} %get-tuple-element.11.refs_0_), channel_id=1, source_target_pairs={{0,128},{32,160},{128,32},{160,0},{1,129},{33,161},{129,33},{161,1... | collective-permute-start | bytes 786440 | tf_op jit(solution)/shard_map/ppermute | solution.py:140
  75.5 9.0 %collective-permute-start.22 = (bf16[4,32,1024]{2,1,0:T(8,128)(2,1)S(1)}, bf16[4,32,1024]{2,1,0:T(8,128)(2,1)S(1)}, u32[]{:S(2)}, u32[]{:S(2)}) collective-permute-start(bf16[4,32,1024]{2,1,0:T(8,128)(2,1)S(1)} %get-tuple-element.12.refs_1_), channel_id=1, source_target_pairs={{0,160},{32,128},{128,0},{160,32},{1,161},{33,129},{129,1},{161,33... | collective-permute-start | bytes 786440 | tf_op jit(solution)/shard_map/ppermute | solution.py:140
  76.5 19.6 %collective-permute-start.16 = (bf16[4,32,1024]{2,1,0:T(8,128)(2,1)S(1)}, bf16[4,32,1024]{2,1,0:T(8,128)(2,1)S(1)}, u32[]{:S(2)}, u32[]{:S(2)}) collective-permute-start(bf16[4,32,1024]{2,1,0:T(8,128)(2,1)S(1)} %get-tuple-element.11.refs_0_), channel_id=1, source_target_pairs={{0,8},{8,16},{16,24},{24,0},{1,9},{9,17},{17,25},{25,1},{2,10},{10... | collective-permute-start | bytes 786440 | tf_op jit(solution)/shard_map/ppermute | solution.py:22
  77.3 20.0 %collective-permute-start.15 = (bf16[4,32,1024]{2,1,0:T(8,128)(2,1)S(1)}, bf16[4,32,1024]{2,1,0:T(8,128)(2,1)S(1)}, u32[]{:S(2)}, u32[]{:S(2)}) collective-permute-start(bf16[4,32,1024]{2,1,0:T(8,128)(2,1)S(1)} %get-tuple-element.12.refs_1_), channel_id=1, source_target_pairs={{0,24},{8,0},{16,8},{24,16},{1,25},{9,1},{17,9},{25,17},{2,26},{10... | collective-permute-start | bytes 786440 | tf_op jit(solution)/shard_map/ppermute | solution.py:22
  82.9 15.1 %collective-permute-start.21 = (bf16[4,32,1024]{2,1,0:T(8,128)(2,1)S(1)}, bf16[4,32,1024]{2,1,0:T(8,128)(2,1)S(1)}, u32[]{:S(2)}, u32[]{:S(2)}) collective-permute-start(bf16[4,32,1024]{2,1,0:T(8,128)(2,1)S(1)} %collective-permute-done.20), channel_id=1, source_target_pairs={{0,128},{32,160},{128,32},{160,0},{1,129},{33,161},{129,33},{161,1... | collective-permute-start | bytes 786440 | tf_op jit(solution)/shard_map/ppermute | solution.py:140
  84.5 13.9 %collective-permute-start.23 = (bf16[4,32,1024]{2,1,0:T(8,128)(2,1)S(1)}, bf16[4,32,1024]{2,1,0:T(8,128)(2,1)S(1)}, u32[]{:S(2)}, u32[]{:S(2)}) collective-permute-start(bf16[4,32,1024]{2,1,0:T(8,128)(2,1)S(1)} %collective-permute-done.22), channel_id=1, source_target_pairs={{0,160},{32,128},{128,0},{160,32},{1,161},{33,129},{129,1},{161,33... | collective-permute-start | bytes 786440 | tf_op jit(solution)/shard_map/ppermute | solution.py:140
  85.8 5.7 %collective-permute-start.11 = (bf16[32,1024]{1,0:T(8,128)(2,1)S(1)}, bf16[32,1024]{1,0:T(8,128)(2,1)S(1)}, u32[]{:S(2)}, u32[]{:S(2)}) collective-permute-start(bf16[32,1024]{1,0:T(8,128)(2,1)S(1)} %get-tuple-element.10.m0), channel_id=1, source_target_pairs={{0,128},{128,0},{1,129},{129,1},{2,130},{130,2},{3,131},{131,3},{4... | collective-permute-start | bytes 196616 | tf_op jit(solution)/shard_map/ppermute | solution.py:22
  91.5 1.3 collective-permute-start.12
  92.8 0.6 copy-start.1
  93.4 1.3 collective-permute-start.13
  94.7 0.6 copy-start.3
  95.3 9.2 %collective-permute-start.14 = (bf16[4,32,1024]{2,1,0:T(8,128)(2,1)S(1)}, bf16[4,32,1024]{2,1,0:T(8,128)(2,1)S(1)}, u32[]{:S(2)}, u32[]{:S(2)}) collective-permute-start(bf16[4,32,1024]{2,1,0:T(8,128)(2,1)S(1)} %get-tuple-element.11.refs_0_), channel_id=1, source_target_pairs={{0,24},{8,0},{16,8},{24,16},{1,25},{9,1},{17,9},{25,17},{2,26},{10... | collective-permute-start | bytes 786440 | tf_op jit(solution)/shard_map/ppermute | solution.py:22
  96.1 10.4 %collective-permute-start.17 = (bf16[4,32,1024]{2,1,0:T(8,128)(2,1)S(1)}, bf16[4,32,1024]{2,1,0:T(8,128)(2,1)S(1)}, u32[]{:S(2)}, u32[]{:S(2)}) collective-permute-start(bf16[4,32,1024]{2,1,0:T(8,128)(2,1)S(1)} %get-tuple-element.12.refs_1_), channel_id=1, source_target_pairs={{0,8},{8,16},{16,24},{24,0},{1,9},{9,17},{17,25},{25,1},{2,10},{10... | collective-permute-start | bytes 786440 | tf_op jit(solution)/shard_map/ppermute | solution.py:22
  97.3 14.8 %collective-permute-start.18 = (bf16[4,32,1024]{2,1,0:T(8,128)(2,1)S(1)}, bf16[4,32,1024]{2,1,0:T(8,128)(2,1)S(1)}, u32[]{:S(2)}, u32[]{:S(2)}) collective-permute-start(bf16[4,32,1024]{2,1,0:T(8,128)(2,1)S(1)} %collective-permute-done.16.refs_4_), channel_id=1, source_target_pairs={{0,8},{8,16},{16,24},{24,0},{1,9},{9,17},{17,25},{25,1},{2,10},{10... | collective-permute-start | bytes 786440 | tf_op jit(solution)/shard_map/ppermute | solution.py:22
  98.0 19.7 %collective-permute-start.26 = (bf16[4,32,1024]{2,1,0:T(8,128)(2,1)S(1)}, bf16[4,32,1024]{2,1,0:T(8,128)(2,1)S(1)}, u32[]{:S(2)}, u32[]{:S(2)}) collective-permute-start(bf16[4,32,1024]{2,1,0:T(8,128)(2,1)S(1)} %collective-permute-done.21.refs_8_), channel_id=1, source_target_pairs={{0,8},{8,16},{16,24},{24,0},{1,9},{9,17},{17,25},{25,1},{2,10},{10... | collective-permute-start | bytes 786440 | tf_op jit(solution)/shard_map/ppermute | solution.py:22
  98.3 19.4 %collective-permute-start.25 = (bf16[4,32,1024]{2,1,0:T(8,128)(2,1)S(1)}, bf16[4,32,1024]{2,1,0:T(8,128)(2,1)S(1)}, u32[]{:S(2)}, u32[]{:S(2)}) collective-permute-start(bf16[4,32,1024]{2,1,0:T(8,128)(2,1)S(1)} %collective-permute-done.23.refs_9_), channel_id=1, source_target_pairs={{0,24},{8,0},{16,8},{24,16},{1,25},{9,1},{17,9},{25,17},{2,26},{10... | collective-permute-start | bytes 786440 | tf_op jit(solution)/shard_map/ppermute | solution.py:22
  104.5 16.6 %collective-permute-start.19 = (bf16[4,32,1024]{2,1,0:T(8,128)(2,1)S(1)}, bf16[4,32,1024]{2,1,0:T(8,128)(2,1)}, u32[]{:S(2)}, u32[]{:S(2)}) collective-permute-start(bf16[4,32,1024]{2,1,0:T(8,128)(2,1)S(1)} %collective-permute-done.15.refs_3_), channel_id=1, source_target_pairs={{0,24},{8,0},{16,8},{24,16},{1,25},{9,1},{17,9},{25,17},{2,26},{10... | collective-permute-start | bytes 786440 | tf_op jit(solution)/shard_map/ppermute | solution.py:22
  106.5 19.4 %collective-permute-start.24 = (bf16[4,32,1024]{2,1,0:T(8,128)(2,1)S(1)}, bf16[4,32,1024]{2,1,0:T(8,128)(2,1)S(1)}, u32[]{:S(2)}, u32[]{:S(2)}) collective-permute-start(bf16[4,32,1024]{2,1,0:T(8,128)(2,1)S(1)} %collective-permute-done.21.refs_8_), channel_id=1, source_target_pairs={{0,24},{8,0},{16,8},{24,16},{1,25},{9,1},{17,9},{25,17},{2,26},{10... | collective-permute-start | bytes 786440 | tf_op jit(solution)/shard_map/ppermute | solution.py:22
  112.1 13.8 %collective-permute-start.27 = (bf16[4,32,1024]{2,1,0:T(8,128)(2,1)S(1)}, bf16[4,32,1024]{2,1,0:T(8,128)(2,1)}, u32[]{:S(2)}, u32[]{:S(2)}) collective-permute-start(bf16[4,32,1024]{2,1,0:T(8,128)(2,1)S(1)} %collective-permute-done.23.refs_9_), channel_id=1, source_target_pairs={{0,8},{8,16},{16,24},{24,0},{1,9},{9,17},{17,25},{25,1},{2,10},{10... | collective-permute-start | bytes 786440 | tf_op jit(solution)/shard_map/ppermute | solution.py:22
  117.7 10.4 %collective-permute-start.28 = (bf16[4,32,1024]{2,1,0:T(8,128)(2,1)S(1)}, bf16[4,32,1024]{2,1,0:T(8,128)(2,1)S(1)}, u32[]{:S(2)}, u32[]{:S(2)}) collective-permute-start(bf16[4,32,1024]{2,1,0:T(8,128)(2,1)S(1)} %collective-permute-done.26.refs_2_), channel_id=1, source_target_pairs={{0,8},{8,16},{16,24},{24,0},{1,9},{9,17},{17,25},{25,1},{2,10},{10... | collective-permute-start | bytes 786440 | tf_op jit(solution)/shard_map/ppermute | solution.py:22
  117.7 10.4 %collective-permute-start.29 = (bf16[4,32,1024]{2,1,0:T(8,128)(2,1)S(1)}, bf16[4,32,1024]{2,1,0:T(8,128)(2,1)}, u32[]{:S(2)}, u32[]{:S(2)}) collective-permute-start(bf16[4,32,1024]{2,1,0:T(8,128)(2,1)S(1)} %collective-permute-done.25.refs_1_), channel_id=1, source_target_pairs={{0,24},{8,0},{16,8},{24,16},{1,25},{9,1},{17,9},{25,17},{2,26},{10... | collective-permute-start | bytes 786440 | tf_op jit(solution)/shard_map/ppermute | solution.py:22
  121.0 0.8 copy-start.2
  121.9 0.8 copy-start.4
